TPU v7x, 32 devices: a whole 2x2x4 slice. The times are simulated.
32 devices in a mesh: groups: 2 (over y), rows: 4 (over z), cams: 2 (over x), cols: 2 (over core).
Axes of the slice: x: 2, y: 2, z: 4, core: 2. Of those that a mesh axis runs over, the one named last changes fastest.
Arguments:
- left_feats: bfloat16 [4, 32, 1024, 128], P(('groups', 'cams'), 'rows', 'cols'), parts along dimension 0, may hold values from -6 to 6
- right_feats: bfloat16 [4, 32, 1024, 128], P(('groups', 'cams'), 'rows', 'cols'), parts along dimension 0, may hold values from -6 to 6
- prev_hidden: bfloat16 [4, 32, 1024, 128], P(('groups', 'cams'), 'rows', 'cols'), parts along dimension 0, may hold values from -1 to 1
- warp_list: int32 [4, 32, 8, 4], P(('groups', 'cams'), 'rows', 'cols'), parts along dimension 0, may hold values from -1 to 7, as said below
- enc_weight: bfloat16 [192, 128], replicated, may hold values from -0.4375 to 0.4375
- hgate_w: bfloat16 [5, 256, 256], replicated, may hold values from -0.15625 to 0.15625
- hcand_w: bfloat16 [5, 256, 128], replicated, may hold values from -0.15625 to 0.15625
- vgate_w: bfloat16 [5, 256, 256], replicated, may hold values from -0.15625 to 0.15625
- vcand_w: bfloat16 [5, 256, 128], replicated, may hold values from -0.15625 to 0.15625
Outputs:
- hidden_next: bfloat16 [4, 32, 1024, 128], P(('groups', 'cams'), 'rows', 'cols'), parts along dimension 0
There are 2 independent parts, one for each index of `groups`. A program takes and returns all parts, laid end to end along the dimension named above; an argument that names none is the same for every part. Nothing has to cross between parts.
Inputs may be any that keep to these rules, and one draw needn't show every extreme that they name: Entry 0 of warp_list is the band offset k, entry 1 the source row within a band of 8 rows, entry 2 the source block among the 4 blocks of the same column half, entry 3 the valid flag. Among the 32 blocks of one band and column half of one view, exactly half take offset 0 and a quarter each take -1 and 1, so at most 8 come from one neighbouring band, and the blocks that take one offset name distinct source blocks. The flag is 0 wherever the source band lies outside the image.
All inputs are finite; a program needn't handle non-finite values.
Results may differ from a plain program's by a relative error of at most 0.0062.
Values may be sent and summed in bfloat16 or wider, within the bound.
No kernel may reach another device: no remote copies, remote signals or barrier semaphores. Data moves between devices by JAX's collectives and lax.ppermute only.
A program may use at most 128 MiB of HBM per device.

v0:
```python
import functools

import jax
import jax.numpy as jnp
from jax import lax
from jax.experimental import pallas as pl
from jax.experimental.pallas import tpu as pltpu
from jax.sharding import PartitionSpec as P

bf16 = jnp.bfloat16
f32 = jnp.float32
SEAM = 16


def dotf(a, b):
    return jnp.dot(a, b, preferred_element_type=f32)


def sigmoid(v):
    return 0.5 * jnp.tanh(0.5 * v) + 0.5


def state_rows(*pieces):
    return [(piece, r) for piece in pieces for r in range(piece.shape[0])]


def swap_near(value, axis):
    count = lax.axis_size(axis)
    pairs = [(i, i ^ 1) for i in range(count) if i ^ 1 < count]
    return lax.ppermute(value, axis, pairs)


def swap_far(value, axis):
    count = lax.axis_size(axis)
    pairs = []
    for i in range(1, count - 1, 2):
        pairs += [(i, i + 1), (i + 1, i)]
    return lax.ppermute(value, axis, pairs)


IN_VMEM = pl.BlockSpec(memory_space=pltpu.VMEM)
IN_SMEM = pl.BlockSpec(memory_space=pltpu.SMEM)
IN_HBM = pl.BlockSpec(memory_space=pltpu.HBM)


def in_hbm(value):
    return pltpu.with_memory_space_constraint(value, pltpu.HBM)


def params(megabytes):
    return pltpu.CompilerParams(vmem_limit_bytes=megabytes << 20)


def motion_kernel(
    first, left_feats, right_feats, edge_ref, weight_ref, out_ref, left_ref, window, sems
):
    disparities = weight_ref.shape[0]
    rows, width, feats = left_ref.shape
    tile = 128
    own = pl.ds(first, rows)
    loads = [
        pltpu.make_async_copy(left_feats.at[0, own], left_ref, sems.at[0]),
        pltpu.make_async_copy(
            right_feats.at[0, own], window.at[:, pl.ds(disparities, width), :], sems.at[1]
        ),
    ]
    for load in loads:
        load.start()
    far_edge = edge_ref.shape[2] - disparities
    for r in range(rows):
        window[r, pl.ds(0, disparities), :] = edge_ref[
            0, first + r, pl.ds(far_edge, disparities), :
        ]
    scale = feats**-0.5
    lane = lax.broadcasted_iota(jnp.int32, (tile, tile), 1)
    row = lax.broadcasted_iota(jnp.int32, (tile, tile), 0)
    keep = lane < row
    flip = (lane + row == tile - 1).astype(f32).astype(bf16)
    turned = jnp.concatenate(
        [
            dotf(flip, weight_ref[pl.ds(disparities - tile, tile), :]).astype(bf16),
            dotf(flip, weight_ref[pl.ds(0, tile), :]).astype(bf16)[2 * tile - disparities :, :],
        ],
        axis=0,
    )
    span = disparities + tile
    blocks = -(-span // tile)
    tiles = [(r, t * tile) for r in range(rows) for t in range(width // tile)]
    for load in loads:
        load.wait()
    flipped = [dotf(flip, left_ref[r, pl.ds(x, tile), :]).astype(bf16) for r, x in tiles]
    scores = [
        lax.dot_general(
            part,
            window[r, pl.ds(x, blocks * tile), :],
            (((1,), (1,)), ((), ())),
            preferred_element_type=f32,
        )
        * scale
        for part, (r, x) in zip(flipped, tiles)
    ]
    skewed = []
    for score in scores:
        rolled = [
            pltpu.roll(score[:, tile * j : tile * (j + 1)], 0, 1, stride=1, stride_axis=0)
            for j in range(blocks)
        ]
        lanes = [jnp.where(keep, rolled[j], rolled[j + 1]).astype(bf16) for j in range(blocks - 1)]
        skewed.append(jnp.concatenate(lanes, axis=1)[:, :disparities])
    motions = [dotf(part, turned).astype(bf16) for part in skewed]
    for part, (r, x) in zip(motions, tiles):
        out_ref[r, pl.ds(x, tile), :] = dotf(flip, part).astype(bf16)


def motion_of(first, rows, left, right, edge, weight):
    width, feats = left.shape[2:]
    return pl.pallas_call(
        functools.partial(motion_kernel, first),
        in_specs=[IN_HBM, IN_HBM, IN_VMEM, IN_VMEM],
        out_specs=IN_VMEM,
        out_shape=jax.ShapeDtypeStruct((rows, width, weight.shape[1]), bf16),
        scratch_shapes=[
            pltpu.VMEM((rows, width, feats), bf16),
            pltpu.VMEM((rows, width + 256, feats), bf16),
            pltpu.SemaphoreType.DMA((2,)),
        ],
        compiler_params=params(16),
        name="motion",
    )(in_hbm(left), in_hbm(right), edge, weight)


def edges_kernel(place_ref, low_ref, high_ref, near_ref, far_ref):
    count = near_ref.shape[0]
    low, high = low_ref[pl.ds(0, count)], high_ref[pl.ds(high_ref.shape[0] - count, count)]
    below = place_ref[1] == 1
    near_ref[...] = jnp.where(below, high, low)
    far_ref[...] = jnp.where(below, low, high)


def edges_of(place, low, high, count):
    shape = jax.ShapeDtypeStruct((count,) + low.shape[1:], bf16)
    return pl.pallas_call(
        edges_kernel,
        in_specs=[IN_SMEM, IN_VMEM, IN_VMEM],
        out_specs=[IN_VMEM, IN_VMEM],
        out_shape=[shape, shape],
        compiler_params=params(4),
        name="edges",
    )(place, low, high)


def gather_kernel(
    place_ref, near_list, far_list, prev_ref, near_out, far_out, near_ref, far_ref, picks, sems
):
    lists = [
        pltpu.make_async_copy(near_list, near_ref, sems.at[0, 0]),
        pltpu.make_async_copy(far_list, far_ref, sems.at[1, 0]),
    ]
    for load in lists:
        load.start()
    _, band_blocks, _, band_rows = near_ref.shape
    slots, width, _ = near_out.shape
    sign = 2 * place_ref[1] - 1
    copies = []
    sides = ((near_ref, near_out, sign), (far_ref, far_out, -sign))
    for side, (list_ref, out, wanted) in enumerate(sides):
        lists[side].wait()
        count, source = jnp.int32(0), jnp.int32(0)
        for r in range(band_rows):
            for block in range(band_blocks):
                hit = list_ref[0, block, 0, r] == wanted
                count = count + hit.astype(jnp.int32)
                here = list_ref[0, block, 1, r] * band_blocks + list_ref[0, block, 2, r]
                source = jnp.where(hit & (count <= slots), here, source)
                picks[side, jnp.clip(count - 1, 0, slots - 1)] = source
        for slot in range(slots):
            row = picks[side, slot] // band_blocks
            column = pl.multiple_of(picks[side, slot] % band_blocks * width, width)
            block = prev_ref.at[0, row, pl.ds(column, width), :]
            copies.append(pltpu.make_async_copy(block, out.at[slot], sems.at[side, slot]))
            copies[-1].start()
    for copy in copies:
        copy.wait()


def gather_blocks(place, near_list, far_list, prev):
    _, band_blocks, _, band_rows = near_list.shape
    _, _, width, hidden = prev.shape
    slots = band_rows * band_blocks // 4
    shape = jax.ShapeDtypeStruct((slots, width // band_blocks, hidden), bf16)
    return pl.pallas_call(
        gather_kernel,
        in_specs=[IN_SMEM, IN_VMEM, IN_VMEM, IN_HBM],
        out_specs=[IN_VMEM, IN_VMEM],
        out_shape=[shape, shape],
        scratch_shapes=[pltpu.SMEM(near_list.shape, jnp.int32)] * 2
        + [pltpu.SMEM((2, slots), jnp.int32), pltpu.SemaphoreType.DMA((2, slots))],
        compiler_params=params(4),
        name="gather",
    )(place, near_list, far_list, in_hbm(prev))


def pick_blocks(place_ref, list_ref, visit):
    _, band_blocks, _, band_rows = list_ref.shape
    last = band_rows * band_blocks // 4 - 1
    sign = 2 * place_ref[1] - 1
    nears, fars = jnp.int32(0), jnp.int32(0)
    for row in range(band_rows):
        for block in range(band_blocks):
            offset = list_ref[0, block, 0, row]
            is_near, is_far = offset == -sign, offset == sign
            visit(row, block, is_near, is_far, jnp.minimum(nears, last), jnp.minimum(fars, last))
            nears += is_near.astype(jnp.int32)
            fars += is_far.astype(jnp.int32)


def seam_kernel(place_ref, list_ref, prev_ref, near_ref, far_ref, low_ref, high_ref, seam_ref):
    band_blocks = list_ref.shape[1]
    width, ch = near_ref.shape[1:]
    is_left = place_ref[0] == 0
    start = pl.multiple_of((width - SEAM) * (1 - place_ref[0]), SEAM)
    inside = pl.ds(start, SEAM)

    def visit(row, block, is_near, is_far, near_slot, far_slot):
        if block in (0, band_blocks - 1):
            source = pl.multiple_of(list_ref[0, block, 2, row] * width + start, SEAM)
            local = prev_ref[0, list_ref[0, block, 1, row], pl.ds(source, SEAM), :]
            near, far = near_ref[near_slot, inside, :], far_ref[far_slot, inside, :]
            picked = jnp.where(is_near, near, jnp.where(is_far, far, local))
            picked = jnp.where(list_ref[0, block, 3, row] > 0, picked, jnp.zeros_like(picked))
            if block > 0:
                picked = jnp.where(is_left, picked, seam_ref[row, :, 0:ch])
            seam_ref[row, :, 0:ch] = picked

    pick_blocks(place_ref, list_ref, visit)
    edge = pl.multiple_of((band_blocks * width - SEAM) * (1 - place_ref[0]), SEAM)
    half = low_ref.shape[0]
    seam_ref[pl.ds(0, half), :, ch : 2 * ch] = low_ref[:, pl.ds(edge, SEAM), :]
    seam_ref[pl.ds(half, half), :, ch : 2 * ch] = high_ref[:, pl.ds(edge, SEAM), :]


def seam_of(place, warp_list, prev, near, far, low, high):
    _, rows, _, ch = prev.shape
    return pl.pallas_call(
        seam_kernel,
        in_specs=[IN_SMEM, IN_SMEM] + [IN_VMEM] * 5,
        out_specs=IN_VMEM,
        out_shape=jax.ShapeDtypeStruct((rows, SEAM, 2 * ch), bf16),
        compiler_params=params(4),
        name="seam",
    )(place, warp_list, prev, near, far, low, high)


def warp_kernel(place_ref, list_ref, prev_ref, near_ref, far_ref, out_ref):
    width = near_ref.shape[1]

    def visit(row, block, is_near, is_far, near_slot, far_slot):
        column = pl.multiple_of(list_ref[0, block, 2, row] * width, width)
        local = prev_ref[0, list_ref[0, block, 1, row], pl.ds(column, width), :]
        picked = jnp.where(
            is_near, near_ref[near_slot], jnp.where(is_far, far_ref[far_slot], local)
        )
        picked = jnp.where(list_ref[0, block, 3, row] > 0, picked, jnp.zeros_like(picked))
        out_ref[row, pl.ds(block * width, width), :] = picked

    pick_blocks(place_ref, list_ref, visit)


def warp_of(place, warp_list, prev, near, far):
    return pl.pallas_call(
        warp_kernel,
        in_specs=[IN_SMEM, IN_SMEM] + [IN_VMEM] * 3,
        out_specs=IN_VMEM,
        out_shape=jax.ShapeDtypeStruct(prev.shape[1:], bf16),
        compiler_params=params(4),
        name="warp",
    )(place, warp_list, prev, near, far)


def horizontal_kernel(
    rows, place_ref, hidden_ref, low_ref, high_ref, seam_ref, gates_ref, cand_ref, out_ref, *rest
):
    *edges, joined, reset, partial = rest
    _, width, ch = hidden_ref.shape
    taps = gates_ref.shape[0]
    half = taps // 2
    right = place_ref[0]
    pad = SEAM
    own = pl.multiple_of(pad + pad * right, pad)
    seam = pl.multiple_of(pad + width * (1 - right), pad)
    span = width + SEAM
    flow = state_rows(low_ref, high_ref)
    gates = gates_ref[...].reshape(taps * 2 * ch, 2 * ch)
    count = range(len(rows))
    for r in count:
        piece, at = flow[rows[r]]
        for edge in (0, span + pad):
            joined[r, pl.ds(edge, pad), :] = jnp.zeros((pad, 2 * ch), bf16)
            reset[r, pl.ds(edge, pad), :] = jnp.zeros((pad, ch), bf16)
        joined[r, pl.ds(own, width), 0:ch] = hidden_ref[rows[r]]
        joined[r, pl.ds(own, width), ch : 2 * ch] = piece[at]
        joined[r, pl.ds(seam, SEAM), :] = seam_ref[rows[r]]
    sums = [
        dotf(
            jnp.concatenate(
                [joined[r, pl.ds(pad - half + t, span), :] for t in range(taps)], axis=1
            ),
            gates,
        )
        for r in count
    ]
    update = []
    for r in count:
        update.append(sigmoid(sums[r][:, :ch]))
        current = joined[r, pl.ds(pad, span), 0:ch].astype(f32)
        reset[r, pl.ds(pad, span), :] = (sigmoid(sums[r][:, ch:]) * current).astype(bf16)
    for r in count:
        both = jnp.concatenate([reset[r], joined[r, :, ch : 2 * ch]], axis=1)
        for t in range(0, taps, 2):
            pair = jnp.concatenate([cand_ref[k] for k in range(t, min(t + 2, taps))], axis=1)
            partial[r, :, pl.ds(t * ch, pair.shape[1])] = dotf(both, pair)
    totals = []
    for r in count:
        total = None
        for t in range(taps):
            part = partial[r, pl.ds(pad - half + t, span), pl.ds(t * ch, ch)]
            total = part if total is None else total + part
        totals.append(total)
    for r in count:
        current = joined[r, pl.ds(pad, span), 0:ch].astype(f32)
        cand = jnp.tanh(totals[r])
        blended = (1.0 - update[r]) * current + update[r] * cand
        reset[r, pl.ds(pad, span), :] = blended.astype(bf16)
    for r in count:
        out_ref[r] = reset[r, pl.ds(own, width), :]
    if edges:
        near_ref, far_ref = edges
        near_ref[...] = out_ref[pl.ds(half * place_ref[1], half)]
        far_ref[...] = out_ref[pl.ds(half - half * place_ref[1], half)]


def horizontal_pass(rows, send, place, hidden, low, high, seam, gates, cand):
    _, width, ch = hidden.shape
    taps = gates.shape[0]
    length = width + SEAM + 2 * SEAM
    shape = lambda count: jax.ShapeDtypeStruct((count, width, ch), bf16)
    shapes = [shape(len(rows))] + [shape(taps // 2)] * (2 if send else 0)
    return pl.pallas_call(
        functools.partial(horizontal_kernel, rows),
        in_specs=[IN_SMEM] + [IN_VMEM] * 6,
        out_specs=[IN_VMEM] * len(shapes),
        out_shape=shapes,
        scratch_shapes=[
            pltpu.VMEM((len(rows), length, 2 * ch), bf16),
            pltpu.VMEM((len(rows), length, ch), bf16),
            pltpu.VMEM((len(rows), length, taps * ch), f32),
        ],
        compiler_params=params(24),
        name="horizontal",
    )(place, hidden, low, high, seam, gates, cand)


def pairs_kernel(cand_ref, out_ref):
    taps, depth, ch = cand_ref.shape
    for j in range(taps + 1):
        none = jnp.zeros((depth, ch), bf16)
        out_ref[j, :, 0:ch] = cand_ref[j] if j < taps else none
        out_ref[j, :, ch : 2 * ch] = cand_ref[j - 1] if j > 0 else none


def pairs_of(cand):
    taps, depth, ch = cand.shape
    return pl.pallas_call(
        pairs_kernel,
        in_specs=[IN_VMEM],
        out_specs=IN_VMEM,
        out_shape=jax.ShapeDtypeStruct((taps + 1, depth, 2 * ch), bf16),
        compiler_params=params(4),
        name="pairs",
    )(cand)


def banded(outer_ref, inner_ref, half):
    outer = state_rows(outer_ref)
    return outer[:half] + state_rows(inner_ref) + outer[half:]


def stack(sources, rows):
    return jnp.concatenate(
        [piece[at] for y in rows for piece, at in (source[y] for source in sources)], axis=1
    )


def gates_kernel(
    outer_ref, inner_ref, low_ref, high_ref, gates_ref, update_ref, reset_ref, partial_ref
):
    taps, depth, wide = gates_ref.shape
    ch = wide // 2
    half = taps // 2
    state = banded(outer_ref, inner_ref, half)
    sources = (state, state_rows(low_ref, high_ref))
    rows = len(state)
    inner = range(half, rows - half)
    weights = lambda first, last: gates_ref[pl.ds(first, last - first)].reshape(-1, wide)
    sums = [dotf(stack(sources, range(y - half, y + half + 1)), weights(0, taps)) for y in inner]
    for i, y in enumerate([*range(half), *range(rows - half, rows)]):
        first, last = max(y - half, 0), min(y + half + 1, rows)
        partial_ref[i] = dotf(
            stack(sources, range(first, last)), weights(first - y + half, last - y + half)
        )
    for i, y in enumerate(inner):
        piece, at = state[y]
        update_ref[i] = sigmoid(sums[i][:, :ch])
        reset_ref[i] = (sigmoid(sums[i][:, ch:]) * piece[at].astype(f32)).astype(bf16)


def inner_gates(outer, inner, low, high, gates):
    count, width, ch = inner.shape
    half = gates.shape[0] // 2
    return pl.pallas_call(
        gates_kernel,
        in_specs=[IN_VMEM] * 5,
        out_specs=[IN_VMEM] * 3,
        out_shape=[
            jax.ShapeDtypeStruct((count, width, ch), f32),
            jax.ShapeDtypeStruct((count, width, ch), bf16),
            jax.ShapeDtypeStruct((2 * half, width, 2 * ch), f32),
        ],
        compiler_params=params(24),
        name="inner_gates",
    )(outer, inner, low, high, gates)


def outer_kernel(
    place_ref, outer_ref, partial_ref, hidden_near, hidden_far, motion_near, motion_far, gates_ref,
    update_ref, reset_ref, near_ref, far_ref, hidden_rim, motion_rim,
):
    taps, _, wide = gates_ref.shape
    ch = wide // 2
    half = taps // 2
    near = half * place_ref[1]
    far = half - near
    hidden_rim[pl.ds(near, half)] = hidden_near[...]
    hidden_rim[pl.ds(far, half)] = hidden_far[...]
    motion_rim[pl.ds(near, half)] = motion_near[...]
    motion_rim[pl.ds(far, half)] = motion_far[...]
    sources = (state_rows(hidden_rim), state_rows(motion_rim))
    weights = lambda first, last: gates_ref[pl.ds(first, last - first)].reshape(-1, wide)
    sums = []
    for i in range(half):
        sums.append(dotf(stack(sources, range(i, half)), weights(0, half - i)))
    for i in range(half):
        sums.append(dotf(stack(sources, range(half, half + i + 1)), weights(taps - 1 - i, taps)))
    for i in range(2 * half):
        total = sums[i] + partial_ref[i]
        update_ref[i] = sigmoid(total[:, :ch])
        reset_ref[i] = (sigmoid(total[:, ch:]) * outer_ref[i].astype(f32)).astype(bf16)
    near_ref[...] = reset_ref[pl.ds(near, half)]
    far_ref[...] = reset_ref[pl.ds(far, half)]


def outer_gates(place, outer, partial, rims, gates):
    count, width, ch = outer.shape
    half = gates.shape[0] // 2
    shape = lambda n, kind: jax.ShapeDtypeStruct((n, width, ch), kind)
    return pl.pallas_call(
        outer_kernel,
        in_specs=[IN_SMEM] + [IN_VMEM] * 7,
        out_specs=[IN_VMEM] * 4,
        out_shape=[shape(count, f32), shape(count, bf16), shape(half, bf16), shape(half, bf16)],
        scratch_shapes=[pltpu.VMEM((2 * half, width, ch), bf16)] * 2,
        compiler_params=params(16),
        name="outer_gates",
    )(place, outer, partial, *rims, gates)


def blend(state, update, total):
    return ((1.0 - update) * state.astype(f32) + update * jnp.tanh(total)).astype(bf16)


def cand_kernel(
    place_ref, reset_outer, reset_inner, low_ref, high_ref, motion_near, motion_far, inner_ref,
    update_ref, pairs_ref, out_ref, partial_ref, motion_rim,
):
    blocks, depth, wide = pairs_ref.shape
    ch = wide // 2
    half = (blocks - 1) // 2
    near = half * place_ref[1]
    motion_rim[pl.ds(near, half)] = motion_near[...]
    motion_rim[pl.ds(half - near, half)] = motion_far[...]
    reset = banded(reset_outer, reset_inner, half)
    sources = (reset, state_rows(low_ref, high_ref))
    rows = len(reset)
    weights = lambda first, last: pairs_ref[pl.ds(first, last - first)].reshape(-1, wide)
    sums = {}
    for y in range(half, rows - half, 2):
        rows_read = range(y - half, y + half + 2)
        sums[y] = dotf(stack(sources, rows_read), weights(0, blocks))
    rim = state_rows(motion_rim)
    flow_weights = lambda first, last: pairs_ref[pl.ds(first, last - first), ch:, :].reshape(
        -1, wide
    )
    for i, y in enumerate((0, rows - half)):
        first, last = max(y - half, 0), min(y + half + 2, rows)
        total = dotf(stack(sources, range(first, last)), weights(first - y + half, last - y + half))
        at = (0, half) if i == 0 else (blocks - half, blocks)
        total += dotf(stack((rim,), range(half * i, half * i + half)), flow_weights(*at))
        partial_ref[2 * i], partial_ref[2 * i + 1] = total[:, :ch], total[:, ch:]
    for y in range(half, rows - half, 2):
        for k in range(2):
            i = y - half + k
            total = sums[y][:, k * ch : (k + 1) * ch]
            out_ref[i] = blend(inner_ref[i], update_ref[i], total)


def inner_states(place, resets, low, high, motion_rims, inner, update, pairs):
    count, width, ch = inner.shape
    half = (pairs.shape[0] - 1) // 2
    return pl.pallas_call(
        cand_kernel,
        in_specs=[IN_SMEM] + [IN_VMEM] * 9,
        out_specs=[IN_VMEM] * 2,
        out_shape=[
            jax.ShapeDtypeStruct((count, width, ch), bf16),
            jax.ShapeDtypeStruct((2 * half, width, ch), f32),
        ],
        scratch_shapes=[pltpu.VMEM((2 * half, width, ch), bf16)],
        compiler_params=params(16),
        name="inner_states",
    )(place, *resets, low, high, *motion_rims, inner, update, pairs)


def final_kernel(
    place_ref, inner_ref, reset_near, reset_far, outer_ref, update_ref, partial_ref, pairs_ref,
    out_ref, reset_rim, done, sems,
):
    blocks, _, wide = pairs_ref.shape
    ch = wide // 2
    half = (blocks - 1) // 2
    rows = out_ref.shape[1]
    count = inner_ref.shape[0]
    stores = [pltpu.make_async_copy(inner_ref, out_ref.at[0, pl.ds(half, count)], sems.at[0])]
    stores[0].start()
    near = half * place_ref[1]
    reset_rim[pl.ds(near, half)] = reset_near[...]
    reset_rim[pl.ds(half - near, half)] = reset_far[...]
    rim = state_rows(reset_rim)
    sums = []
    for i in range(2):
        first = 0 if i == 0 else blocks - half
        weights = pairs_ref[pl.ds(first, half), :ch, :].reshape(-1, wide)
        sums.append(dotf(stack((rim,), range(half * i, half * i + half)), weights))
    for i in range(2):
        for k in range(2):
            at = 2 * i + k
            total = partial_ref[at] + sums[i][:, k * ch : (k + 1) * ch]
            done[at] = blend(outer_ref[at], update_ref[at], total)
        target = out_ref.at[0, pl.ds(0 if i == 0 else rows - half, half)]
        stores.append(pltpu.make_async_copy(done.at[pl.ds(half * i, half)], target, sems.at[i + 1]))
        stores[-1].start()
    for store in stores:
        store.wait()


def final_states(place, inner, reset_rims, outer, update, partial, pairs):
    count, width, ch = outer.shape
    rows = count + inner.shape[0]
    return pl.pallas_call(
        final_kernel,
        in_specs=[IN_SMEM] + [IN_VMEM] * 7,
        out_specs=IN_HBM,
        out_shape=jax.ShapeDtypeStruct((1, rows, width, ch), bf16),
        scratch_shapes=[pltpu.VMEM((count, width, ch), bf16)] * 2 + [pltpu.SemaphoreType.DMA((3,))],
        compiler_params=params(16),
        name="final_states",
    )(place, inner, *reset_rims, outer, update, partial, pairs)


def shards(
    left_feats, right_feats, prev_hidden, warp_list, enc_weight, hgate_w, hcand_w, vgate_w, vcand_w
):
    rows = prev_hidden.shape[1]
    half = vgate_w.shape[0] // 2
    outer_rows = (*range(half), *range(rows - half, rows))
    inner_rows = tuple(range(half, rows - half))
    right = lax.axis_index("cols")
    below = 1 - lax.axis_index("rows") % 2
    place = jnp.stack([right, below]).astype(jnp.int32)
    swap_cols = lambda value: lax.ppermute(value, "cols", [(0, 1), (1, 0)])
    swap_rows = lambda near, far: (swap_near(near, "rows"), swap_far(far, "rows"))
    pinned = lax.optimization_barrier

    warp_list = jnp.transpose(warp_list, (0, 2, 3, 1))
    edge = lax.ppermute(right_feats, "cols", [(0, 1)])
    lists = swap_rows(warp_list, warp_list)
    low = motion_of(0, rows // 2, left_feats, right_feats, edge, enc_weight)
    pairs = pairs_of(vcand_w)
    lists, low, pairs = pinned((lists, low, pairs))
    blocks = gather_blocks(place, *lists, prev_hidden)
    edge, blocks = pinned((edge, blocks))
    near, far = swap_rows(*blocks)
    high = motion_of(rows // 2, rows // 2, left_feats, right_feats, edge, enc_weight)
    high, edges = pinned((high, edges_of(place, low, high, half)))
    motion_rims = swap_rows(*edges)
    seam = seam_of(place, warp_list, prev_hidden, near, far, low, high)
    near, seam = pinned((near, seam))
    warped = warp_of(place, warp_list, prev_hidden, near, far)
    seam = swap_cols(seam)
    outer, *edges = horizontal_pass(
        outer_rows, True, place, warped, low, high, seam, hgate_w, hcand_w
    )
    warped, edges = pinned((warped, edges))
    hidden_rims = swap_rows(*edges)
    (inner,) = horizontal_pass(
        inner_rows, False, place, warped, low, high, seam, hgate_w, hcand_w
    )
    update_inner, reset_inner, partial = inner_gates(outer, inner, low, high, vgate_w)
    update_outer, reset_outer, *edges = outer_gates(
        place, outer, partial, hidden_rims + motion_rims, vgate_w
    )
    reset_inner, edges = pinned((reset_inner, edges))
    reset_rims = swap_rows(*edges)
    inner, partial = inner_states(
        place, (reset_outer, reset_inner), low, high, motion_rims, inner, update_inner, pairs
    )
    return final_states(place, inner, reset_rims, outer, update_outer, partial, pairs)


def solution(mesh):
    spread = P(("groups", "cams"), "rows", "cols", None)
    return jax.shard_map(
        shards,
        mesh=mesh,
        in_specs=(spread,) * 4 + (P(),) * 5,
        out_specs=spread,
        check_vma=False,
    )
```

profile of v0, /device:TPU:8, one launch (start us, length us, event | category | flops | bytes accessed | tf_op | source)
XLA Modules:
  0.0 54.9 jit_solution(4736465249728703526)
XLA Ops:
  0.0 1.8 %collective-permute-start = (bf16[1,8,512,128]{3,2,1,0:T(8,128)(2,1)}, bf16[1,8,512,128]{3,2,1,0:T(8,128)(2,1)S(1)}, u32[]{:S(2)}, u32[]{:S(2)}) collective-permute-start(bf16[1,8,512,128]{3,2,1,0:T(8,128)(2,1)} %right_feats.3), channel_id=1, source_target_pairs={{0,1},{2,3},{4,5},{6,7},{8,9},{10,11},{12,13},{14,15},{16,17},{18,... | collective-permute-start | bytes 3145736 | tf_op jit(solution)/shard_map/ppermute | solution.py:594
  1.8 3.5 %collective-permute-start.2 = (s32[1,4,4,8]{3,2,1,0:T(4,128)}, s32[1,4,4,8]{3,2,1,0:T(4,128)S(1)}, u32[]{:S(2)}, u32[]{:S(2)}) collective-permute-start(s32[1,4,4,8]{3,2,1,0:T(4,128)} %bitcast.3), channel_id=1, source_target_pairs={{4,8},{8,4},{5,9},{9,5},{6,10},{10,6},{7,11},{11,7},{20,24},{24,20... | collective-permute-start | bytes 1544 | tf_op jit(solution)/shard_map/ppermute | solution.py:38
  5.3 0.1 collective-permute-start.1
  5.4 0.1 pad_add_fusion.place_ref
  5.5 1.0 %copy-done.4 = bf16[5,256,128]{2,1,0:T(8,128)(2,1)S(1)} copy-done((bf16[5,256,128]{2,1,0:T(8,128)(2,1)S(1)}, bf16[5,256,128]{2,1,0:T(8,128)(2,1)}, u32[]{:S(2)}) %copy-start.4) | copy-done | bytes 327704
  6.4 0.1 pairs.1.pairs_ref
  6.5 0.0 collective-permute-done.edge_ref
  6.6 0.0 copy-start.5
  6.6 0.8 %copy-done.5 = bf16[192,128]{1,0:T(8,128)(2,1)S(1)} copy-done((bf16[192,128]{1,0:T(8,128)(2,1)S(1)}, bf16[192,128]{1,0:T(8,128)(2,1)}, u32[]{:S(2)}) %copy-start.5) | copy-done | bytes 49176
  7.4 2.6 %motion.2.low_ref = bf16[4,512,128]{2,1,0:T(8,128)(2,1)S(1)} custom-call(bf16[1,8,512,128]{3,2,1,0:T(8,128)(2,1)} %left_feats.3, bf16[1,8,512,128]{3,2,1,0:T(8,128)(2,1)} %right_feats.3, bf16[1,8,512,128]{3,2,1,0:T(8,128)(2,1)S(1)} %collective-permute-done.edge_ref, bf16[192,128]{1,0:T(8,128)(2,1)S(1)} %copy-done.5), custom_call_target="tpu_custom_call" | custom-call | tf_op jit(solution)/shard_map/motion/pallas_call | solution.py:117
  10.0 0.0 collective-permute-done.2.far_list
  10.0 0.0 collective-permute-done.1.near_list
  10.0 2.7 %gather.1 = (bf16[8,128,128]{2,1,0:T(8,128)(2,1)S(1)}, bf16[8,128,128]{2,1,0:T(8,128)(2,1)S(1)}) custom-call(s32[2]{0:T(128)S(1)} %pad_add_fusion.place_ref, s32[1,4,4,8]{3,2,1,0:T(4,128)S(1)} %collective-permute-done.1.near_list, s32[1,4,4,8]{3,2,1,0:T(4,128)S(1)} %collective-permute-done.2.far_list, bf16[1,8,512,128]{3,2,1,0:T(8,128)(2,1)} %prev_ref.5), custom_call_target="tpu_custom_call" | custom-call | tf_op jit(solution)/shard_map/gather/pallas_call | solution.py:191
  12.7 0.0 copy-start
  12.7 0.0 copy-start.7
  12.7 2.2 %collective-permute-start.3 = (bf16[8,128,128]{2,1,0:T(8,128)(2,1)S(1)}, bf16[8,128,128]{2,1,0:T(8,128)(2,1)S(1)}, u32[]{:S(2)}, u32[]{:S(2)}) collective-permute-start(bf16[8,128,128]{2,1,0:T(8,128)(2,1)S(1)} %get-tuple-element.43), channel_id=1, source_target_pairs={{0,4},{4,0},{8,12},{12,8},{1,5},{5,1},{9,13},{13,9},{2,6},{6,2},{1... | collective-permute-start | bytes 786440 | tf_op jit(solution)/shard_map/ppermute | solution.py:30
  15.0 2.3 %collective-permute-start.4 = (bf16[8,128,128]{2,1,0:T(8,128)(2,1)S(1)}, bf16[8,128,128]{2,1,0:T(8,128)(2,1)S(1)}, u32[]{:S(2)}, u32[]{:S(2)}) collective-permute-start(bf16[8,128,128]{2,1,0:T(8,128)(2,1)S(1)} %get-tuple-element.44), channel_id=1, source_target_pairs={{4,8},{8,4},{5,9},{9,5},{6,10},{10,6},{7,11},{11,7},{20,24},{24,20... | collective-permute-start | bytes 786440 | tf_op jit(solution)/shard_map/ppermute | solution.py:38
  17.3 0.0 copy-done.6
  17.3 2.6 %motion.3.high_ref = bf16[4,512,128]{2,1,0:T(8,128)(2,1)S(1)} custom-call(bf16[1,8,512,128]{3,2,1,0:T(8,128)(2,1)} %left_feats.3, bf16[1,8,512,128]{3,2,1,0:T(8,128)(2,1)} %right_feats.3, bf16[1,8,512,128]{3,2,1,0:T(8,128)(2,1)S(1)} %collective-permute-done.edge_ref, bf16[192,128]{1,0:T(8,128)(2,1)S(1)} %copy-done.6), custom_call_target="tpu_custom_call" | custom-call | tf_op jit(solution)/shard_map/motion/pallas_call | solution.py:117
  20.0 0.6 %edges.1 = (bf16[2,512,128]{2,1,0:T(8,128)(2,1)S(1)}, bf16[2,512,128]{2,1,0:T(8,128)(2,1)S(1)}) custom-call(s32[2]{0:T(128)S(1)} %pad_add_fusion.place_ref, bf16[4,512,128]{2,1,0:T(8,128)(2,1)S(1)} %motion.2.low_ref, bf16[4,512,128]{2,1,0:T(8,128)(2,1)S(1)} %motion.3.high_ref), custom_call_target="tpu_custom_call" | custom-call | tf_op jit(solution)/shard_map/edges/pallas_call | solution.py:142
  20.6 0.0 copy-start.2
  20.6 0.0 copy-start.3
  20.6 0.0 collective-permute-done.3.near_ref
  20.6 2.9 %collective-permute-done.4.far_ref = bf16[8,128,128]{2,1,0:T(8,128)(2,1)S(1)} collective-permute-done((bf16[8,128,128]{2,1,0:T(8,128)(2,1)S(1)}, bf16[8,128,128]{2,1,0:T(8,128)(2,1)S(1)}, u32[]{:S(2)}, u32[]{:S(2)}) %collective-permute-start.4) | collective-permute-done | bytes 262176 | tf_op jit(solution)/shard_map/ppermute | solution.py:38
  23.6 0.9 %seam.1 = bf16[8,16,256]{2,1,0:T(8,128)(2,1)S(1)} custom-call(s32[2]{0:T(128)S(1)} %pad_add_fusion.place_ref, s32[1,4,4,8]{3,2,1,0:T(4,128)S(1)} %bitcast.5, bf16[1,8,512,128]{3,2,1,0:T(8,128)(2,1)S(1)} %copy-done, bf16[8,128,128]{2,1,0:T(8,128)(2,1)S(1)} %collective-permute-done.3.near_ref, bf16[8,128,128]{2,1,0:T(8,128)(2,1)S(1)} %collective-permute-done.4.far_ref, ...), custom_call_target="tpu_custom_call" | custom-call | tf_op jit(solution)/shard_map/seam/pallas_call | solution.py:244
  24.4 0.1 collective-permute-start.5
  24.5 0.1 collective-permute-start.8
  24.6 2.4 %collective-permute-start.9 = (bf16[2,512,128]{2,1,0:T(8,128)(2,1)S(1)}, bf16[2,512,128]{2,1,0:T(8,128)(2,1)S(1)}, u32[]{:S(2)}, u32[]{:S(2)}) collective-permute-start(bf16[2,512,128]{2,1,0:T(8,128)(2,1)S(1)} %get-tuple-element.60), channel_id=1, source_target_pairs={{4,8},{8,4},{5,9},{9,5},{6,10},{10,6},{7,11},{11,7},{20,24},{24,20... | collective-permute-start | bytes 786440 | tf_op jit(solution)/shard_map/ppermute | solution.py:38
  27.0 1.2 %warp.1.hidden_ref = bf16[8,512,128]{2,1,0:T(8,128)(2,1)S(1)} custom-call(s32[2]{0:T(128)S(1)} %pad_add_fusion.place_ref, s32[1,4,4,8]{3,2,1,0:T(4,128)S(1)} %bitcast.6, bf16[1,8,512,128]{3,2,1,0:T(8,128)(2,1)S(1)} %copy-done, bf16[8,128,128]{2,1,0:T(8,128)(2,1)S(1)} %collective-permute-done.3.near_ref, bf16[8,128,128]{2,1,0:T(8,128)(2,1)S(1)} %collective-permute-done.4.far_ref), custom_call_target="tpu_custom_call" | custom-call | tf_op jit(solution)/shard_map/warp/pallas_call | solution.py:270
  28.1 0.0 collective-permute-done.5.seam_ref
  28.1 0.0 copy-done.2
  28.2 3.5 %horizontal.2 = (bf16[4,512,128]{2,1,0:T(8,128)(2,1)S(1)}, bf16[2,512,128]{2,1,0:T(8,128)(2,1)S(1)}, bf16[2,512,128]{2,1,0:T(8,128)(2,1)S(1)}) custom-call(s32[2]{0:T(128)S(1)} %pad_add_fusion.place_ref, bf16[8,512,128]{2,1,0:T(8,128)(2,1)S(1)} %warp.1.hidden_ref, bf16[4,512,128]{2,1,0:T(8,128)(2,1)S(1)} %motion.2.low_ref, ...), custom_call_target="tpu_custom_call" | custom-call | tf_op jit(solution)/shard_map/horizontal/pallas_call | solution.py:348
  31.7 0.0 copy-start.1
  31.7 0.4 collective-permute-start.6
  32.1 3.5 %collective-permute-start.7 = (bf16[2,512,128]{2,1,0:T(8,128)(2,1)S(1)}, bf16[2,512,128]{2,1,0:T(8,128)(2,1)S(1)}, u32[]{:S(2)}, u32[]{:S(2)}) collective-permute-start(bf16[2,512,128]{2,1,0:T(8,128)(2,1)S(1)} %get-tuple-element.58), channel_id=1, source_target_pairs={{4,8},{8,4},{5,9},{9,5},{6,10},{10,6},{7,11},{11,7},{20,24},{24,20... | collective-permute-start | bytes 786440 | tf_op jit(solution)/shard_map/ppermute | solution.py:38
  35.6 3.5 %horizontal.3.inner_ref = bf16[4,512,128]{2,1,0:T(8,128)(2,1)S(1)} custom-call(s32[2]{0:T(128)S(1)} %pad_add_fusion.place_ref, bf16[8,512,128]{2,1,0:T(8,128)(2,1)S(1)} %warp.1.hidden_ref, bf16[4,512,128]{2,1,0:T(8,128)(2,1)S(1)} %motion.2.low_ref, bf16[4,512,128]{2,1,0:T(8,128)(2,1)S(1)} %motion.3.high_ref, ...), custom_call_target="tpu_custom_call" | custom-call | tf_op jit(solution)/shard_map/horizontal/pallas_call | solution.py:348
  39.1 2.5 %inner_gates.1 = (f32[4,512,128]{2,1,0:T(8,128)S(1)}, bf16[4,512,128]{2,1,0:T(8,128)(2,1)S(1)}, f32[4,512,256]{2,1,0:T(8,128)S(1)}) custom-call(bf16[4,512,128]{2,1,0:T(8,128)(2,1)S(1)} %get-tuple-element.52.outer_ref, bf16[4,512,128]{2,1,0:T(8,128)(2,1)S(1)} %horizontal.3.inner_ref, bf16[4,512,128]{2,1,0:T(8,128)(2,1)S(1)} %motion.2.low_ref, ...), custom_call_target="tpu_custom_call" | custom-call | tf_op jit(solution)/shard_map/inner_gates/pallas_call | solution.py:420
  41.5 0.0 collective-permute-done.8.motion_near
  41.6 0.0 collective-permute-done.9.motion_far
  41.6 0.0 collective-permute-done.6.hidden_near
  41.6 0.6 %collective-permute-done.7.hidden_far = bf16[2,512,128]{2,1,0:T(8,128)(2,1)S(1)} collective-permute-done((bf16[2,512,128]{2,1,0:T(8,128)(2,1)S(1)}, bf16[2,512,128]{2,1,0:T(8,128)(2,1)S(1)}, u32[]{:S(2)}, u32[]{:S(2)}) %collective-permute-start.7) | collective-permute-done | bytes 262176 | tf_op jit(solution)/shard_map/ppermute | solution.py:38
  42.2 1.3 %outer_gates.1 = (f32[4,512,128]{2,1,0:T(8,128)S(1)}, bf16[4,512,128]{2,1,0:T(8,128)(2,1)S(1)}, bf16[2,512,128]{2,1,0:T(8,128)(2,1)S(1)}, bf16[2,512,128]{2,1,0:T(8,128)(2,1)S(1)}) custom-call(s32[2]{0:T(128)S(1)} %pad_add_fusion.place_ref, bf16[4,512,128]{2,1,0:T(8,128)(2,1)S(1)} %get-tuple-element.52.outer_ref, ...), custom_call_target="tpu_custom_call" | custom-call | tf_op jit(solution)/shard_map/outer_gates/pallas_call | solution.py:466
  43.5 0.1 collective-permute-start.10
  43.6 3.5 %collective-permute-start.11 = (bf16[2,512,128]{2,1,0:T(8,128)(2,1)S(1)}, bf16[2,512,128]{2,1,0:T(8,128)(2,1)S(1)}, u32[]{:S(2)}, u32[]{:S(2)}) collective-permute-start(bf16[2,512,128]{2,1,0:T(8,128)(2,1)S(1)} %get-tuple-element.70), channel_id=1, source_target_pairs={{4,8},{8,4},{5,9},{9,5},{6,10},{10,6},{7,11},{11,7},{20,24},{24,20... | collective-permute-start | bytes 786440 | tf_op jit(solution)/shard_map/ppermute | solution.py:38
  47.0 2.3 %inner_states.1 = (bf16[4,512,128]{2,1,0:T(8,128)(2,1)S(1)}, f32[4,512,128]{2,1,0:T(8,128)S(1)}) custom-call(s32[2]{0:T(128)S(1)} %pad_add_fusion.place_ref, bf16[4,512,128]{2,1,0:T(8,128)(2,1)S(1)} %get-tuple-element.61.reset_outer, bf16[4,512,128]{2,1,0:T(8,128)(2,1)S(1)} %get-tuple-element.65.reset_inner, bf16[4,512,128]{2,1,0:T(8,128)(2,1)S(1)} %motion.2.low_ref, ...), custom_call_target="tpu_custom_call" | custom-call | tf_op jit(solution)/shard_map/inner_states/pallas_call | solution.py:519
  49.3 1.7 %collective-permute-done.10.reset_near = bf16[2,512,128]{2,1,0:T(8,128)(2,1)S(1)} collective-permute-done((bf16[2,512,128]{2,1,0:T(8,128)(2,1)S(1)}, bf16[2,512,128]{2,1,0:T(8,128)(2,1)S(1)}, u32[]{:S(2)}, u32[]{:S(2)}) %collective-permute-start.10) | collective-permute-done | bytes 262176 | tf_op jit(solution)/shard_map/ppermute | solution.py:30
  51.0 1.9 %collective-permute-done.11.reset_far = bf16[2,512,128]{2,1,0:T(8,128)(2,1)S(1)} collective-permute-done((bf16[2,512,128]{2,1,0:T(8,128)(2,1)S(1)}, bf16[2,512,128]{2,1,0:T(8,128)(2,1)S(1)}, u32[]{:S(2)}, u32[]{:S(2)}) %collective-permute-start.11) | collective-permute-done | bytes 262176 | tf_op jit(solution)/shard_map/ppermute | solution.py:38
  52.9 1.8 %final_states.1 = bf16[1,8,512,128]{3,2,1,0:T(8,128)(2,1)} custom-call(s32[2]{0:T(128)S(1)} %pad_add_fusion.place_ref, bf16[4,512,128]{2,1,0:T(8,128)(2,1)S(1)} %get-tuple-element.68.inner_ref, bf16[2,512,128]{2,1,0:T(8,128)(2,1)S(1)} %collective-permute-done.10.reset_near, bf16[2,512,128]{2,1,0:T(8,128)(2,1)S(1)} %collective-permute-done.11.reset_far, ...), custom_call_target="tpu_custom_call" | custom-call | tf_op jit(solution)/shard_map/final_states/pallas_call | solution.py:568
  (6 shorter events, 0.0 us)
Async XLA Ops:
  0.0 6.5 %collective-permute-start = (bf16[1,8,512,128]{3,2,1,0:T(8,128)(2,1)}, bf16[1,8,512,128]{3,2,1,0:T(8,128)(2,1)S(1)}, u32[]{:S(2)}, u32[]{:S(2)}) collective-permute-start(bf16[1,8,512,128]{3,2,1,0:T(8,128)(2,1)} %right_feats.3), channel_id=1, source_target_pairs={{0,1},{2,3},{4,5},{6,7},{8,9},{10,11},{12,13},{14,15},{16,17},{18,... | collective-permute-start | bytes 3145736 | tf_op jit(solution)/shard_map/ppermute | solution.py:594
  1.8 8.2 %collective-permute-start.2 = (s32[1,4,4,8]{3,2,1,0:T(4,128)}, s32[1,4,4,8]{3,2,1,0:T(4,128)S(1)}, u32[]{:S(2)}, u32[]{:S(2)}) collective-permute-start(s32[1,4,4,8]{3,2,1,0:T(4,128)} %bitcast.3), channel_id=1, source_target_pairs={{4,8},{8,4},{5,9},{9,5},{6,10},{10,6},{7,11},{11,7},{20,24},{24,20... | collective-permute-start | bytes 1544 | tf_op jit(solution)/shard_map/ppermute | solution.py:38
  5.3 4.7 %collective-permute-start.1 = (s32[1,4,4,8]{3,2,1,0:T(4,128)}, s32[1,4,4,8]{3,2,1,0:T(4,128)S(1)}, u32[]{:S(2)}, u32[]{:S(2)}) collective-permute-start(s32[1,4,4,8]{3,2,1,0:T(4,128)} %bitcast.4), channel_id=1, source_target_pairs={{0,4},{4,0},{8,12},{12,8},{1,5},{5,1},{9,13},{13,9},{2,6},{6,2},{1... | collective-permute-start | bytes 1544 | tf_op jit(solution)/shard_map/ppermute | solution.py:30
  5.5 1.0 %copy-start.4 = (bf16[5,256,128]{2,1,0:T(8,128)(2,1)S(1)}, bf16[5,256,128]{2,1,0:T(8,128)(2,1)}, u32[]{:S(2)}) copy-start(bf16[5,256,128]{2,1,0:T(8,128)(2,1)} %cand_ref.3) | copy-start | bytes 983044
  6.6 0.8 %copy-start.5 = (bf16[192,128]{1,0:T(8,128)(2,1)S(1)}, bf16[192,128]{1,0:T(8,128)(2,1)}, u32[]{:S(2)}) copy-start(bf16[192,128]{1,0:T(8,128)(2,1)} %weight_ref.3) | copy-start | bytes 147460
  7.4 10.0 %copy-start.6 = (bf16[192,128]{1,0:T(8,128)(2,1)S(1)}, bf16[192,128]{1,0:T(8,128)(2,1)}, u32[]{:S(2)}) copy-start(bf16[192,128]{1,0:T(8,128)(2,1)} %weight_ref.3) | copy-start | bytes 147460
  12.7 10.8 %copy-start = (bf16[1,8,512,128]{3,2,1,0:T(8,128)(2,1)S(1)}, bf16[1,8,512,128]{3,2,1,0:T(8,128)(2,1)}, u32[]{:S(2)}) copy-start(bf16[1,8,512,128]{3,2,1,0:T(8,128)(2,1)} %prev_ref.5) | copy-start | bytes 3145732
  12.7 10.8 %copy-start.7 = (s32[1,8,4,4]{1,3,2,0:T(4,128)S(1)}, s32[1,8,4,4]{1,3,2,0:T(4,128)}, u32[]{:S(2)}) copy-start(s32[1,8,4,4]{1,3,2,0:T(4,128)} %param.12) | copy-start | bytes 1540
  12.7 7.9 %collective-permute-start.3 = (bf16[8,128,128]{2,1,0:T(8,128)(2,1)S(1)}, bf16[8,128,128]{2,1,0:T(8,128)(2,1)S(1)}, u32[]{:S(2)}, u32[]{:S(2)}) collective-permute-start(bf16[8,128,128]{2,1,0:T(8,128)(2,1)S(1)} %get-tuple-element.43), channel_id=1, source_target_pairs={{0,4},{4,0},{8,12},{12,8},{1,5},{5,1},{9,13},{13,9},{2,6},{6,2},{1... | collective-permute-start | bytes 786440 | tf_op jit(solution)/shard_map/ppermute | solution.py:30
  15.0 8.6 %collective-permute-start.4 = (bf16[8,128,128]{2,1,0:T(8,128)(2,1)S(1)}, bf16[8,128,128]{2,1,0:T(8,128)(2,1)S(1)}, u32[]{:S(2)}, u32[]{:S(2)}) collective-permute-start(bf16[8,128,128]{2,1,0:T(8,128)(2,1)S(1)} %get-tuple-element.44), channel_id=1, source_target_pairs={{4,8},{8,4},{5,9},{9,5},{6,10},{10,6},{7,11},{11,7},{20,24},{24,20... | collective-permute-start | bytes 786440 | tf_op jit(solution)/shard_map/ppermute | solution.py:38
  20.6 7.5 %copy-start.2 = (bf16[5,256,256]{2,1,0:T(8,128)(2,1)S(1)}, bf16[5,256,256]{2,1,0:T(8,128)(2,1)}, u32[]{:S(2)}) copy-start(bf16[5,256,256]{2,1,0:T(8,128)(2,1)} %gates_ref.5) | copy-start | bytes 1966084
  20.6 7.5 %copy-start.3 = (bf16[5,256,128]{2,1,0:T(8,128)(2,1)S(1)}, bf16[5,256,128]{2,1,0:T(8,128)(2,1)}, u32[]{:S(2)}) copy-start(bf16[5,256,128]{2,1,0:T(8,128)(2,1)} %cand_ref.5) | copy-start | bytes 983044
  24.4 3.7 %collective-permute-start.5 = (bf16[8,16,256]{2,1,0:T(8,128)(2,1)S(1)}, bf16[8,16,256]{2,1,0:T(8,128)(2,1)S(1)}, u32[]{:S(2)}, u32[]{:S(2)}) collective-permute-start(bf16[8,16,256]{2,1,0:T(8,128)(2,1)S(1)} %seam.1), channel_id=1, source_target_pairs={{0,1},{1,0},{2,3},{3,2},{4,5},{5,4},{6,7},{7,6},{8,9},{9,8},{10,11... | collective-permute-start | bytes 196616 | tf_op jit(solution)/shard_map/ppermute | solution.py:589
  24.5 17.0 %collective-permute-start.8 = (bf16[2,512,128]{2,1,0:T(8,128)(2,1)S(1)}, bf16[2,512,128]{2,1,0:T(8,128)(2,1)S(1)}, u32[]{:S(2)}, u32[]{:S(2)}) collective-permute-start(bf16[2,512,128]{2,1,0:T(8,128)(2,1)S(1)} %get-tuple-element.59), channel_id=1, source_target_pairs={{0,4},{4,0},{8,12},{12,8},{1,5},{5,1},{9,13},{13,9},{2,6},{6,2},{1... | collective-permute-start | bytes 786440 | tf_op jit(solution)/shard_map/ppermute | solution.py:30
  24.6 17.0 %collective-permute-start.9 = (bf16[2,512,128]{2,1,0:T(8,128)(2,1)S(1)}, bf16[2,512,128]{2,1,0:T(8,128)(2,1)S(1)}, u32[]{:S(2)}, u32[]{:S(2)}) collective-permute-start(bf16[2,512,128]{2,1,0:T(8,128)(2,1)S(1)} %get-tuple-element.60), channel_id=1, source_target_pairs={{4,8},{8,4},{5,9},{9,5},{6,10},{10,6},{7,11},{11,7},{20,24},{24,20... | collective-permute-start | bytes 786440 | tf_op jit(solution)/shard_map/ppermute | solution.py:38
  31.7 7.4 %copy-start.1 = (bf16[5,256,256]{2,1,0:T(8,128)(2,1)S(1)}, bf16[5,256,256]{2,1,0:T(8,128)(2,1)}, u32[]{:S(2)}) copy-start(bf16[5,256,256]{2,1,0:T(8,128)(2,1)} %gates_ref.7) | copy-start | bytes 1966084
  31.7 9.9 %collective-permute-start.6 = (bf16[2,512,128]{2,1,0:T(8,128)(2,1)S(1)}, bf16[2,512,128]{2,1,0:T(8,128)(2,1)S(1)}, u32[]{:S(2)}, u32[]{:S(2)}) collective-permute-start(bf16[2,512,128]{2,1,0:T(8,128)(2,1)S(1)} %get-tuple-element.57), channel_id=1, source_target_pairs={{0,4},{4,0},{8,12},{12,8},{1,5},{5,1},{9,13},{13,9},{2,6},{6,2},{1... | collective-permute-start | bytes 786440 | tf_op jit(solution)/shard_map/ppermute | solution.py:30
  32.1 10.1 %collective-permute-start.7 = (bf16[2,512,128]{2,1,0:T(8,128)(2,1)S(1)}, bf16[2,512,128]{2,1,0:T(8,128)(2,1)S(1)}, u32[]{:S(2)}, u32[]{:S(2)}) collective-permute-start(bf16[2,512,128]{2,1,0:T(8,128)(2,1)S(1)} %get-tuple-element.58), channel_id=1, source_target_pairs={{4,8},{8,4},{5,9},{9,5},{6,10},{10,6},{7,11},{11,7},{20,24},{24,20... | collective-permute-start | bytes 786440 | tf_op jit(solution)/shard_map/ppermute | solution.py:38
  43.5 7.6 %collective-permute-start.10 = (bf16[2,512,128]{2,1,0:T(8,128)(2,1)S(1)}, bf16[2,512,128]{2,1,0:T(8,128)(2,1)S(1)}, u32[]{:S(2)}, u32[]{:S(2)}) collective-permute-start(bf16[2,512,128]{2,1,0:T(8,128)(2,1)S(1)} %get-tuple-element.69), channel_id=1, source_target_pairs={{0,4},{4,0},{8,12},{12,8},{1,5},{5,1},{9,13},{13,9},{2,6},{6,2},{1... | collective-permute-start | bytes 786440 | tf_op jit(solution)/shard_map/ppermute | solution.py:30
  43.6 9.4 %collective-permute-start.11 = (bf16[2,512,128]{2,1,0:T(8,128)(2,1)S(1)}, bf16[2,512,128]{2,1,0:T(8,128)(2,1)S(1)}, u32[]{:S(2)}, u32[]{:S(2)}) collective-permute-start(bf16[2,512,128]{2,1,0:T(8,128)(2,1)S(1)} %get-tuple-element.70), channel_id=1, source_target_pairs={{4,8},{8,4},{5,9},{9,5},{6,10},{10,6},{7,11},{11,7},{20,24},{24,20... | collective-permute-start | bytes 786440 | tf_op jit(solution)/shard_map/ppermute | solution.py:38
where the time goes:
time: 55.4 us; the launch traced here: 54.9 us
  Pallas kernels  25.5 us (46%)
  starting transfers between devices  19.8 us (36%)
  waiting for transfers between devices  7.15 us (13%)
  local copies, waits for them, and re-layouts  1.8 us (3%)
    ppermute x5, starting transfers between devices, swap_far(): return lax.ppermute(value, axis, pairs)  15.1 us
    pallas_call x2, Pallas kernels, horizontal_pass(): pl.pallas_call(functools.partial(horizontal_kernel, rows), in_specs=[IN_S...  6.98 us
    ppermute x5, waiting for transfers between devices, swap_far(): return lax.ppermute(value, axis, pairs)  5.42 us
    pallas_call x2, Pallas kernels, motion_of(): pl.pallas_call(functools.partial(motion_kernel, first), in_specs=[IN_HBM,...  5.25 us
    ppermute x5, starting transfers between devices, swap_near(): return lax.ppermute(value, axis, pairs)  2.84 us
    pallas_call x1, Pallas kernels, gather_blocks(): pl.pallas_call(gather_kernel, in_specs=[IN_SMEM, IN_VMEM, IN_VMEM, IN_HBM...  2.69 us
    pallas_call x1, Pallas kernels, inner_gates(): pl.pallas_call(gates_kernel, in_specs=[IN_VMEM] * 5, out_specs=[IN_VMEM]...  2.48 us
    pallas_call x1, Pallas kernels, inner_states(): pl.pallas_call(cand_kernel, in_specs=[IN_SMEM] + [IN_VMEM] * 9, out_specs...  2.3 us
  transfers between devices with their start and end apart: 12, of which 4 were waited for; matrix products, arithmetic and copies ran while one was open for 0% of the time, Pallas kernels for 34%

commit v1 on v0

--- a/solution.py
+++ b/solution.py
@@ -43,6 +43,14 @@
 IN_HBM = pl.BlockSpec(memory_space=pltpu.HBM)
 
 
+def right_half():
+    return lax.axis_index("cols")
+
+
+def near_below():
+    return 1 - lax.axis_index("rows") % 2
+
+
 def in_hbm(value):
     return pltpu.with_memory_space_constraint(value, pltpu.HBM)
 
@@ -52,7 +60,8 @@
 
 
 def motion_kernel(
-    first, left_feats, right_feats, edge_ref, weight_ref, out_ref, left_ref, window, sems
+    first, left_feats, right_feats, edge_ref, weight, out_ref, left_ref, window,
+    weight_ref, sems,
 ):
     disparities = weight_ref.shape[0]
     rows, width, feats = left_ref.shape
@@ -63,19 +72,23 @@
         pltpu.make_async_copy(
             right_feats.at[0, own], window.at[:, pl.ds(disparities, width), :], sems.at[1]
         ),
+        pltpu.make_async_copy(weight, weight_ref, sems.at[2]),
     ]
     for load in loads:
         load.start()
     far_edge = edge_ref.shape[2] - disparities
     for r in range(rows):
-        window[r, pl.ds(0, disparities), :] = edge_ref[
-            0, first + r, pl.ds(far_edge, disparities), :
-        ]
+        other = edge_ref[0, first + r, pl.ds(far_edge, disparities), :]
+        window[r, pl.ds(0, disparities), :] = jnp.where(
+            right_half() == 1, other, jnp.zeros_like(other)
+        )
     scale = feats**-0.5
     lane = lax.broadcasted_iota(jnp.int32, (tile, tile), 1)
     row = lax.broadcasted_iota(jnp.int32, (tile, tile), 0)
     keep = lane < row
     flip = (lane + row == tile - 1).astype(f32).astype(bf16)
+    for load in loads:
+        load.wait()
     turned = jnp.concatenate(
         [
             dotf(flip, weight_ref[pl.ds(disparities - tile, tile), :]).astype(bf16),
@@ -86,8 +99,6 @@
     span = disparities + tile
     blocks = -(-span // tile)
     tiles = [(r, t * tile) for r in range(rows) for t in range(width // tile)]
-    for load in loads:
-        load.wait()
     flipped = [dotf(flip, left_ref[r, pl.ds(x, tile), :]).astype(bf16) for r, x in tiles]
     scores = [
         lax.dot_general(
@@ -116,66 +127,66 @@
     width, feats = left.shape[2:]
     return pl.pallas_call(
         functools.partial(motion_kernel, first),
-        in_specs=[IN_HBM, IN_HBM, IN_VMEM, IN_VMEM],
+        in_specs=[IN_HBM, IN_HBM, IN_VMEM, IN_HBM],
         out_specs=IN_VMEM,
         out_shape=jax.ShapeDtypeStruct((rows, width, weight.shape[1]), bf16),
         scratch_shapes=[
             pltpu.VMEM((rows, width, feats), bf16),
             pltpu.VMEM((rows, width + 256, feats), bf16),
-            pltpu.SemaphoreType.DMA((2,)),
+            pltpu.VMEM(weight.shape, bf16),
+            pltpu.SemaphoreType.DMA((3,)),
         ],
         compiler_params=params(16),
         name="motion",
-    )(in_hbm(left), in_hbm(right), edge, weight)
-
-
-def edges_kernel(place_ref, low_ref, high_ref, near_ref, far_ref):
+    )(in_hbm(left), in_hbm(right), edge, in_hbm(weight))
+
+
+def edges_kernel(low_ref, high_ref, near_ref, far_ref):
     count = near_ref.shape[0]
     low, high = low_ref[pl.ds(0, count)], high_ref[pl.ds(high_ref.shape[0] - count, count)]
-    below = place_ref[1] == 1
+    below = near_below() == 1
     near_ref[...] = jnp.where(below, high, low)
     far_ref[...] = jnp.where(below, low, high)
 
 
-def edges_of(place, low, high, count):
+def edges_of(low, high, count):
     shape = jax.ShapeDtypeStruct((count,) + low.shape[1:], bf16)
     return pl.pallas_call(
         edges_kernel,
-        in_specs=[IN_SMEM, IN_VMEM, IN_VMEM],
+        in_specs=[IN_VMEM, IN_VMEM],
         out_specs=[IN_VMEM, IN_VMEM],
         out_shape=[shape, shape],
         compiler_params=params(4),
         name="edges",
-    )(place, low, high)
-
-
-def gather_kernel(
-    place_ref, near_list, far_list, prev_ref, near_out, far_out, near_ref, far_ref, picks, sems
-):
-    lists = [
-        pltpu.make_async_copy(near_list, near_ref, sems.at[0, 0]),
-        pltpu.make_async_copy(far_list, far_ref, sems.at[1, 0]),
-    ]
-    for load in lists:
-        load.start()
-    _, band_blocks, _, band_rows = near_ref.shape
+    )(low, high)
+
+
+def gather_kernel(near_list, far_list, prev_ref, near_out, far_out, sems):
+    _, band_blocks, _, band_rows = near_list.shape
     slots, width, _ = near_out.shape
-    sign = 2 * place_ref[1] - 1
+    sign = 2 * near_below() - 1
+    lane = lax.broadcasted_iota(jnp.int32, (1, band_rows), 1)
     copies = []
-    sides = ((near_ref, near_out, sign), (far_ref, far_out, -sign))
+    sides = ((near_list, near_out, sign), (far_list, far_out, -sign))
     for side, (list_ref, out, wanted) in enumerate(sides):
-        lists[side].wait()
-        count, source = jnp.int32(0), jnp.int32(0)
-        for r in range(band_rows):
-            for block in range(band_blocks):
-                hit = list_ref[0, block, 0, r] == wanted
-                count = count + hit.astype(jnp.int32)
-                here = list_ref[0, block, 1, r] * band_blocks + list_ref[0, block, 2, r]
-                source = jnp.where(hit & (count <= slots), here, source)
-                picks[side, jnp.clip(count - 1, 0, slots - 1)] = source
+        before = jnp.zeros((1, 1), jnp.int32)
+        ranks, asked = [], []
+        for block in range(band_blocks):
+            field = lambda k: list_ref[0, block, pl.ds(k, 1), :]
+            hit = (field(0) == wanted).astype(jnp.int32)
+            rank = jnp.broadcast_to(before, (1, band_rows))
+            for r in range(band_rows - 1):
+                rank = rank + jnp.where(lane > r, hit[:, r : r + 1], 0)
+            ranks.append(jnp.where(hit > 0, rank, -1))
+            asked.append(field(1) * band_blocks + field(2))
+            before = before + jnp.sum(hit, axis=1, keepdims=True)
         for slot in range(slots):
-            row = picks[side, slot] // band_blocks
-            column = pl.multiple_of(picks[side, slot] % band_blocks * width, width)
+            found = sum(
+                jnp.where(rank == slot, source, 0) for rank, source in zip(ranks, asked)
+            )
+            source = jnp.sum(found)
+            row = source // band_blocks
+            column = pl.multiple_of(source % band_blocks * width, width)
             block = prev_ref.at[0, row, pl.ds(column, width), :]
             copies.append(pltpu.make_async_copy(block, out.at[slot], sems.at[side, slot]))
             copies[-1].start()
@@ -183,108 +194,112 @@
         copy.wait()
 
 
-def gather_blocks(place, near_list, far_list, prev):
+def gather_blocks(near_list, far_list, prev):
     _, band_blocks, _, band_rows = near_list.shape
     _, _, width, hidden = prev.shape
     slots = band_rows * band_blocks // 4
     shape = jax.ShapeDtypeStruct((slots, width // band_blocks, hidden), bf16)
     return pl.pallas_call(
         gather_kernel,
-        in_specs=[IN_SMEM, IN_VMEM, IN_VMEM, IN_HBM],
+        in_specs=[IN_VMEM, IN_VMEM, IN_HBM],
         out_specs=[IN_VMEM, IN_VMEM],
         out_shape=[shape, shape],
-        scratch_shapes=[pltpu.SMEM(near_list.shape, jnp.int32)] * 2
-        + [pltpu.SMEM((2, slots), jnp.int32), pltpu.SemaphoreType.DMA((2, slots))],
+        scratch_shapes=[pltpu.SemaphoreType.DMA((2, slots))],
         compiler_params=params(4),
         name="gather",
-    )(place, near_list, far_list, in_hbm(prev))
-
-
-def pick_blocks(place_ref, list_ref, visit):
-    _, band_blocks, _, band_rows = list_ref.shape
-    last = band_rows * band_blocks // 4 - 1
-    sign = 2 * place_ref[1] - 1
+    )(near_list, far_list, in_hbm(prev))
+
+
+def pick_blocks(list_ref, rows, blocks, visit):
+    last = rows * blocks // 4 - 1
+    sign = 2 * near_below() - 1
     nears, fars = jnp.int32(0), jnp.int32(0)
-    for row in range(band_rows):
-        for block in range(band_blocks):
-            offset = list_ref[0, block, 0, row]
+    for block in range(blocks):
+        for row in range(rows):
+            field = lambda k: list_ref[(block * 4 + k) * rows + row]
+            offset = field(0)
             is_near, is_far = offset == -sign, offset == sign
-            visit(row, block, is_near, is_far, jnp.minimum(nears, last), jnp.minimum(fars, last))
+            visit(
+                row, block, field, is_near, is_far, jnp.minimum(nears, last),
+                jnp.minimum(fars, last),
+            )
             nears += is_near.astype(jnp.int32)
             fars += is_far.astype(jnp.int32)
 
 
-def seam_kernel(place_ref, list_ref, prev_ref, near_ref, far_ref, low_ref, high_ref, seam_ref):
-    band_blocks = list_ref.shape[1]
+def seam_kernel(list_ref, prev_ref, near_ref, far_ref, low_ref, high_ref, seam_ref):
     width, ch = near_ref.shape[1:]
-    is_left = place_ref[0] == 0
-    start = pl.multiple_of((width - SEAM) * (1 - place_ref[0]), SEAM)
+    rows, total = prev_ref.shape[1:3]
+    band_blocks = total // width
+    is_left = right_half() == 0
+    start = pl.multiple_of((width - SEAM) * (1 - right_half()), SEAM)
     inside = pl.ds(start, SEAM)
 
-    def visit(row, block, is_near, is_far, near_slot, far_slot):
+    def visit(row, block, field, is_near, is_far, near_slot, far_slot):
         if block in (0, band_blocks - 1):
-            source = pl.multiple_of(list_ref[0, block, 2, row] * width + start, SEAM)
-            local = prev_ref[0, list_ref[0, block, 1, row], pl.ds(source, SEAM), :]
+            source = pl.multiple_of(field(2) * width + start, SEAM)
+            local = prev_ref[0, field(1), pl.ds(source, SEAM), :]
             near, far = near_ref[near_slot, inside, :], far_ref[far_slot, inside, :]
             picked = jnp.where(is_near, near, jnp.where(is_far, far, local))
-            picked = jnp.where(list_ref[0, block, 3, row] > 0, picked, jnp.zeros_like(picked))
+            picked = jnp.where(field(3) > 0, picked, jnp.zeros_like(picked))
             if block > 0:
                 picked = jnp.where(is_left, picked, seam_ref[row, :, 0:ch])
             seam_ref[row, :, 0:ch] = picked
 
-    pick_blocks(place_ref, list_ref, visit)
-    edge = pl.multiple_of((band_blocks * width - SEAM) * (1 - place_ref[0]), SEAM)
+    pick_blocks(list_ref, rows, band_blocks, visit)
+    edge = pl.multiple_of((band_blocks * width - SEAM) * (1 - right_half()), SEAM)
     half = low_ref.shape[0]
     seam_ref[pl.ds(0, half), :, ch : 2 * ch] = low_ref[:, pl.ds(edge, SEAM), :]
     seam_ref[pl.ds(half, half), :, ch : 2 * ch] = high_ref[:, pl.ds(edge, SEAM), :]
 
 
-def seam_of(place, warp_list, prev, near, far, low, high):
+def seam_of(warp_list, prev, near, far, low, high):
     _, rows, _, ch = prev.shape
     return pl.pallas_call(
         seam_kernel,
-        in_specs=[IN_SMEM, IN_SMEM] + [IN_VMEM] * 5,
+        in_specs=[IN_SMEM] + [IN_VMEM] * 5,
         out_specs=IN_VMEM,
         out_shape=jax.ShapeDtypeStruct((rows, SEAM, 2 * ch), bf16),
         compiler_params=params(4),
         name="seam",
-    )(place, warp_list, prev, near, far, low, high)
-
-
-def warp_kernel(place_ref, list_ref, prev_ref, near_ref, far_ref, out_ref):
+    )(warp_list, prev, near, far, low, high)
+
+
+def warp_kernel(list_ref, prev_ref, near_ref, far_ref, out_ref):
     width = near_ref.shape[1]
 
-    def visit(row, block, is_near, is_far, near_slot, far_slot):
-        column = pl.multiple_of(list_ref[0, block, 2, row] * width, width)
-        local = prev_ref[0, list_ref[0, block, 1, row], pl.ds(column, width), :]
+    def visit(row, block, field, is_near, is_far, near_slot, far_slot):
+        column = pl.multiple_of(field(2) * width, width)
+        local = prev_ref[0, field(1), pl.ds(column, width), :]
         picked = jnp.where(
             is_near, near_ref[near_slot], jnp.where(is_far, far_ref[far_slot], local)
         )
-        picked = jnp.where(list_ref[0, block, 3, row] > 0, picked, jnp.zeros_like(picked))
+        picked = jnp.where(field(3) > 0, picked, jnp.zeros_like(picked))
         out_ref[row, pl.ds(block * width, width), :] = picked
 
-    pick_blocks(place_ref, list_ref, visit)
-
-
-def warp_of(place, warp_list, prev, near, far):
+    rows, total = prev_ref.shape[1:3]
+    pick_blocks(list_ref, rows, total // width, visit)
+
+
+def warp_of(warp_list, prev, near, far):
     return pl.pallas_call(
         warp_kernel,
-        in_specs=[IN_SMEM, IN_SMEM] + [IN_VMEM] * 3,
+        in_specs=[IN_SMEM] + [IN_VMEM] * 3,
         out_specs=IN_VMEM,
         out_shape=jax.ShapeDtypeStruct(prev.shape[1:], bf16),
         compiler_params=params(4),
         name="warp",
-    )(place, warp_list, prev, near, far)
+    )(warp_list, prev, near, far)
 
 
 def horizontal_kernel(
-    rows, place_ref, hidden_ref, low_ref, high_ref, seam_ref, gates_ref, cand_ref, out_ref, *rest
+    rows, hidden_ref, low_ref, high_ref, seam_ref, gates_ref, cand_ref, out_ref, *rest
 ):
     *edges, joined, reset, partial = rest
     _, width, ch = hidden_ref.shape
     taps = gates_ref.shape[0]
     half = taps // 2
-    right = place_ref[0]
+    right = right_half()
     pad = SEAM
     own = pl.multiple_of(pad + pad * right, pad)
     seam = pl.multiple_of(pad + width * (1 - right), pad)
@@ -335,11 +350,11 @@
         out_ref[r] = reset[r, pl.ds(own, width), :]
     if edges:
         near_ref, far_ref = edges
-        near_ref[...] = out_ref[pl.ds(half * place_ref[1], half)]
-        far_ref[...] = out_ref[pl.ds(half - half * place_ref[1], half)]
-
-
-def horizontal_pass(rows, send, place, hidden, low, high, seam, gates, cand):
+        near_ref[...] = out_ref[pl.ds(half * near_below(), half)]
+        far_ref[...] = out_ref[pl.ds(half - half * near_below(), half)]
+
+
+def horizontal_pass(rows, send, hidden, low, high, seam, gates, cand):
     _, width, ch = hidden.shape
     taps = gates.shape[0]
     length = width + SEAM + 2 * SEAM
@@ -347,7 +362,7 @@
     shapes = [shape(len(rows))] + [shape(taps // 2)] * (2 if send else 0)
     return pl.pallas_call(
         functools.partial(horizontal_kernel, rows),
-        in_specs=[IN_SMEM] + [IN_VMEM] * 6,
+        in_specs=[IN_VMEM] * 6,
         out_specs=[IN_VMEM] * len(shapes),
         out_shape=shapes,
         scratch_shapes=[
@@ -357,7 +372,7 @@
         ],
         compiler_params=params(24),
         name="horizontal",
-    )(place, hidden, low, high, seam, gates, cand)
+    )(hidden, low, high, seam, gates, cand)
 
 
 def pairs_kernel(cand_ref, out_ref):
@@ -432,13 +447,13 @@
 
 
 def outer_kernel(
-    place_ref, outer_ref, partial_ref, hidden_near, hidden_far, motion_near, motion_far, gates_ref,
+    outer_ref, partial_ref, hidden_near, hidden_far, motion_near, motion_far, gates_ref,
     update_ref, reset_ref, near_ref, far_ref, hidden_rim, motion_rim,
 ):
     taps, _, wide = gates_ref.shape
     ch = wide // 2
     half = taps // 2
-    near = half * place_ref[1]
+    near = half * near_below()
     far = half - near
     hidden_rim[pl.ds(near, half)] = hidden_near[...]
     hidden_rim[pl.ds(far, half)] = hidden_far[...]
@@ -459,19 +474,19 @@
     far_ref[...] = reset_ref[pl.ds(far, half)]
 
 
-def outer_gates(place, outer, partial, rims, gates):
+def outer_gates(outer, partial, rims, gates):
     count, width, ch = outer.shape
     half = gates.shape[0] // 2
     shape = lambda n, kind: jax.ShapeDtypeStruct((n, width, ch), kind)
     return pl.pallas_call(
         outer_kernel,
-        in_specs=[IN_SMEM] + [IN_VMEM] * 7,
+        in_specs=[IN_VMEM] * 7,
         out_specs=[IN_VMEM] * 4,
         out_shape=[shape(count, f32), shape(count, bf16), shape(half, bf16), shape(half, bf16)],
         scratch_shapes=[pltpu.VMEM((2 * half, width, ch), bf16)] * 2,
         compiler_params=params(16),
         name="outer_gates",
-    )(place, outer, partial, *rims, gates)
+    )(outer, partial, *rims, gates)
 
 
 def blend(state, update, total):
@@ -479,13 +494,13 @@
 
 
 def cand_kernel(
-    place_ref, reset_outer, reset_inner, low_ref, high_ref, motion_near, motion_far, inner_ref,
+    reset_outer, reset_inner, low_ref, high_ref, motion_near, motion_far, inner_ref,
     update_ref, pairs_ref, out_ref, partial_ref, motion_rim,
 ):
     blocks, depth, wide = pairs_ref.shape
     ch = wide // 2
     half = (blocks - 1) // 2
-    near = half * place_ref[1]
+    near = half * near_below()
     motion_rim[pl.ds(near, half)] = motion_near[...]
     motion_rim[pl.ds(half - near, half)] = motion_far[...]
     reset = banded(reset_outer, reset_inner, half)
@@ -513,12 +528,12 @@
             out_ref[i] = blend(inner_ref[i], update_ref[i], total)
 
 
-def inner_states(place, resets, low, high, motion_rims, inner, update, pairs):
+def inner_states(resets, low, high, motion_rims, inner, update, pairs):
     count, width, ch = inner.shape
     half = (pairs.shape[0] - 1) // 2
     return pl.pallas_call(
         cand_kernel,
-        in_specs=[IN_SMEM] + [IN_VMEM] * 9,
+        in_specs=[IN_VMEM] * 9,
         out_specs=[IN_VMEM] * 2,
         out_shape=[
             jax.ShapeDtypeStruct((count, width, ch), bf16),
@@ -527,11 +542,11 @@
         scratch_shapes=[pltpu.VMEM((2 * half, width, ch), bf16)],
         compiler_params=params(16),
         name="inner_states",
-    )(place, *resets, low, high, *motion_rims, inner, update, pairs)
+    )(*resets, low, high, *motion_rims, inner, update, pairs)
 
 
 def final_kernel(
-    place_ref, inner_ref, reset_near, reset_far, outer_ref, update_ref, partial_ref, pairs_ref,
+    inner_ref, reset_near, reset_far, outer_ref, update_ref, partial_ref, pairs_ref,
     out_ref, reset_rim, done, sems,
 ):
     blocks, _, wide = pairs_ref.shape
@@ -541,7 +556,7 @@
     count = inner_ref.shape[0]
     stores = [pltpu.make_async_copy(inner_ref, out_ref.at[0, pl.ds(half, count)], sems.at[0])]
     stores[0].start()
-    near = half * place_ref[1]
+    near = half * near_below()
     reset_rim[pl.ds(near, half)] = reset_near[...]
     reset_rim[pl.ds(half - near, half)] = reset_far[...]
     rim = state_rows(reset_rim)
@@ -562,18 +577,18 @@
         store.wait()
 
 
-def final_states(place, inner, reset_rims, outer, update, partial, pairs):
+def final_states(inner, reset_rims, outer, update, partial, pairs):
     count, width, ch = outer.shape
     rows = count + inner.shape[0]
     return pl.pallas_call(
         final_kernel,
-        in_specs=[IN_SMEM] + [IN_VMEM] * 7,
+        in_specs=[IN_VMEM] * 7,
         out_specs=IN_HBM,
         out_shape=jax.ShapeDtypeStruct((1, rows, width, ch), bf16),
         scratch_shapes=[pltpu.VMEM((count, width, ch), bf16)] * 2 + [pltpu.SemaphoreType.DMA((3,))],
         compiler_params=params(16),
         name="final_states",
-    )(place, inner, *reset_rims, outer, update, partial, pairs)
+    )(inner, *reset_rims, outer, update, partial, pairs)
 
 
 def shards(
@@ -583,47 +598,45 @@
     half = vgate_w.shape[0] // 2
     outer_rows = (*range(half), *range(rows - half, rows))
     inner_rows = tuple(range(half, rows - half))
-    right = lax.axis_index("cols")
-    below = 1 - lax.axis_index("rows") % 2
-    place = jnp.stack([right, below]).astype(jnp.int32)
     swap_cols = lambda value: lax.ppermute(value, "cols", [(0, 1), (1, 0)])
     swap_rows = lambda near, far: (swap_near(near, "rows"), swap_far(far, "rows"))
     pinned = lax.optimization_barrier
 
     warp_list = jnp.transpose(warp_list, (0, 2, 3, 1))
-    edge = lax.ppermute(right_feats, "cols", [(0, 1)])
+    flat_list = warp_list.reshape(-1)
     lists = swap_rows(warp_list, warp_list)
+    edge = swap_cols(right_feats)
     low = motion_of(0, rows // 2, left_feats, right_feats, edge, enc_weight)
-    pairs = pairs_of(vcand_w)
-    lists, low, pairs = pinned((lists, low, pairs))
-    blocks = gather_blocks(place, *lists, prev_hidden)
+    lists, low = pinned((lists, low))
+    blocks = gather_blocks(*lists, prev_hidden)
     edge, blocks = pinned((edge, blocks))
     near, far = swap_rows(*blocks)
     high = motion_of(rows // 2, rows // 2, left_feats, right_feats, edge, enc_weight)
-    high, edges = pinned((high, edges_of(place, low, high, half)))
+    pairs = pairs_of(vcand_w)
+    high, edges, pairs = pinned((high, edges_of(low, high, half), pairs))
     motion_rims = swap_rows(*edges)
-    seam = seam_of(place, warp_list, prev_hidden, near, far, low, high)
+    seam = seam_of(flat_list, prev_hidden, near, far, low, high)
     near, seam = pinned((near, seam))
-    warped = warp_of(place, warp_list, prev_hidden, near, far)
+    warped = warp_of(flat_list, prev_hidden, near, far)
     seam = swap_cols(seam)
     outer, *edges = horizontal_pass(
-        outer_rows, True, place, warped, low, high, seam, hgate_w, hcand_w
+        outer_rows, True, warped, low, high, seam, hgate_w, hcand_w
     )
     warped, edges = pinned((warped, edges))
     hidden_rims = swap_rows(*edges)
     (inner,) = horizontal_pass(
-        inner_rows, False, place, warped, low, high, seam, hgate_w, hcand_w
+        inner_rows, False, warped, low, high, seam, hgate_w, hcand_w
     )
     update_inner, reset_inner, partial = inner_gates(outer, inner, low, high, vgate_w)
     update_outer, reset_outer, *edges = outer_gates(
-        place, outer, partial, hidden_rims + motion_rims, vgate_w
+        outer, partial, hidden_rims + motion_rims, vgate_w
     )
     reset_inner, edges = pinned((reset_inner, edges))
     reset_rims = swap_rows(*edges)
     inner, partial = inner_states(
-        place, (reset_outer, reset_inner), low, high, motion_rims, inner, update_inner, pairs
-    )
-    return final_states(place, inner, reset_rims, outer, update_outer, partial, pairs)
+        (reset_outer, reset_inner), low, high, motion_rims, inner, update_inner, pairs
+    )
+    return final_states(inner, reset_rims, outer, update_outer, partial, pairs)
 
 
 def solution(mesh):

time: 55.4 us -> 50 us (0.903)
  Pallas kernels: 25.5 us -> 21 us
  waiting for transfers between devices: 7.15 us -> 10.9 us
  starting transfers between devices: 19.8 us -> 17 us
  local copies, waits for them, and re-layouts: 1.8 us -> 0.12 us
    pallas_call x9, Pallas kernels: 17.7 us -> 13.1 us  [the longest x2 5.9 us: horizontal_pass(): pl.pallas_call(functools.partial(horizontal_kernel, rows), in_specs=[IN_V...]
    ppermute x5, waiting for transfers between devices: 1.72 us -> 4.39 us  [swap_near(): return lax.ppermute(value, axis, pairs)]
    ppermute x1 -> x0, starting transfers between devices: 1.8 us -> none  [shards(): edge = lax.ppermute(right_feats, 'cols', [(0, 1)])]
    unnamed x16 -> x12, local copies, waits for them, and re-layouts: 1.8 us -> 0.03 us
    ppermute x5, starting transfers between devices: 2.84 us -> 1.65 us  [swap_near(): return lax.ppermute(value, axis, pairs)]
    ppermute x5, waiting for transfers between devices: 5.42 us -> 6.55 us  [swap_far(): return lax.ppermute(value, axis, pairs)]
  transfers between devices with their start and end apart: 12 -> 12, of which waited for: 4 -> 6; matrix products, arithmetic and copies ran while one was open for 0% -> 0% of each run, Pallas kernels for 34% -> 34%
where the time goes in v1:
time: 50 us; the launch traced here: 49.6 us
  Pallas kernels  21 us (42%)
  starting transfers between devices  17 us (34%)
  waiting for transfers between devices  10.9 us (22%)
    ppermute x5, starting transfers between devices, swap_far(): return lax.ppermute(value, axis, pairs)  15.3 us
    ppermute x5, waiting for transfers between devices, swap_far(): return lax.ppermute(value, axis, pairs)  6.55 us
    pallas_call x2, Pallas kernels, horizontal_pass(): pl.pallas_call(functools.partial(horizontal_kernel, rows), in_specs=[IN_V...  5.9 us
    pallas_call x2, Pallas kernels, motion_of(): pl.pallas_call(functools.partial(motion_kernel, first), in_specs=[IN_HBM,...  5.38 us
    ppermute x5, waiting for transfers between devices, swap_near(): return lax.ppermute(value, axis, pairs)  4.39 us
    pallas_call x1, Pallas kernels, inner_gates(): pl.pallas_call(gates_kernel, in_specs=[IN_VMEM] * 5, out_specs=[IN_VMEM]...  2.48 us
    pallas_call x1, Pallas kernels, inner_states(): pl.pallas_call(cand_kernel, in_specs=[IN_VMEM] * 9, out_specs=[IN_VMEM] *...  1.71 us
    ppermute x5, starting transfers between devices, swap_near(): return lax.ppermute(value, axis, pairs)  1.65 us
  transfers between devices with their start and end apart: 12, of which 6 were waited for; matrix products, arithmetic and copies ran while one was open for 0% of the time, Pallas kernels for 34%

profile of v1, /device:TPU:8, one launch (start us, length us, event | category | flops | bytes accessed | tf_op | source)
XLA Modules:
  0.0 49.6 jit_solution(3741788669350654502)
XLA Ops:
  0.0 0.0 collective-permute-start
  0.0 0.0 copy-start.5
  0.0 3.6 %collective-permute-start.2 = (s32[1,4,4,8]{3,2,1,0:T(4,128)}, s32[1,4,4,8]{3,2,1,0:T(4,128)S(1)}, u32[]{:S(2)}, u32[]{:S(2)}) collective-permute-start(s32[1,4,4,8]{3,2,1,0:T(4,128)} %bitcast.1), channel_id=1, source_target_pairs={{4,8},{8,4},{5,9},{9,5},{6,10},{10,6},{7,11},{11,7},{20,24},{24,20... | collective-permute-start | bytes 1544 | tf_op jit(solution)/shard_map/ppermute | solution.py:38
  3.6 0.1 collective-permute-start.1
  3.7 0.0 collective-permute-done.edge_ref
  3.7 2.6 %motion.2.low_ref = bf16[4,512,128]{2,1,0:T(8,128)(2,1)S(1)} custom-call(bf16[1,8,512,128]{3,2,1,0:T(8,128)(2,1)} %left_feats.3, bf16[1,8,512,128]{3,2,1,0:T(8,128)(2,1)} %right_feats.3, bf16[1,8,512,128]{3,2,1,0:T(8,128)(2,1)S(1)} %collective-permute-done.edge_ref, bf16[192,128]{1,0:T(8,128)(2,1)} %weight.3), custom_call_target="tpu_custom_call" | custom-call | tf_op jit(solution)/shard_map/motion/pallas_call | solution.py:128
  6.4 0.0 collective-permute-done.2.far_list
  6.4 1.2 %collective-permute-done.1.near_list = s32[1,4,4,8]{3,2,1,0:T(4,128)S(1)} collective-permute-done((s32[1,4,4,8]{3,2,1,0:T(4,128)}, s32[1,4,4,8]{3,2,1,0:T(4,128)S(1)}, u32[]{:S(2)}, u32[]{:S(2)}) %collective-permute-start.1) | collective-permute-done | bytes 544 | tf_op jit(solution)/shard_map/ppermute | solution.py:30
  7.6 1.6 %gather.1 = (bf16[8,128,128]{2,1,0:T(8,128)(2,1)S(1)}, bf16[8,128,128]{2,1,0:T(8,128)(2,1)S(1)}) custom-call(s32[1,4,4,8]{3,2,1,0:T(4,128)S(1)} %collective-permute-done.1.near_list, s32[1,4,4,8]{3,2,1,0:T(4,128)S(1)} %collective-permute-done.2.far_list, bf16[1,8,512,128]{3,2,1,0:T(8,128)(2,1)} %prev_ref.5), custom_call_target="tpu_custom_call" | custom-call | tf_op jit(solution)/shard_map/gather/pallas_call | solution.py:202
  9.1 1.1 %collective-permute-start.3 = (bf16[8,128,128]{2,1,0:T(8,128)(2,1)S(1)}, bf16[8,128,128]{2,1,0:T(8,128)(2,1)S(1)}, u32[]{:S(2)}, u32[]{:S(2)}) collective-permute-start(bf16[8,128,128]{2,1,0:T(8,128)(2,1)S(1)} %get-tuple-element.43), channel_id=1, source_target_pairs={{0,4},{4,0},{8,12},{12,8},{1,5},{5,1},{9,13},{13,9},{2,6},{6,2},{1... | collective-permute-start | bytes 786440 | tf_op jit(solution)/shard_map/ppermute | solution.py:30
  10.2 2.3 %collective-permute-start.4 = (bf16[8,128,128]{2,1,0:T(8,128)(2,1)S(1)}, bf16[8,128,128]{2,1,0:T(8,128)(2,1)S(1)}, u32[]{:S(2)}, u32[]{:S(2)}) collective-permute-start(bf16[8,128,128]{2,1,0:T(8,128)(2,1)S(1)} %get-tuple-element.44), channel_id=1, source_target_pairs={{4,8},{8,4},{5,9},{9,5},{6,10},{10,6},{7,11},{11,7},{20,24},{24,20... | collective-permute-start | bytes 786440 | tf_op jit(solution)/shard_map/ppermute | solution.py:38
  12.6 0.0 copy-done.5
  12.6 0.1 reshape.3.list_ref
  12.7 0.0 copy-done.4
  12.7 0.1 pairs.1.pairs_ref
  12.8 0.0 copy-start
  12.8 2.7 %motion.3.high_ref = bf16[4,512,128]{2,1,0:T(8,128)(2,1)S(1)} custom-call(bf16[1,8,512,128]{3,2,1,0:T(8,128)(2,1)} %left_feats.3, bf16[1,8,512,128]{3,2,1,0:T(8,128)(2,1)} %right_feats.3, bf16[1,8,512,128]{3,2,1,0:T(8,128)(2,1)S(1)} %collective-permute-done.edge_ref, bf16[192,128]{1,0:T(8,128)(2,1)} %weight.3), custom_call_target="tpu_custom_call" | custom-call | tf_op jit(solution)/shard_map/motion/pallas_call | solution.py:128
  15.6 0.1 edges.1
  15.7 0.0 copy-start.1
  15.7 0.0 copy-start.3
  15.7 0.9 %collective-permute-done.3.near_ref = bf16[8,128,128]{2,1,0:T(8,128)(2,1)S(1)} collective-permute-done((bf16[8,128,128]{2,1,0:T(8,128)(2,1)S(1)}, bf16[8,128,128]{2,1,0:T(8,128)(2,1)S(1)}, u32[]{:S(2)}, u32[]{:S(2)}) %collective-permute-start.3) | collective-permute-done | bytes 262176 | tf_op jit(solution)/shard_map/ppermute | solution.py:30
  16.6 3.3 %collective-permute-done.4.far_ref = bf16[8,128,128]{2,1,0:T(8,128)(2,1)S(1)} collective-permute-done((bf16[8,128,128]{2,1,0:T(8,128)(2,1)S(1)}, bf16[8,128,128]{2,1,0:T(8,128)(2,1)S(1)}, u32[]{:S(2)}, u32[]{:S(2)}) %collective-permute-start.4) | collective-permute-done | bytes 262176 | tf_op jit(solution)/shard_map/ppermute | solution.py:38
  20.0 0.0 copy-done
  20.0 0.7 %seam.1 = bf16[8,16,256]{2,1,0:T(8,128)(2,1)S(1)} custom-call(s32[128]{0:T(128)S(1)} %reshape.3.list_ref, bf16[1,8,512,128]{3,2,1,0:T(8,128)(2,1)S(1)} %copy-done, bf16[8,128,128]{2,1,0:T(8,128)(2,1)S(1)} %collective-permute-done.3.near_ref, bf16[8,128,128]{2,1,0:T(8,128)(2,1)S(1)} %collective-permute-done.4.far_ref, ...), custom_call_target="tpu_custom_call" | custom-call | tf_op jit(solution)/shard_map/seam/pallas_call | solution.py:258
  20.7 0.1 collective-permute-start.5
  20.8 0.1 collective-permute-start.8
  20.9 2.4 %collective-permute-start.9 = (bf16[2,512,128]{2,1,0:T(8,128)(2,1)S(1)}, bf16[2,512,128]{2,1,0:T(8,128)(2,1)S(1)}, u32[]{:S(2)}, u32[]{:S(2)}) collective-permute-start(bf16[2,512,128]{2,1,0:T(8,128)(2,1)S(1)} %get-tuple-element.60), channel_id=1, source_target_pairs={{4,8},{8,4},{5,9},{9,5},{6,10},{10,6},{7,11},{11,7},{20,24},{24,20... | collective-permute-start | bytes 786440 | tf_op jit(solution)/shard_map/ppermute | solution.py:38
  23.3 1.0 %warp.1.hidden_ref = bf16[8,512,128]{2,1,0:T(8,128)(2,1)S(1)} custom-call(s32[128]{0:T(128)S(1)} %reshape.3.list_ref, bf16[1,8,512,128]{3,2,1,0:T(8,128)(2,1)S(1)} %copy-done, bf16[8,128,128]{2,1,0:T(8,128)(2,1)S(1)} %collective-permute-done.3.near_ref, bf16[8,128,128]{2,1,0:T(8,128)(2,1)S(1)} %collective-permute-done.4.far_ref), custom_call_target="tpu_custom_call" | custom-call | tf_op jit(solution)/shard_map/warp/pallas_call | solution.py:285
  24.3 0.0 collective-permute-done.5.seam_ref
  24.4 0.0 copy-done.1
  24.4 0.0 copy-done.3
  24.4 3.0 %horizontal.2 = (bf16[4,512,128]{2,1,0:T(8,128)(2,1)S(1)}, bf16[2,512,128]{2,1,0:T(8,128)(2,1)S(1)}, bf16[2,512,128]{2,1,0:T(8,128)(2,1)S(1)}) custom-call(bf16[8,512,128]{2,1,0:T(8,128)(2,1)S(1)} %warp.1.hidden_ref, bf16[4,512,128]{2,1,0:T(8,128)(2,1)S(1)} %motion.2.low_ref, bf16[4,512,128]{2,1,0:T(8,128)(2,1)S(1)} %motion.3.high_ref, ...), custom_call_target="tpu_custom_call" | custom-call | tf_op jit(solution)/shard_map/horizontal/pallas_call | solution.py:363
  27.4 0.3 collective-permute-start.6
  27.8 3.5 %collective-permute-start.7 = (bf16[2,512,128]{2,1,0:T(8,128)(2,1)S(1)}, bf16[2,512,128]{2,1,0:T(8,128)(2,1)S(1)}, u32[]{:S(2)}, u32[]{:S(2)}) collective-permute-start(bf16[2,512,128]{2,1,0:T(8,128)(2,1)S(1)} %get-tuple-element.58), channel_id=1, source_target_pairs={{4,8},{8,4},{5,9},{9,5},{6,10},{10,6},{7,11},{11,7},{20,24},{24,20... | collective-permute-start | bytes 786440 | tf_op jit(solution)/shard_map/ppermute | solution.py:38
  31.3 2.9 %horizontal.3.inner_ref = bf16[4,512,128]{2,1,0:T(8,128)(2,1)S(1)} custom-call(bf16[8,512,128]{2,1,0:T(8,128)(2,1)S(1)} %warp.1.hidden_ref, bf16[4,512,128]{2,1,0:T(8,128)(2,1)S(1)} %motion.2.low_ref, bf16[4,512,128]{2,1,0:T(8,128)(2,1)S(1)} %motion.3.high_ref, bf16[8,16,256]{2,1,0:T(8,128)(2,1)S(1)} %collective-permute-done.5.seam_ref, ...), custom_call_target="tpu_custom_call" | custom-call | tf_op jit(solution)/shard_map/horizontal/pallas_call | solution.py:363
  34.1 0.0 copy-done.2
  34.1 2.5 %inner_gates.1 = (f32[4,512,128]{2,1,0:T(8,128)S(1)}, bf16[4,512,128]{2,1,0:T(8,128)(2,1)S(1)}, f32[4,512,256]{2,1,0:T(8,128)S(1)}) custom-call(bf16[4,512,128]{2,1,0:T(8,128)(2,1)S(1)} %get-tuple-element.52.outer_ref, bf16[4,512,128]{2,1,0:T(8,128)(2,1)S(1)} %horizontal.3.inner_ref, bf16[4,512,128]{2,1,0:T(8,128)(2,1)S(1)} %motion.2.low_ref, ...), custom_call_target="tpu_custom_call" | custom-call | tf_op jit(solution)/shard_map/inner_gates/pallas_call | solution.py:435
  36.6 0.0 collective-permute-done.8.motion_near
  36.6 0.0 collective-permute-done.9.motion_far
  36.6 0.0 collective-permute-done.6.hidden_near
  36.7 1.3 %collective-permute-done.7.hidden_far = bf16[2,512,128]{2,1,0:T(8,128)(2,1)S(1)} collective-permute-done((bf16[2,512,128]{2,1,0:T(8,128)(2,1)S(1)}, bf16[2,512,128]{2,1,0:T(8,128)(2,1)S(1)}, u32[]{:S(2)}, u32[]{:S(2)}) %collective-permute-start.7) | collective-permute-done | bytes 262176 | tf_op jit(solution)/shard_map/ppermute | solution.py:38
  38.0 0.7 %outer_gates.1 = (f32[4,512,128]{2,1,0:T(8,128)S(1)}, bf16[4,512,128]{2,1,0:T(8,128)(2,1)S(1)}, bf16[2,512,128]{2,1,0:T(8,128)(2,1)S(1)}, bf16[2,512,128]{2,1,0:T(8,128)(2,1)S(1)}) custom-call(bf16[4,512,128]{2,1,0:T(8,128)(2,1)S(1)} %get-tuple-element.52.outer_ref, f32[4,512,256]{2,1,0:T(8,128)S(1)} %get-tuple-element.56.partial_ref, ...), custom_call_target="tpu_custom_call" | custom-call | tf_op jit(solution)/shard_map/outer_gates/pallas_call | solution.py:481
  38.7 0.1 collective-permute-start.10
  38.8 3.5 %collective-permute-start.11 = (bf16[2,512,128]{2,1,0:T(8,128)(2,1)S(1)}, bf16[2,512,128]{2,1,0:T(8,128)(2,1)S(1)}, u32[]{:S(2)}, u32[]{:S(2)}) collective-permute-start(bf16[2,512,128]{2,1,0:T(8,128)(2,1)S(1)} %get-tuple-element.70), channel_id=1, source_target_pairs={{4,8},{8,4},{5,9},{9,5},{6,10},{10,6},{7,11},{11,7},{20,24},{24,20... | collective-permute-start | bytes 786440 | tf_op jit(solution)/shard_map/ppermute | solution.py:38
  42.2 1.7 %inner_states.1 = (bf16[4,512,128]{2,1,0:T(8,128)(2,1)S(1)}, f32[4,512,128]{2,1,0:T(8,128)S(1)}) custom-call(bf16[4,512,128]{2,1,0:T(8,128)(2,1)S(1)} %get-tuple-element.61.reset_outer, bf16[4,512,128]{2,1,0:T(8,128)(2,1)S(1)} %get-tuple-element.65.reset_inner, bf16[4,512,128]{2,1,0:T(8,128)(2,1)S(1)} %motion.2.low_ref, ...), custom_call_target="tpu_custom_call" | custom-call | tf_op jit(solution)/shard_map/inner_states/pallas_call | solution.py:534
  43.9 2.3 %collective-permute-done.10.reset_near = bf16[2,512,128]{2,1,0:T(8,128)(2,1)S(1)} collective-permute-done((bf16[2,512,128]{2,1,0:T(8,128)(2,1)S(1)}, bf16[2,512,128]{2,1,0:T(8,128)(2,1)S(1)}, u32[]{:S(2)}, u32[]{:S(2)}) %collective-permute-start.10) | collective-permute-done | bytes 262176 | tf_op jit(solution)/shard_map/ppermute | solution.py:30
  46.2 1.9 %collective-permute-done.11.reset_far = bf16[2,512,128]{2,1,0:T(8,128)(2,1)S(1)} collective-permute-done((bf16[2,512,128]{2,1,0:T(8,128)(2,1)S(1)}, bf16[2,512,128]{2,1,0:T(8,128)(2,1)S(1)}, u32[]{:S(2)}, u32[]{:S(2)}) %collective-permute-start.11) | collective-permute-done | bytes 262176 | tf_op jit(solution)/shard_map/ppermute | solution.py:38
  48.1 1.3 %final_states.1 = bf16[1,8,512,128]{3,2,1,0:T(8,128)(2,1)} custom-call(bf16[4,512,128]{2,1,0:T(8,128)(2,1)S(1)} %get-tuple-element.68.inner_ref, bf16[2,512,128]{2,1,0:T(8,128)(2,1)S(1)} %collective-permute-done.10.reset_near, bf16[2,512,128]{2,1,0:T(8,128)(2,1)S(1)} %collective-permute-done.11.reset_far, ...), custom_call_target="tpu_custom_call" | custom-call | tf_op jit(solution)/shard_map/final_states/pallas_call | solution.py:583
  (2 shorter events, 0.0 us)
Async XLA Ops:
  0.0 3.7 %collective-permute-start = (bf16[1,8,512,128]{3,2,1,0:T(8,128)(2,1)}, bf16[1,8,512,128]{3,2,1,0:T(8,128)(2,1)S(1)}, u32[]{:S(2)}, u32[]{:S(2)}) collective-permute-start(bf16[1,8,512,128]{3,2,1,0:T(8,128)(2,1)} %right_feats.3), channel_id=1, source_target_pairs={{0,1},{1,0},{2,3},{3,2},{4,5},{5,4},{6,7},{7,6},{8,9},{9,8},{10,11... | collective-permute-start | bytes 3145736 | tf_op jit(solution)/shard_map/ppermute | solution.py:601
  0.0 12.6 %copy-start.5 = (s32[1,8,4,4]{1,3,2,0:T(4,128)S(1)}, s32[1,8,4,4]{1,3,2,0:T(4,128)}, u32[]{:S(2)}) copy-start(s32[1,8,4,4]{1,3,2,0:T(4,128)} %param.12) | copy-start | bytes 1540
  0.0 12.7 %copy-start.4 = (bf16[5,256,128]{2,1,0:T(8,128)(2,1)S(1)}, bf16[5,256,128]{2,1,0:T(8,128)(2,1)}, u32[]{:S(2)}) copy-start(bf16[5,256,128]{2,1,0:T(8,128)(2,1)} %cand_ref.3) | copy-start | bytes 983044
  0.0 6.4 %collective-permute-start.2 = (s32[1,4,4,8]{3,2,1,0:T(4,128)}, s32[1,4,4,8]{3,2,1,0:T(4,128)S(1)}, u32[]{:S(2)}, u32[]{:S(2)}) collective-permute-start(s32[1,4,4,8]{3,2,1,0:T(4,128)} %bitcast.1), channel_id=1, source_target_pairs={{4,8},{8,4},{5,9},{9,5},{6,10},{10,6},{7,11},{11,7},{20,24},{24,20... | collective-permute-start | bytes 1544 | tf_op jit(solution)/shard_map/ppermute | solution.py:38
  3.6 3.9 %collective-permute-start.1 = (s32[1,4,4,8]{3,2,1,0:T(4,128)}, s32[1,4,4,8]{3,2,1,0:T(4,128)S(1)}, u32[]{:S(2)}, u32[]{:S(2)}) collective-permute-start(s32[1,4,4,8]{3,2,1,0:T(4,128)} %bitcast.2), channel_id=1, source_target_pairs={{0,4},{4,0},{8,12},{12,8},{1,5},{5,1},{9,13},{13,9},{2,6},{6,2},{1... | collective-permute-start | bytes 1544 | tf_op jit(solution)/shard_map/ppermute | solution.py:30
  9.1 7.5 %collective-permute-start.3 = (bf16[8,128,128]{2,1,0:T(8,128)(2,1)S(1)}, bf16[8,128,128]{2,1,0:T(8,128)(2,1)S(1)}, u32[]{:S(2)}, u32[]{:S(2)}) collective-permute-start(bf16[8,128,128]{2,1,0:T(8,128)(2,1)S(1)} %get-tuple-element.43), channel_id=1, source_target_pairs={{0,4},{4,0},{8,12},{12,8},{1,5},{5,1},{9,13},{13,9},{2,6},{6,2},{1... | collective-permute-start | bytes 786440 | tf_op jit(solution)/shard_map/ppermute | solution.py:30
  10.2 9.8 %collective-permute-start.4 = (bf16[8,128,128]{2,1,0:T(8,128)(2,1)S(1)}, bf16[8,128,128]{2,1,0:T(8,128)(2,1)S(1)}, u32[]{:S(2)}, u32[]{:S(2)}) collective-permute-start(bf16[8,128,128]{2,1,0:T(8,128)(2,1)S(1)} %get-tuple-element.44), channel_id=1, source_target_pairs={{4,8},{8,4},{5,9},{9,5},{6,10},{10,6},{7,11},{11,7},{20,24},{24,20... | collective-permute-start | bytes 786440 | tf_op jit(solution)/shard_map/ppermute | solution.py:38
  12.8 7.2 %copy-start = (bf16[1,8,512,128]{3,2,1,0:T(8,128)(2,1)S(1)}, bf16[1,8,512,128]{3,2,1,0:T(8,128)(2,1)}, u32[]{:S(2)}) copy-start(bf16[1,8,512,128]{3,2,1,0:T(8,128)(2,1)} %prev_ref.5) | copy-start | bytes 3145732
  15.7 8.7 %copy-start.1 = (bf16[5,256,256]{2,1,0:T(8,128)(2,1)S(1)}, bf16[5,256,256]{2,1,0:T(8,128)(2,1)}, u32[]{:S(2)}) copy-start(bf16[5,256,256]{2,1,0:T(8,128)(2,1)} %gates_ref.5) | copy-start | bytes 1966084
  15.7 8.7 %copy-start.3 = (bf16[5,256,128]{2,1,0:T(8,128)(2,1)S(1)}, bf16[5,256,128]{2,1,0:T(8,128)(2,1)}, u32[]{:S(2)}) copy-start(bf16[5,256,128]{2,1,0:T(8,128)(2,1)} %cand_ref.5) | copy-start | bytes 983044
  20.7 3.6 %collective-permute-start.5 = (bf16[8,16,256]{2,1,0:T(8,128)(2,1)S(1)}, bf16[8,16,256]{2,1,0:T(8,128)(2,1)S(1)}, u32[]{:S(2)}, u32[]{:S(2)}) collective-permute-start(bf16[8,16,256]{2,1,0:T(8,128)(2,1)S(1)} %seam.1), channel_id=1, source_target_pairs={{0,1},{1,0},{2,3},{3,2},{4,5},{5,4},{6,7},{7,6},{8,9},{9,8},{10,11... | collective-permute-start | bytes 196616 | tf_op jit(solution)/shard_map/ppermute | solution.py:601
  20.8 15.8 %collective-permute-start.8 = (bf16[2,512,128]{2,1,0:T(8,128)(2,1)S(1)}, bf16[2,512,128]{2,1,0:T(8,128)(2,1)S(1)}, u32[]{:S(2)}, u32[]{:S(2)}) collective-permute-start(bf16[2,512,128]{2,1,0:T(8,128)(2,1)S(1)} %get-tuple-element.59), channel_id=1, source_target_pairs={{0,4},{4,0},{8,12},{12,8},{1,5},{5,1},{9,13},{13,9},{2,6},{6,2},{1... | collective-permute-start | bytes 786440 | tf_op jit(solution)/shard_map/ppermute | solution.py:30
  20.9 15.8 %collective-permute-start.9 = (bf16[2,512,128]{2,1,0:T(8,128)(2,1)S(1)}, bf16[2,512,128]{2,1,0:T(8,128)(2,1)S(1)}, u32[]{:S(2)}, u32[]{:S(2)}) collective-permute-start(bf16[2,512,128]{2,1,0:T(8,128)(2,1)S(1)} %get-tuple-element.60), channel_id=1, source_target_pairs={{4,8},{8,4},{5,9},{9,5},{6,10},{10,6},{7,11},{11,7},{20,24},{24,20... | collective-permute-start | bytes 786440 | tf_op jit(solution)/shard_map/ppermute | solution.py:38
  27.4 6.7 %copy-start.2 = (bf16[5,256,256]{2,1,0:T(8,128)(2,1)S(1)}, bf16[5,256,256]{2,1,0:T(8,128)(2,1)}, u32[]{:S(2)}) copy-start(bf16[5,256,256]{2,1,0:T(8,128)(2,1)} %gates_ref.7) | copy-start | bytes 1966084
  27.4 9.2 %collective-permute-start.6 = (bf16[2,512,128]{2,1,0:T(8,128)(2,1)S(1)}, bf16[2,512,128]{2,1,0:T(8,128)(2,1)S(1)}, u32[]{:S(2)}, u32[]{:S(2)}) collective-permute-start(bf16[2,512,128]{2,1,0:T(8,128)(2,1)S(1)} %get-tuple-element.57), channel_id=1, source_target_pairs={{0,4},{4,0},{8,12},{12,8},{1,5},{5,1},{9,13},{13,9},{2,6},{6,2},{1... | collective-permute-start | bytes 786440 | tf_op jit(solution)/shard_map/ppermute | solution.py:30
  27.8 10.2 %collective-permute-start.7 = (bf16[2,512,128]{2,1,0:T(8,128)(2,1)S(1)}, bf16[2,512,128]{2,1,0:T(8,128)(2,1)S(1)}, u32[]{:S(2)}, u32[]{:S(2)}) collective-permute-start(bf16[2,512,128]{2,1,0:T(8,128)(2,1)S(1)} %get-tuple-element.58), channel_id=1, source_target_pairs={{4,8},{8,4},{5,9},{9,5},{6,10},{10,6},{7,11},{11,7},{20,24},{24,20... | collective-permute-start | bytes 786440 | tf_op jit(solution)/shard_map/ppermute | solution.py:38
  38.7 7.5 %collective-permute-start.10 = (bf16[2,512,128]{2,1,0:T(8,128)(2,1)S(1)}, bf16[2,512,128]{2,1,0:T(8,128)(2,1)S(1)}, u32[]{:S(2)}, u32[]{:S(2)}) collective-permute-start(bf16[2,512,128]{2,1,0:T(8,128)(2,1)S(1)} %get-tuple-element.69), channel_id=1, source_target_pairs={{0,4},{4,0},{8,12},{12,8},{1,5},{5,1},{9,13},{13,9},{2,6},{6,2},{1... | collective-permute-start | bytes 786440 | tf_op jit(solution)/shard_map/ppermute | solution.py:30
  38.8 9.4 %collective-permute-start.11 = (bf16[2,512,128]{2,1,0:T(8,128)(2,1)S(1)}, bf16[2,512,128]{2,1,0:T(8,128)(2,1)S(1)}, u32[]{:S(2)}, u32[]{:S(2)}) collective-permute-start(bf16[2,512,128]{2,1,0:T(8,128)(2,1)S(1)} %get-tuple-element.70), channel_id=1, source_target_pairs={{4,8},{8,4},{5,9},{9,5},{6,10},{10,6},{7,11},{11,7},{20,24},{24,20... | collective-permute-start | bytes 786440 | tf_op jit(solution)/shard_map/ppermute | solution.py:38

commit v2 on v1

--- a/solution.py
+++ b/solution.py
@@ -24,6 +24,13 @@
     return [(piece, r) for piece in pieces for r in range(piece.shape[0])]
 
 
+def fill_rim(rim_ref, near_ref, far_ref):
+    count = near_ref.shape[0]
+    near = count * near_below()
+    rim_ref[pl.ds(near, count)] = near_ref[...]
+    rim_ref[pl.ds(count - near, count)] = far_ref[...]
+
+
 def swap_near(value, axis):
     count = lax.axis_size(axis)
     pairs = [(i, i ^ 1) for i in range(count) if i ^ 1 < count]
@@ -41,6 +48,10 @@
 IN_VMEM = pl.BlockSpec(memory_space=pltpu.VMEM)
 IN_SMEM = pl.BlockSpec(memory_space=pltpu.SMEM)
 IN_HBM = pl.BlockSpec(memory_space=pltpu.HBM)
+
+
+def ordered(kernel, inputs, earlier):
+    return lambda *refs: kernel(*refs[:inputs], *refs[inputs + len(earlier) :])
 
 
 def right_half():
@@ -123,11 +134,11 @@
         out_ref[r, pl.ds(x, tile), :] = dotf(flip, part).astype(bf16)
 
 
-def motion_of(first, rows, left, right, edge, weight):
+def motion_of(first, rows, left, right, edge, weight, *earlier):
     width, feats = left.shape[2:]
     return pl.pallas_call(
-        functools.partial(motion_kernel, first),
-        in_specs=[IN_HBM, IN_HBM, IN_VMEM, IN_HBM],
+        ordered(functools.partial(motion_kernel, first), 4, earlier),
+        in_specs=[IN_HBM, IN_HBM, IN_VMEM, IN_HBM] + [IN_VMEM] * len(earlier),
         out_specs=IN_VMEM,
         out_shape=jax.ShapeDtypeStruct((rows, width, weight.shape[1]), bf16),
         scratch_shapes=[
@@ -136,9 +147,9 @@
             pltpu.VMEM(weight.shape, bf16),
             pltpu.SemaphoreType.DMA((3,)),
         ],
-        compiler_params=params(16),
+        compiler_params=params(4),
         name="motion",
-    )(in_hbm(left), in_hbm(right), edge, in_hbm(weight))
+    )(in_hbm(left), in_hbm(right), edge, in_hbm(weight), *earlier)
 
 
 def edges_kernel(low_ref, high_ref, near_ref, far_ref):
@@ -153,12 +164,26 @@
     shape = jax.ShapeDtypeStruct((count,) + low.shape[1:], bf16)
     return pl.pallas_call(
         edges_kernel,
-        in_specs=[IN_VMEM, IN_VMEM],
+        in_specs=[IN_VMEM] * 2,
         out_specs=[IN_VMEM, IN_VMEM],
         out_shape=[shape, shape],
         compiler_params=params(4),
         name="edges",
     )(low, high)
+
+
+def held_until(values, *earlier):
+    anywhere = pl.BlockSpec(memory_space=pl.ANY)
+    count = len(values)
+    return pl.pallas_call(
+        lambda *refs: None,
+        in_specs=[anywhere] * count + [IN_VMEM] * len(earlier),
+        out_specs=[anywhere] * count,
+        out_shape=[jax.ShapeDtypeStruct(value.shape, value.dtype) for value in values],
+        input_output_aliases={i: i for i in range(count)},
+        compiler_params=params(4),
+        name="held",
+    )(*values, *earlier)
 
 
 def gather_kernel(near_list, far_list, prev_ref, near_out, far_out, sems):
@@ -194,20 +219,20 @@
         copy.wait()
 
 
-def gather_blocks(near_list, far_list, prev):
+def gather_blocks(near_list, far_list, prev, *earlier):
     _, band_blocks, _, band_rows = near_list.shape
     _, _, width, hidden = prev.shape
     slots = band_rows * band_blocks // 4
     shape = jax.ShapeDtypeStruct((slots, width // band_blocks, hidden), bf16)
     return pl.pallas_call(
-        gather_kernel,
-        in_specs=[IN_VMEM, IN_VMEM, IN_HBM],
+        ordered(gather_kernel, 3, earlier),
+        in_specs=[IN_VMEM, IN_VMEM, IN_HBM] + [IN_VMEM] * len(earlier),
         out_specs=[IN_VMEM, IN_VMEM],
         out_shape=[shape, shape],
         scratch_shapes=[pltpu.SemaphoreType.DMA((2, slots))],
         compiler_params=params(4),
         name="gather",
-    )(near_list, far_list, in_hbm(prev))
+    )(near_list, far_list, in_hbm(prev), *earlier)
 
 
 def pick_blocks(list_ref, rows, blocks, visit):
@@ -216,7 +241,7 @@
     nears, fars = jnp.int32(0), jnp.int32(0)
     for block in range(blocks):
         for row in range(rows):
-            field = lambda k: list_ref[(block * 4 + k) * rows + row]
+            field = lambda k: list_ref[0, block, k, row]
             offset = field(0)
             is_near, is_far = offset == -sign, offset == sign
             visit(
@@ -281,21 +306,21 @@
     pick_blocks(list_ref, rows, total // width, visit)
 
 
-def warp_of(warp_list, prev, near, far):
-    return pl.pallas_call(
-        warp_kernel,
-        in_specs=[IN_SMEM] + [IN_VMEM] * 3,
+def warp_of(warp_list, prev, near, far, *earlier):
+    return pl.pallas_call(
+        ordered(warp_kernel, 4, earlier),
+        in_specs=[IN_SMEM] + [IN_VMEM] * (3 + len(earlier)),
         out_specs=IN_VMEM,
         out_shape=jax.ShapeDtypeStruct(prev.shape[1:], bf16),
         compiler_params=params(4),
         name="warp",
-    )(warp_list, prev, near, far)
+    )(warp_list, prev, near, far, *earlier)
 
 
 def horizontal_kernel(
-    rows, hidden_ref, low_ref, high_ref, seam_ref, gates_ref, cand_ref, out_ref, *rest
+    rows, hidden_ref, low_ref, high_ref, seam_ref, gates_ref, cand_ref, out_ref, near_ref, far_ref,
+    joined, reset, partial,
 ):
-    *edges, joined, reset, partial = rest
     _, width, ch = hidden_ref.shape
     taps = gates_ref.shape[0]
     half = taps // 2
@@ -348,21 +373,19 @@
         reset[r, pl.ds(pad, span), :] = blended.astype(bf16)
     for r in count:
         out_ref[r] = reset[r, pl.ds(own, width), :]
-    if edges:
-        near_ref, far_ref = edges
-        near_ref[...] = out_ref[pl.ds(half * near_below(), half)]
-        far_ref[...] = out_ref[pl.ds(half - half * near_below(), half)]
-
-
-def horizontal_pass(rows, send, hidden, low, high, seam, gates, cand):
+    near_ref[...] = out_ref[pl.ds(half * near_below(), half)]
+    far_ref[...] = out_ref[pl.ds(half - half * near_below(), half)]
+
+
+def horizontal_pass(rows, hidden, low, high, seam, gates, cand, *earlier):
     _, width, ch = hidden.shape
     taps = gates.shape[0]
     length = width + SEAM + 2 * SEAM
     shape = lambda count: jax.ShapeDtypeStruct((count, width, ch), bf16)
-    shapes = [shape(len(rows))] + [shape(taps // 2)] * (2 if send else 0)
-    return pl.pallas_call(
-        functools.partial(horizontal_kernel, rows),
-        in_specs=[IN_VMEM] * 6,
+    shapes = [shape(len(rows))] + [shape(taps // 2)] * 2
+    return pl.pallas_call(
+        ordered(functools.partial(horizontal_kernel, rows), 6, earlier),
+        in_specs=[IN_VMEM] * (6 + len(earlier)),
         out_specs=[IN_VMEM] * len(shapes),
         out_shape=shapes,
         scratch_shapes=[
@@ -370,29 +393,33 @@
             pltpu.VMEM((len(rows), length, ch), bf16),
             pltpu.VMEM((len(rows), length, taps * ch), f32),
         ],
-        compiler_params=params(24),
+        compiler_params=params(11),
         name="horizontal",
-    )(hidden, low, high, seam, gates, cand)
-
-
-def pairs_kernel(cand_ref, out_ref):
+    )(hidden, low, high, seam, gates, cand, *earlier)
+
+
+def pairs_kernel(gates_ref, cand_ref, reset_out, cand_out):
     taps, depth, ch = cand_ref.shape
-    for j in range(taps + 1):
-        none = jnp.zeros((depth, ch), bf16)
-        out_ref[j, :, 0:ch] = cand_ref[j] if j < taps else none
-        out_ref[j, :, ch : 2 * ch] = cand_ref[j - 1] if j > 0 else none
-
-
-def pairs_of(cand):
+    none = jnp.zeros((depth, ch), bf16)
+    reset = lambda j: gates_ref[j, :, pl.ds(ch, ch)]
+    cand = lambda j: cand_ref[j]
+    for out_ref, tap in ((reset_out, reset), (cand_out, cand)):
+        for j in range(taps + 1):
+            out_ref[j, :, 0:ch] = tap(j) if j < taps else none
+            out_ref[j, :, ch : 2 * ch] = tap(j - 1) if j > 0 else none
+
+
+def pairs_of(gates, cand):
     taps, depth, ch = cand.shape
+    shape = jax.ShapeDtypeStruct((taps + 1, depth, 2 * ch), bf16)
     return pl.pallas_call(
         pairs_kernel,
-        in_specs=[IN_VMEM],
-        out_specs=IN_VMEM,
-        out_shape=jax.ShapeDtypeStruct((taps + 1, depth, 2 * ch), bf16),
+        in_specs=[IN_VMEM] * 2,
+        out_specs=[IN_VMEM] * 2,
+        out_shape=[shape, shape],
         compiler_params=params(4),
         name="pairs",
-    )(cand)
+    )(gates, cand)
 
 
 def banded(outer_ref, inner_ref, half):
@@ -441,52 +468,66 @@
             jax.ShapeDtypeStruct((count, width, ch), bf16),
             jax.ShapeDtypeStruct((2 * half, width, 2 * ch), f32),
         ],
-        compiler_params=params(24),
+        compiler_params=params(4),
         name="inner_gates",
     )(outer, inner, low, high, gates)
 
 
 def outer_kernel(
-    outer_ref, partial_ref, hidden_near, hidden_far, motion_near, motion_far, gates_ref,
-    update_ref, reset_ref, near_ref, far_ref, hidden_rim, motion_rim,
+    outer_ref, partial_ref, low_ref, high_ref, hidden_near, hidden_far, motion_near, motion_far,
+    gates_ref, pairs_ref, update_ref, reset_ref, rim_ref, motion_rim, hidden_rim,
 ):
     taps, _, wide = gates_ref.shape
     ch = wide // 2
     half = taps // 2
-    near = half * near_below()
-    far = half - near
-    hidden_rim[pl.ds(near, half)] = hidden_near[...]
-    hidden_rim[pl.ds(far, half)] = hidden_far[...]
-    motion_rim[pl.ds(near, half)] = motion_near[...]
-    motion_rim[pl.ds(far, half)] = motion_far[...]
-    sources = (state_rows(hidden_rim), state_rows(motion_rim))
+    fill_rim(motion_rim, motion_near, motion_far)
+    fill_rim(hidden_rim, hidden_near, hidden_far)
+    above, below = state_rows(hidden_rim)[:half], state_rows(hidden_rim)[half:]
+    own, flow = state_rows(outer_ref), state_rows(low_ref, high_ref)
+    rim = state_rows(motion_rim)
+    top = (above + own[:half], rim[half : 2 * half] + flow[:half])
+    bottom = (own[half:] + below, flow[-half:] + rim[2 * half : 3 * half])
     weights = lambda first, last: gates_ref[pl.ds(first, last - first)].reshape(-1, wide)
+    pairs = lambda first, last: pairs_ref[pl.ds(first, last - first)].reshape(-1, wide)
+    flow_pairs = lambda first: pairs_ref[pl.ds(first, half), ch:, :].reshape(-1, wide)
     sums = []
     for i in range(half):
-        sums.append(dotf(stack(sources, range(i, half)), weights(0, half - i)))
+        sums.append(dotf(stack(top, range(i, half)), weights(0, half - i)))
     for i in range(half):
-        sums.append(dotf(stack(sources, range(half, half + i + 1)), weights(taps - 1 - i, taps)))
+        rows = range(half, half + i + 1)
+        sums.append(dotf(stack(bottom, rows), weights(taps - 1 - i, taps)))
+    beyond = [
+        dotf(stack(top, range(2 * half)), pairs(half, taps + 1))
+        + dotf(stack((rim,), range(half)), flow_pairs(0)),
+        dotf(stack(bottom, range(2 * half)), pairs(0, 2 * half))
+        + dotf(stack((rim,), range(3 * half, 4 * half)), flow_pairs(2 * half)),
+    ]
     for i in range(2 * half):
         total = sums[i] + partial_ref[i]
         update_ref[i] = sigmoid(total[:, :ch])
         reset_ref[i] = (sigmoid(total[:, ch:]) * outer_ref[i].astype(f32)).astype(bf16)
-    near_ref[...] = reset_ref[pl.ds(near, half)]
-    far_ref[...] = reset_ref[pl.ds(far, half)]
-
-
-def outer_gates(outer, partial, rims, gates):
+    for i in range(2):
+        rim_ref[2 * i], rim_ref[2 * i + 1] = beyond[i][:, :ch], beyond[i][:, ch:]
+
+
+def outer_gates(outer, partial, low, high, hidden_rims, motion_rims, gates, pairs):
     count, width, ch = outer.shape
     half = gates.shape[0] // 2
-    shape = lambda n, kind: jax.ShapeDtypeStruct((n, width, ch), kind)
+    shape = lambda kind: jax.ShapeDtypeStruct((count, width, ch), kind)
     return pl.pallas_call(
         outer_kernel,
-        in_specs=[IN_VMEM] * 7,
+        in_specs=[IN_VMEM] * 10,
         out_specs=[IN_VMEM] * 4,
-        out_shape=[shape(count, f32), shape(count, bf16), shape(half, bf16), shape(half, bf16)],
-        scratch_shapes=[pltpu.VMEM((2 * half, width, ch), bf16)] * 2,
-        compiler_params=params(16),
+        out_shape=[
+            shape(f32),
+            shape(bf16),
+            shape(f32),
+            jax.ShapeDtypeStruct((4 * half, width, ch), bf16),
+        ],
+        scratch_shapes=[pltpu.VMEM((2 * half, width, ch), bf16)],
+        compiler_params=params(4),
         name="outer_gates",
-    )(outer, partial, *rims, gates)
+    )(outer, partial, low, high, *hidden_rims, *motion_rims, gates, pairs)
 
 
 def blend(state, update, total):
@@ -494,15 +535,12 @@
 
 
 def cand_kernel(
-    reset_outer, reset_inner, low_ref, high_ref, motion_near, motion_far, inner_ref,
-    update_ref, pairs_ref, out_ref, partial_ref, motion_rim,
+    reset_outer, reset_inner, low_ref, high_ref, motion_rim, inner_ref, update_ref, pairs_ref,
+    out_ref, partial_ref,
 ):
     blocks, depth, wide = pairs_ref.shape
     ch = wide // 2
     half = (blocks - 1) // 2
-    near = half * near_below()
-    motion_rim[pl.ds(near, half)] = motion_near[...]
-    motion_rim[pl.ds(half - near, half)] = motion_far[...]
     reset = banded(reset_outer, reset_inner, half)
     sources = (reset, state_rows(low_ref, high_ref))
     rows = len(reset)
@@ -519,7 +557,7 @@
         first, last = max(y - half, 0), min(y + half + 2, rows)
         total = dotf(stack(sources, range(first, last)), weights(first - y + half, last - y + half))
         at = (0, half) if i == 0 else (blocks - half, blocks)
-        total += dotf(stack((rim,), range(half * i, half * i + half)), flow_weights(*at))
+        total += dotf(stack((rim,), range(half * (i + 1), half * (i + 2))), flow_weights(*at))
         partial_ref[2 * i], partial_ref[2 * i + 1] = total[:, :ch], total[:, ch:]
     for y in range(half, rows - half, 2):
         for k in range(2):
@@ -528,43 +566,45 @@
             out_ref[i] = blend(inner_ref[i], update_ref[i], total)
 
 
-def inner_states(resets, low, high, motion_rims, inner, update, pairs):
+def inner_states(resets, low, high, motion_rim, inner, update, pairs):
     count, width, ch = inner.shape
     half = (pairs.shape[0] - 1) // 2
     return pl.pallas_call(
         cand_kernel,
-        in_specs=[IN_VMEM] * 9,
+        in_specs=[IN_VMEM] * 8,
         out_specs=[IN_VMEM] * 2,
         out_shape=[
             jax.ShapeDtypeStruct((count, width, ch), bf16),
             jax.ShapeDtypeStruct((2 * half, width, ch), f32),
         ],
-        scratch_shapes=[pltpu.VMEM((2 * half, width, ch), bf16)],
-        compiler_params=params(16),
+        compiler_params=params(4),
         name="inner_states",
-    )(*resets, low, high, *motion_rims, inner, update, pairs)
+    )(*resets, low, high, motion_rim, inner, update, pairs)
 
 
 def final_kernel(
-    inner_ref, reset_near, reset_far, outer_ref, update_ref, partial_ref, pairs_ref,
-    out_ref, reset_rim, done, sems,
+    inner_ref, edge_near, edge_far, last_near, last_far, outer_ref, update_ref, partial_ref,
+    beyond_ref, reset_pairs, cand_pairs, out_ref, edge_rim, last_rim, reset_rim, done, sems,
 ):
-    blocks, _, wide = pairs_ref.shape
+    blocks, _, wide = cand_pairs.shape
     ch = wide // 2
     half = (blocks - 1) // 2
     rows = out_ref.shape[1]
     count = inner_ref.shape[0]
     stores = [pltpu.make_async_copy(inner_ref, out_ref.at[0, pl.ds(half, count)], sems.at[0])]
     stores[0].start()
-    near = half * near_below()
-    reset_rim[pl.ds(near, half)] = reset_near[...]
-    reset_rim[pl.ds(half - near, half)] = reset_far[...]
-    rim = state_rows(reset_rim)
-    sums = []
+    fill_rim(edge_rim, edge_near, edge_far)
+    fill_rim(last_rim, last_near, last_far)
+    last, rim = state_rows(last_rim), state_rows(reset_rim)
+    side = lambda i: range(half * i, half * i + half)
+    weights = lambda ref, i: ref[pl.ds((blocks - half) * i, half), :ch, :].reshape(-1, wide)
+    beyond = [dotf(stack((last,), side(i)), weights(reset_pairs, i)) for i in range(2)]
     for i in range(2):
-        first = 0 if i == 0 else blocks - half
-        weights = pairs_ref[pl.ds(first, half), :ch, :].reshape(-1, wide)
-        sums.append(dotf(stack((rim,), range(half * i, half * i + half)), weights))
+        for k in range(2):
+            at = 2 * i + k
+            total = beyond_ref[at] + beyond[i][:, k * ch : (k + 1) * ch]
+            reset_rim[at] = (sigmoid(total) * edge_rim[at].astype(f32)).astype(bf16)
+    sums = [dotf(stack((rim,), side(i)), weights(cand_pairs, i)) for i in range(2)]
     for i in range(2):
         for k in range(2):
             at = 2 * i + k
@@ -577,18 +617,18 @@
         store.wait()
 
 
-def final_states(inner, reset_rims, outer, update, partial, pairs):
+def final_states(inner, edge_rims, last_rims, outer, update, partial, beyond, reset_pairs, cand_pairs):
     count, width, ch = outer.shape
     rows = count + inner.shape[0]
     return pl.pallas_call(
         final_kernel,
-        in_specs=[IN_VMEM] * 7,
+        in_specs=[IN_VMEM] * 11,
         out_specs=IN_HBM,
         out_shape=jax.ShapeDtypeStruct((1, rows, width, ch), bf16),
-        scratch_shapes=[pltpu.VMEM((count, width, ch), bf16)] * 2 + [pltpu.SemaphoreType.DMA((3,))],
-        compiler_params=params(16),
+        scratch_shapes=[pltpu.VMEM((count, width, ch), bf16)] * 4 + [pltpu.SemaphoreType.DMA((3,))],
+        compiler_params=params(4),
         name="final_states",
-    )(inner, *reset_rims, outer, update, partial, pairs)
+    )(inner, *edge_rims, *last_rims, outer, update, partial, beyond, reset_pairs, cand_pairs)
 
 
 def shards(
@@ -603,40 +643,37 @@
     pinned = lax.optimization_barrier
 
     warp_list = jnp.transpose(warp_list, (0, 2, 3, 1))
-    flat_list = warp_list.reshape(-1)
     lists = swap_rows(warp_list, warp_list)
     edge = swap_cols(right_feats)
     low = motion_of(0, rows // 2, left_feats, right_feats, edge, enc_weight)
-    lists, low = pinned((lists, low))
-    blocks = gather_blocks(*lists, prev_hidden)
-    edge, blocks = pinned((edge, blocks))
+    blocks = gather_blocks(*lists, prev_hidden, low)
     near, far = swap_rows(*blocks)
-    high = motion_of(rows // 2, rows // 2, left_feats, right_feats, edge, enc_weight)
-    pairs = pairs_of(vcand_w)
-    high, edges, pairs = pinned((high, edges_of(low, high, half), pairs))
+    high = motion_of(rows // 2, rows // 2, left_feats, right_feats, edge, enc_weight, *blocks)
+    reset_pairs, cand_pairs = pairs_of(vgate_w, vcand_w)
+    edges = held_until(edges_of(low, high, rows // 2), near, far, reset_pairs)
     motion_rims = swap_rows(*edges)
-    seam = seam_of(flat_list, prev_hidden, near, far, low, high)
-    near, seam = pinned((near, seam))
-    warped = warp_of(flat_list, prev_hidden, near, far)
+    seam = seam_of(warp_list, prev_hidden, near, far, low, high)
+    warped = warp_of(warp_list, prev_hidden, near, far, seam)
     seam = swap_cols(seam)
-    outer, *edges = horizontal_pass(
-        outer_rows, True, warped, low, high, seam, hgate_w, hcand_w
-    )
-    warped, edges = pinned((warped, edges))
-    hidden_rims = swap_rows(*edges)
-    (inner,) = horizontal_pass(
-        inner_rows, False, warped, low, high, seam, hgate_w, hcand_w
-    )
+    outer, *edges = horizontal_pass(outer_rows, warped, low, high, seam, hgate_w, hcand_w)
+    edge_rims = swap_rows(*edges)
+    inner, *edges = horizontal_pass(
+        inner_rows, warped, low, high, seam, hgate_w, hcand_w, *edges
+    )
+    inner, edges, motion_near = pinned((inner, edges, motion_rims[0]))
+    motion_rims = (motion_near, motion_rims[1])
+    last_rims = swap_rows(*edges)
     update_inner, reset_inner, partial = inner_gates(outer, inner, low, high, vgate_w)
-    update_outer, reset_outer, *edges = outer_gates(
-        outer, partial, hidden_rims + motion_rims, vgate_w
-    )
-    reset_inner, edges = pinned((reset_inner, edges))
-    reset_rims = swap_rows(*edges)
+    update_outer, reset_outer, beyond, motion_rim = outer_gates(
+        outer, partial, low, high, edge_rims, motion_rims, vgate_w, reset_pairs
+    )
+    resets = (reset_outer, reset_inner)
     inner, partial = inner_states(
-        (reset_outer, reset_inner), low, high, motion_rims, inner, update_inner, pairs
-    )
-    return final_states(inner, reset_rims, outer, update_outer, partial, pairs)
+        resets, low, high, motion_rim, inner, update_inner, cand_pairs
+    )
+    return final_states(
+        inner, edge_rims, last_rims, outer, update_outer, partial, beyond, reset_pairs, cand_pairs
+    )
 
 
 def solution(mesh):

time: 50 us -> 47.9 us (0.958)
  waiting for transfers between devices: 10.9 us -> 8.47 us
  Pallas kernels: 21 us -> 22.5 us
  starting transfers between devices: 17 us -> 16.2 us
    ppermute x5, waiting for transfers between devices: 4.39 us -> 2.09 us  [swap_near(): return lax.ppermute(value, axis, pairs)]
    pallas_call x11 -> x12, Pallas kernels: 17.8 us -> 19.1 us  [the longest x2 6.06 us: horizontal_pass(): pl.pallas_call(ordered(functools.partial(horizontal_kernel, rows), 6, ear...]
    ppermute x5, starting transfers between devices: 15.3 us -> 14.5 us  [swap_far(): return lax.ppermute(value, axis, pairs)]
  transfers between devices with their start and end apart: 12 -> 12, of which waited for: 6 -> 6; matrix products, arithmetic and copies ran while one was open for 0% -> 0% of each run, Pallas kernels for 34% -> 41%
where the time goes in v2:
time: 47.9 us; the launch traced here: 47.6 us
  Pallas kernels  22.5 us (47%)
  starting transfers between devices  16.2 us (34%)
  waiting for transfers between devices  8.47 us (18%)
    ppermute x5, starting transfers between devices, swap_far(): return lax.ppermute(value, axis, pairs)  14.5 us
    ppermute x5, waiting for transfers between devices, swap_far(): return lax.ppermute(value, axis, pairs)  6.3 us
    pallas_call x2, Pallas kernels, horizontal_pass(): pl.pallas_call(ordered(functools.partial(horizontal_kernel, rows), 6, ear...  6.06 us
    pallas_call x2, Pallas kernels, motion_of(): pl.pallas_call(ordered(functools.partial(motion_kernel, first), 4, earlie...  5.3 us
    pallas_call x1, Pallas kernels, inner_gates(): pl.pallas_call(gates_kernel, in_specs=[IN_VMEM] * 5, out_specs=[IN_VMEM]...  2.48 us
    ppermute x5, waiting for transfers between devices, swap_near(): return lax.ppermute(value, axis, pairs)  2.09 us
    pallas_call x1, Pallas kernels, inner_states(): pl.pallas_call(cand_kernel, in_specs=[IN_VMEM] * 8, out_specs=[IN_VMEM] *...  1.66 us
    ppermute x5, starting transfers between devices, swap_near(): return lax.ppermute(value, axis, pairs)  1.6 us
  transfers between devices with their start and end apart: 12, of which 6 were waited for; matrix products, arithmetic and copies ran while one was open for 0% of the time, Pallas kernels for 41%

profile of v2, /device:TPU:8, one launch (start us, length us, event | category | flops | bytes accessed | tf_op | source)
XLA Modules:
  0.0 47.6 jit_solution(13337187850532267410)
XLA Ops:
  0.0 0.0 collective-permute-start.2
  0.0 0.0 copy-start.1
  0.0 0.0 copy-start.4
  0.0 3.6 %collective-permute-start.1 = (s32[1,4,4,8]{3,2,1,0:T(4,128)}, s32[1,4,4,8]{3,2,1,0:T(4,128)S(1)}, u32[]{:S(2)}, u32[]{:S(2)}) collective-permute-start(s32[1,4,4,8]{3,2,1,0:T(4,128)} %bitcast.1), channel_id=1, source_target_pairs={{4,8},{8,4},{5,9},{9,5},{6,10},{10,6},{7,11},{11,7},{20,24},{24,20... | collective-permute-start | bytes 1544 | tf_op jit(solution)/shard_map/ppermute | solution.py:45
  3.6 0.1 collective-permute-start
  3.7 0.0 collective-permute-done.2.refs_2_
  3.7 2.6 %motion.2.refs_3_.low_ref.refs_1_ = bf16[4,512,128]{2,1,0:T(8,128)(2,1)S(1)} custom-call(bf16[1,8,512,128]{3,2,1,0:T(8,128)(2,1)} %refs_0_.3, bf16[1,8,512,128]{3,2,1,0:T(8,128)(2,1)} %refs_1_.4, bf16[1,8,512,128]{3,2,1,0:T(8,128)(2,1)S(1)} %collective-permute-done.2.refs_2_, bf16[192,128]{1,0:T(8,128)(2,1)} %refs_3_.3), custom_call_target="tpu_custom_call" | custom-call | tf_op jit(solution)/shard_map/motion/pallas_call | solution.py:139
  6.4 0.0 collective-permute-done.1.refs_1_
  6.4 1.2 %collective-permute-done.refs_0_ = s32[1,4,4,8]{3,2,1,0:T(4,128)S(1)} collective-permute-done((s32[1,4,4,8]{3,2,1,0:T(4,128)}, s32[1,4,4,8]{3,2,1,0:T(4,128)S(1)}, u32[]{:S(2)}, u32[]{:S(2)}) %collective-permute-start) | collective-permute-done | bytes 544 | tf_op jit(solution)/shard_map/ppermute | solution.py:37
  7.6 1.6 %gather.1 = (bf16[8,128,128]{2,1,0:T(8,128)(2,1)S(1)}, bf16[8,128,128]{2,1,0:T(8,128)(2,1)S(1)}) custom-call(s32[1,4,4,8]{3,2,1,0:T(4,128)S(1)} %collective-permute-done.refs_0_, s32[1,4,4,8]{3,2,1,0:T(4,128)S(1)} %collective-permute-done.1.refs_1_, bf16[1,8,512,128]{3,2,1,0:T(8,128)(2,1)} %refs_1_.5, bf16[4,512,128]{2,1,0:T(8,128)(2,1)S(1)} %motion.2.refs_3_.low_ref.refs_1_), custom_call_target="tpu_custom_call" | custom-call | tf_op jit(solution)/shard_map/gather/pallas_call | solution.py:227
  9.1 1.1 %collective-permute-start.3 = (bf16[8,128,128]{2,1,0:T(8,128)(2,1)S(1)}, bf16[8,128,128]{2,1,0:T(8,128)(2,1)S(1)}, u32[]{:S(2)}, u32[]{:S(2)}) collective-permute-start(bf16[8,128,128]{2,1,0:T(8,128)(2,1)S(1)} %get-tuple-element.32.refs_4_), channel_id=1, source_target_pairs={{0,4},{4,0},{8,12},{12,8},{1,5},{5,1},{9,13},{13,9},{2,6},{6,2},{1... | collective-permute-start | bytes 786440 | tf_op jit(solution)/shard_map/ppermute | solution.py:37
  10.2 2.3 %collective-permute-start.4 = (bf16[8,128,128]{2,1,0:T(8,128)(2,1)S(1)}, bf16[8,128,128]{2,1,0:T(8,128)(2,1)S(1)}, u32[]{:S(2)}, u32[]{:S(2)}) collective-permute-start(bf16[8,128,128]{2,1,0:T(8,128)(2,1)S(1)} %get-tuple-element.33.refs_5_), channel_id=1, source_target_pairs={{4,8},{8,4},{5,9},{9,5},{6,10},{10,6},{7,11},{11,7},{20,24},{24,20... | collective-permute-start | bytes 786440 | tf_op jit(solution)/shard_map/ppermute | solution.py:45
  12.6 0.0 copy-done.1
  12.6 0.0 copy-done.4
  12.6 0.2 pairs.1
  12.8 2.6 %motion.3.high_ref.refs_2_ = bf16[4,512,128]{2,1,0:T(8,128)(2,1)S(1)} custom-call(bf16[1,8,512,128]{3,2,1,0:T(8,128)(2,1)} %refs_0_.3, bf16[1,8,512,128]{3,2,1,0:T(8,128)(2,1)} %refs_1_.4, bf16[1,8,512,128]{3,2,1,0:T(8,128)(2,1)S(1)} %collective-permute-done.2.refs_2_, bf16[192,128]{1,0:T(8,128)(2,1)} %refs_3_.3, ...), custom_call_target="tpu_custom_call" | custom-call | tf_op jit(solution)/shard_map/motion/pallas_call | solution.py:139
  15.5 0.0 copy-start
  15.5 0.0 copy-start.5
  15.5 0.2 edges.1
  15.7 0.9 %collective-permute-done.3.near_ref.refs_2_ = bf16[8,128,128]{2,1,0:T(8,128)(2,1)S(1)} collective-permute-done((bf16[8,128,128]{2,1,0:T(8,128)(2,1)S(1)}, bf16[8,128,128]{2,1,0:T(8,128)(2,1)S(1)}, u32[]{:S(2)}, u32[]{:S(2)}) %collective-permute-start.3) | collective-permute-done | bytes 262176 | tf_op jit(solution)/shard_map/ppermute | solution.py:37
  16.6 3.3 %collective-permute-done.4.far_ref.refs_3_ = bf16[8,128,128]{2,1,0:T(8,128)(2,1)S(1)} collective-permute-done((bf16[8,128,128]{2,1,0:T(8,128)(2,1)S(1)}, bf16[8,128,128]{2,1,0:T(8,128)(2,1)S(1)}, u32[]{:S(2)}, u32[]{:S(2)}) %collective-permute-start.4) | collective-permute-done | bytes 262176 | tf_op jit(solution)/shard_map/ppermute | solution.py:45
  20.0 0.0 collective-permute-start.6
  20.0 0.0 copy-start.2
  20.0 2.5 %collective-permute-start.9 = (bf16[4,512,128]{2,1,0:T(8,128)(2,1)S(1)}, bf16[4,512,128]{2,1,0:T(8,128)(2,1)S(1)}, u32[]{:S(2)}, u32[]{:S(2)}) collective-permute-start(bf16[4,512,128]{2,1,0:T(8,128)(2,1)S(1)} %get-tuple-element.47), channel_id=1, source_target_pairs={{4,8},{8,4},{5,9},{9,5},{6,10},{10,6},{7,11},{11,7},{20,24},{24,20... | collective-permute-start | bytes 1572872 | tf_op jit(solution)/shard_map/ppermute | solution.py:45
  22.5 0.0 copy-done
  22.5 0.0 copy-done.5
  22.6 0.9 %seam.1.refs_4_ = bf16[8,16,256]{2,1,0:T(8,128)(2,1)S(1)} custom-call(s32[1,4,4,8]{3,2,1,0:T(4,128)S(1)} %bitcast.3, bf16[1,8,512,128]{3,2,1,0:T(8,128)(2,1)S(1)} %copy-done, bf16[8,128,128]{2,1,0:T(8,128)(2,1)S(1)} %collective-permute-done.3.near_ref.refs_2_, bf16[8,128,128]{2,1,0:T(8,128)(2,1)S(1)} %collective-permute-done.4.far_ref.refs_3_, ...), custom_call_target="tpu_custom_call" | custom-call | tf_op jit(solution)/shard_map/seam/pallas_call | solution.py:283
  23.4 0.1 collective-permute-start.5
  23.5 1.2 %warp.1.refs_0_ = bf16[8,512,128]{2,1,0:T(8,128)(2,1)S(1)} custom-call(s32[1,4,4,8]{3,2,1,0:T(4,128)S(1)} %bitcast.4, bf16[1,8,512,128]{3,2,1,0:T(8,128)(2,1)S(1)} %copy-done, bf16[8,128,128]{2,1,0:T(8,128)(2,1)S(1)} %collective-permute-done.3.near_ref.refs_2_, bf16[8,128,128]{2,1,0:T(8,128)(2,1)S(1)} %collective-permute-done.4.far_ref.refs_3_, ...), custom_call_target="tpu_custom_call" | custom-call | tf_op jit(solution)/shard_map/warp/pallas_call | solution.py:310
  24.7 0.1 collective-permute-done.5.refs_3_
  24.8 0.0 copy-done.2
  24.8 0.0 copy-done.3
  24.8 3.0 %horizontal.2 = (bf16[4,512,128]{2,1,0:T(8,128)(2,1)S(1)}, bf16[2,512,128]{2,1,0:T(8,128)(2,1)S(1)}, bf16[2,512,128]{2,1,0:T(8,128)(2,1)S(1)}) custom-call(bf16[8,512,128]{2,1,0:T(8,128)(2,1)S(1)} %warp.1.refs_0_, bf16[4,512,128]{2,1,0:T(8,128)(2,1)S(1)} %motion.2.refs_3_.low_ref.refs_1_, bf16[4,512,128]{2,1,0:T(8,128)(2,1)S(1)} %motion.3.high_ref.refs_2_, ...), custom_call_target="tpu_custom_call" | custom-call | tf_op jit(solution)/shard_map/horizontal/pallas_call | solution.py:386
  27.8 0.4 collective-permute-start.7
  28.2 3.2 %collective-permute-start.8 = (bf16[2,512,128]{2,1,0:T(8,128)(2,1)S(1)}, bf16[2,512,128]{2,1,0:T(8,128)(2,1)S(1)}, u32[]{:S(2)}, u32[]{:S(2)}) collective-permute-start(bf16[2,512,128]{2,1,0:T(8,128)(2,1)S(1)} %get-tuple-element.36.refs_7_), channel_id=1, source_target_pairs={{4,8},{8,4},{5,9},{9,5},{6,10},{10,6},{7,11},{11,7},{20,24},{24,20... | collective-permute-start | bytes 786440 | tf_op jit(solution)/shard_map/ppermute | solution.py:45
  31.3 3.0 %horizontal.3 = (bf16[4,512,128]{2,1,0:T(8,128)(2,1)S(1)}, bf16[2,512,128]{2,1,0:T(8,128)(2,1)S(1)}, bf16[2,512,128]{2,1,0:T(8,128)(2,1)S(1)}) custom-call(bf16[8,512,128]{2,1,0:T(8,128)(2,1)S(1)} %warp.1.refs_0_, bf16[4,512,128]{2,1,0:T(8,128)(2,1)S(1)} %motion.2.refs_3_.low_ref.refs_1_, bf16[4,512,128]{2,1,0:T(8,128)(2,1)S(1)} %motion.3.high_ref.refs_2_, ...), custom_call_target="tpu_custom_call" | custom-call | tf_op jit(solution)/shard_map/horizontal/pallas_call | solution.py:386
  34.3 0.0 collective-permute-done.6.motion_near
  34.4 0.1 collective-permute-start.10
  34.4 2.9 %collective-permute-start.11 = (bf16[2,512,128]{2,1,0:T(8,128)(2,1)S(1)}, bf16[2,512,128]{2,1,0:T(8,128)(2,1)S(1)}, u32[]{:S(2)}, u32[]{:S(2)}) collective-permute-start(bf16[2,512,128]{2,1,0:T(8,128)(2,1)S(1)} %get-tuple-element.55), channel_id=1, source_target_pairs={{4,8},{8,4},{5,9},{9,5},{6,10},{10,6},{7,11},{11,7},{20,24},{24,20... | collective-permute-start | bytes 786440 | tf_op jit(solution)/shard_map/ppermute | solution.py:45
  37.3 2.5 %inner_gates.1 = (f32[4,512,128]{2,1,0:T(8,128)S(1)}, bf16[4,512,128]{2,1,0:T(8,128)(2,1)S(1)}, f32[4,512,256]{2,1,0:T(8,128)S(1)}) custom-call(bf16[4,512,128]{2,1,0:T(8,128)(2,1)S(1)} %get-tuple-element.34.outer_ref, bf16[4,512,128]{2,1,0:T(8,128)(2,1)S(1)} %get-tuple-element.44.inner_ref, bf16[4,512,128]{2,1,0:T(8,128)(2,1)S(1)} %motion.2.refs_3_.low_ref.refs_1_, ...), custom_call_target="tpu_custom_call" | custom-call | tf_op jit(solution)/shard_map/inner_gates/pallas_call | solution.py:462
  39.8 0.0 collective-permute-done.7.hidden_near.edge_near
  39.8 1.3 %collective-permute-done.8.hidden_far.edge_far = bf16[2,512,128]{2,1,0:T(8,128)(2,1)S(1)} collective-permute-done((bf16[2,512,128]{2,1,0:T(8,128)(2,1)S(1)}, bf16[2,512,128]{2,1,0:T(8,128)(2,1)S(1)}, u32[]{:S(2)}, u32[]{:S(2)}) %collective-permute-start.8) | collective-permute-done | bytes 262176 | tf_op jit(solution)/shard_map/ppermute | solution.py:45
  41.1 0.0 collective-permute-done.9.motion_far
  41.1 1.4 %outer_gates.1 = (f32[4,512,128]{2,1,0:T(8,128)S(1)}, bf16[4,512,128]{2,1,0:T(8,128)(2,1)S(1)}, f32[4,512,128]{2,1,0:T(8,128)S(1)}, bf16[8,512,128]{2,1,0:T(8,128)(2,1)S(1)}) custom-call(bf16[4,512,128]{2,1,0:T(8,128)(2,1)S(1)} %get-tuple-element.34.outer_ref, f32[4,512,256]{2,1,0:T(8,128)S(1)} %get-tuple-element.45.partial_ref, ...), custom_call_target="tpu_custom_call" | custom-call | tf_op jit(solution)/shard_map/outer_gates/pallas_call | solution.py:517
  42.5 1.7 %inner_states.1 = (bf16[4,512,128]{2,1,0:T(8,128)(2,1)S(1)}, f32[4,512,128]{2,1,0:T(8,128)S(1)}) custom-call(bf16[4,512,128]{2,1,0:T(8,128)(2,1)S(1)} %get-tuple-element.48.reset_outer, bf16[4,512,128]{2,1,0:T(8,128)(2,1)S(1)} %get-tuple-element.49.reset_inner, bf16[4,512,128]{2,1,0:T(8,128)(2,1)S(1)} %motion.2.refs_3_.low_ref.refs_1_, ...), custom_call_target="tpu_custom_call" | custom-call | tf_op jit(solution)/shard_map/inner_states/pallas_call | solution.py:572
  44.2 0.0 collective-permute-done.10.last_near
  44.2 1.6 %collective-permute-done.11.last_far = bf16[2,512,128]{2,1,0:T(8,128)(2,1)S(1)} collective-permute-done((bf16[2,512,128]{2,1,0:T(8,128)(2,1)S(1)}, bf16[2,512,128]{2,1,0:T(8,128)(2,1)S(1)}, u32[]{:S(2)}, u32[]{:S(2)}) %collective-permute-start.11) | collective-permute-done | bytes 262176 | tf_op jit(solution)/shard_map/ppermute | solution.py:45
  45.8 1.6 %final_states.1 = bf16[1,8,512,128]{3,2,1,0:T(8,128)(2,1)} custom-call(bf16[4,512,128]{2,1,0:T(8,128)(2,1)S(1)} %get-tuple-element.53.inner_ref, bf16[2,512,128]{2,1,0:T(8,128)(2,1)S(1)} %collective-permute-done.7.hidden_near.edge_near, bf16[2,512,128]{2,1,0:T(8,128)(2,1)S(1)} %collective-permute-done.8.hidden_far.edge_far, ...), custom_call_target="tpu_custom_call" | custom-call | tf_op jit(solution)/shard_map/final_states/pallas_call | solution.py:623
  (2 shorter events, 0.0 us)
Async XLA Ops:
  0.0 3.7 %collective-permute-start.2 = (bf16[1,8,512,128]{3,2,1,0:T(8,128)(2,1)}, bf16[1,8,512,128]{3,2,1,0:T(8,128)(2,1)S(1)}, u32[]{:S(2)}, u32[]{:S(2)}) collective-permute-start(bf16[1,8,512,128]{3,2,1,0:T(8,128)(2,1)} %refs_1_.4), channel_id=1, source_target_pairs={{0,1},{1,0},{2,3},{3,2},{4,5},{5,4},{6,7},{7,6},{8,9},{9,8},{10,11... | collective-permute-start | bytes 3145736 | tf_op jit(solution)/shard_map/ppermute | solution.py:641
  0.0 12.6 %copy-start.1 = (bf16[5,256,256]{2,1,0:T(8,128)(2,1)S(1)}, bf16[5,256,256]{2,1,0:T(8,128)(2,1)}, u32[]{:S(2)}) copy-start(bf16[5,256,256]{2,1,0:T(8,128)(2,1)} %gates_ref.5) | copy-start | bytes 1966084
  0.0 12.6 %copy-start.4 = (bf16[5,256,128]{2,1,0:T(8,128)(2,1)S(1)}, bf16[5,256,128]{2,1,0:T(8,128)(2,1)}, u32[]{:S(2)}) copy-start(bf16[5,256,128]{2,1,0:T(8,128)(2,1)} %cand_ref.1) | copy-start | bytes 983044
  0.0 6.4 %collective-permute-start.1 = (s32[1,4,4,8]{3,2,1,0:T(4,128)}, s32[1,4,4,8]{3,2,1,0:T(4,128)S(1)}, u32[]{:S(2)}, u32[]{:S(2)}) collective-permute-start(s32[1,4,4,8]{3,2,1,0:T(4,128)} %bitcast.1), channel_id=1, source_target_pairs={{4,8},{8,4},{5,9},{9,5},{6,10},{10,6},{7,11},{11,7},{20,24},{24,20... | collective-permute-start | bytes 1544 | tf_op jit(solution)/shard_map/ppermute | solution.py:45
  3.6 3.9 %collective-permute-start = (s32[1,4,4,8]{3,2,1,0:T(4,128)}, s32[1,4,4,8]{3,2,1,0:T(4,128)S(1)}, u32[]{:S(2)}, u32[]{:S(2)}) collective-permute-start(s32[1,4,4,8]{3,2,1,0:T(4,128)} %bitcast.2), channel_id=1, source_target_pairs={{0,4},{4,0},{8,12},{12,8},{1,5},{5,1},{9,13},{13,9},{2,6},{6,2},{1... | collective-permute-start | bytes 1544 | tf_op jit(solution)/shard_map/ppermute | solution.py:37
  9.1 7.5 %collective-permute-start.3 = (bf16[8,128,128]{2,1,0:T(8,128)(2,1)S(1)}, bf16[8,128,128]{2,1,0:T(8,128)(2,1)S(1)}, u32[]{:S(2)}, u32[]{:S(2)}) collective-permute-start(bf16[8,128,128]{2,1,0:T(8,128)(2,1)S(1)} %get-tuple-element.32.refs_4_), channel_id=1, source_target_pairs={{0,4},{4,0},{8,12},{12,8},{1,5},{5,1},{9,13},{13,9},{2,6},{6,2},{1... | collective-permute-start | bytes 786440 | tf_op jit(solution)/shard_map/ppermute | solution.py:37
  10.2 9.7 %collective-permute-start.4 = (bf16[8,128,128]{2,1,0:T(8,128)(2,1)S(1)}, bf16[8,128,128]{2,1,0:T(8,128)(2,1)S(1)}, u32[]{:S(2)}, u32[]{:S(2)}) collective-permute-start(bf16[8,128,128]{2,1,0:T(8,128)(2,1)S(1)} %get-tuple-element.33.refs_5_), channel_id=1, source_target_pairs={{4,8},{8,4},{5,9},{9,5},{6,10},{10,6},{7,11},{11,7},{20,24},{24,20... | collective-permute-start | bytes 786440 | tf_op jit(solution)/shard_map/ppermute | solution.py:45
  15.5 7.1 %copy-start = (bf16[1,8,512,128]{3,2,1,0:T(8,128)(2,1)S(1)}, bf16[1,8,512,128]{3,2,1,0:T(8,128)(2,1)}, u32[]{:S(2)}) copy-start(bf16[1,8,512,128]{3,2,1,0:T(8,128)(2,1)} %refs_1_.5) | copy-start | bytes 3145732
  15.5 7.1 %copy-start.5 = (s32[1,8,4,4]{1,3,2,0:T(4,128)S(1)}, s32[1,8,4,4]{1,3,2,0:T(4,128)}, u32[]{:S(2)}) copy-start(s32[1,8,4,4]{1,3,2,0:T(4,128)} %param.12) | copy-start | bytes 1540
  20.0 14.4 %collective-permute-start.6 = (bf16[4,512,128]{2,1,0:T(8,128)(2,1)S(1)}, bf16[4,512,128]{2,1,0:T(8,128)(2,1)S(1)}, u32[]{:S(2)}, u32[]{:S(2)}) collective-permute-start(bf16[4,512,128]{2,1,0:T(8,128)(2,1)S(1)} %get-tuple-element.43), channel_id=1, source_target_pairs={{0,4},{4,0},{8,12},{12,8},{1,5},{5,1},{9,13},{13,9},{2,6},{6,2},{1... | collective-permute-start | bytes 1572872 | tf_op jit(solution)/shard_map/ppermute | solution.py:37
  20.0 4.8 %copy-start.2 = (bf16[5,256,256]{2,1,0:T(8,128)(2,1)S(1)}, bf16[5,256,256]{2,1,0:T(8,128)(2,1)}, u32[]{:S(2)}) copy-start(bf16[5,256,256]{2,1,0:T(8,128)(2,1)} %refs_4_.3) | copy-start | bytes 1966084
  20.0 4.8 %copy-start.3 = (bf16[5,256,128]{2,1,0:T(8,128)(2,1)S(1)}, bf16[5,256,128]{2,1,0:T(8,128)(2,1)}, u32[]{:S(2)}) copy-start(bf16[5,256,128]{2,1,0:T(8,128)(2,1)} %refs_5_.3) | copy-start | bytes 983044
  20.0 21.1 %collective-permute-start.9 = (bf16[4,512,128]{2,1,0:T(8,128)(2,1)S(1)}, bf16[4,512,128]{2,1,0:T(8,128)(2,1)S(1)}, u32[]{:S(2)}, u32[]{:S(2)}) collective-permute-start(bf16[4,512,128]{2,1,0:T(8,128)(2,1)S(1)} %get-tuple-element.47), channel_id=1, source_target_pairs={{4,8},{8,4},{5,9},{9,5},{6,10},{10,6},{7,11},{11,7},{20,24},{24,20... | collective-permute-start | bytes 1572872 | tf_op jit(solution)/shard_map/ppermute | solution.py:45
  23.4 1.3 %collective-permute-start.5 = (bf16[8,16,256]{2,1,0:T(8,128)(2,1)S(1)}, bf16[8,16,256]{2,1,0:T(8,128)(2,1)S(1)}, u32[]{:S(2)}, u32[]{:S(2)}) collective-permute-start(bf16[8,16,256]{2,1,0:T(8,128)(2,1)S(1)} %seam.1.refs_4_), channel_id=1, source_target_pairs={{0,1},{1,0},{2,3},{3,2},{4,5},{5,4},{6,7},{7,6},{8,9},{9,8},{10,11... | collective-permute-start | bytes 196616 | tf_op jit(solution)/shard_map/ppermute | solution.py:641
  27.8 12.0 %collective-permute-start.7 = (bf16[2,512,128]{2,1,0:T(8,128)(2,1)S(1)}, bf16[2,512,128]{2,1,0:T(8,128)(2,1)S(1)}, u32[]{:S(2)}, u32[]{:S(2)}) collective-permute-start(bf16[2,512,128]{2,1,0:T(8,128)(2,1)S(1)} %get-tuple-element.35.refs_6_), channel_id=1, source_target_pairs={{0,4},{4,0},{8,12},{12,8},{1,5},{5,1},{9,13},{13,9},{2,6},{6,2},{1... | collective-permute-start | bytes 786440 | tf_op jit(solution)/shard_map/ppermute | solution.py:37
  28.2 13.0 %collective-permute-start.8 = (bf16[2,512,128]{2,1,0:T(8,128)(2,1)S(1)}, bf16[2,512,128]{2,1,0:T(8,128)(2,1)S(1)}, u32[]{:S(2)}, u32[]{:S(2)}) collective-permute-start(bf16[2,512,128]{2,1,0:T(8,128)(2,1)S(1)} %get-tuple-element.36.refs_7_), channel_id=1, source_target_pairs={{4,8},{8,4},{5,9},{9,5},{6,10},{10,6},{7,11},{11,7},{20,24},{24,20... | collective-permute-start | bytes 786440 | tf_op jit(solution)/shard_map/ppermute | solution.py:45
  34.4 9.9 %collective-permute-start.10 = (bf16[2,512,128]{2,1,0:T(8,128)(2,1)S(1)}, bf16[2,512,128]{2,1,0:T(8,128)(2,1)S(1)}, u32[]{:S(2)}, u32[]{:S(2)}) collective-permute-start(bf16[2,512,128]{2,1,0:T(8,128)(2,1)S(1)} %get-tuple-element.54), channel_id=1, source_target_pairs={{0,4},{4,0},{8,12},{12,8},{1,5},{5,1},{9,13},{13,9},{2,6},{6,2},{1... | collective-permute-start | bytes 786440 | tf_op jit(solution)/shard_map/ppermute | solution.py:37
  34.4 11.4 %collective-permute-start.11 = (bf16[2,512,128]{2,1,0:T(8,128)(2,1)S(1)}, bf16[2,512,128]{2,1,0:T(8,128)(2,1)S(1)}, u32[]{:S(2)}, u32[]{:S(2)}) collective-permute-start(bf16[2,512,128]{2,1,0:T(8,128)(2,1)S(1)} %get-tuple-element.55), channel_id=1, source_target_pairs={{4,8},{8,4},{5,9},{9,5},{6,10},{10,6},{7,11},{11,7},{20,24},{24,20... | collective-permute-start | bytes 786440 | tf_op jit(solution)/shard_map/ppermute | solution.py:45

commit v3 on v2

--- a/solution.py
+++ b/solution.py
@@ -172,20 +172,6 @@
     )(low, high)
 
 
-def held_until(values, *earlier):
-    anywhere = pl.BlockSpec(memory_space=pl.ANY)
-    count = len(values)
-    return pl.pallas_call(
-        lambda *refs: None,
-        in_specs=[anywhere] * count + [IN_VMEM] * len(earlier),
-        out_specs=[anywhere] * count,
-        out_shape=[jax.ShapeDtypeStruct(value.shape, value.dtype) for value in values],
-        input_output_aliases={i: i for i in range(count)},
-        compiler_params=params(4),
-        name="held",
-    )(*values, *earlier)
-
-
 def gather_kernel(near_list, far_list, prev_ref, near_out, far_out, sems):
     _, band_blocks, _, band_rows = near_list.shape
     slots, width, _ = near_out.shape
@@ -318,9 +304,9 @@
 
 
 def horizontal_kernel(
-    rows, hidden_ref, low_ref, high_ref, seam_ref, gates_ref, cand_ref, out_ref, near_ref, far_ref,
-    joined, reset, partial,
+    rows, hidden_ref, low_ref, high_ref, seam_ref, gates_ref, cand_ref, out_ref, *rest
 ):
+    *sent, joined, reset, partial = rest
     _, width, ch = hidden_ref.shape
     taps = gates_ref.shape[0]
     half = taps // 2
@@ -373,19 +359,20 @@
         reset[r, pl.ds(pad, span), :] = blended.astype(bf16)
     for r in count:
         out_ref[r] = reset[r, pl.ds(own, width), :]
-    near_ref[...] = out_ref[pl.ds(half * near_below(), half)]
-    far_ref[...] = out_ref[pl.ds(half - half * near_below(), half)]
-
-
-def horizontal_pass(rows, hidden, low, high, seam, gates, cand, *earlier):
+    near = half * near_below()
+    for sent_ref, first in zip(sent, (near, half - near)):
+        sent_ref[...] = out_ref[pl.ds(first, half)]
+
+
+def horizontal_pass(rows, send, hidden, low, high, seam, gates, cand):
     _, width, ch = hidden.shape
     taps = gates.shape[0]
     length = width + SEAM + 2 * SEAM
     shape = lambda count: jax.ShapeDtypeStruct((count, width, ch), bf16)
-    shapes = [shape(len(rows))] + [shape(taps // 2)] * 2
-    return pl.pallas_call(
-        ordered(functools.partial(horizontal_kernel, rows), 6, earlier),
-        in_specs=[IN_VMEM] * (6 + len(earlier)),
+    shapes = [shape(len(rows))] + [shape(taps // 2)] * (2 if send else 0)
+    return pl.pallas_call(
+        functools.partial(horizontal_kernel, rows),
+        in_specs=[IN_VMEM] * 6,
         out_specs=[IN_VMEM] * len(shapes),
         out_shape=shapes,
         scratch_shapes=[
@@ -395,7 +382,7 @@
         ],
         compiler_params=params(11),
         name="horizontal",
-    )(hidden, low, high, seam, gates, cand, *earlier)
+    )(hidden, low, high, seam, gates, cand)
 
 
 def pairs_kernel(gates_ref, cand_ref, reset_out, cand_out):
@@ -433,44 +420,67 @@
     )
 
 
-def gates_kernel(
-    outer_ref, inner_ref, low_ref, high_ref, gates_ref, update_ref, reset_ref, partial_ref
+def own_sums_kernel(
+    outer_ref, inner_ref, low_ref, high_ref, gates_ref, partial_ref, near_ref, far_ref
 ):
-    taps, depth, wide = gates_ref.shape
+    taps, _, wide = gates_ref.shape
     ch = wide // 2
     half = taps // 2
-    state = banded(outer_ref, inner_ref, half)
-    sources = (state, state_rows(low_ref, high_ref))
-    rows = len(state)
-    inner = range(half, rows - half)
+    sources = (banded(outer_ref, inner_ref, half), state_rows(low_ref, high_ref))
+    rows = len(sources[0])
     weights = lambda first, last: gates_ref[pl.ds(first, last - first)].reshape(-1, wide)
-    sums = [dotf(stack(sources, range(y - half, y + half + 1)), weights(0, taps)) for y in inner]
     for i, y in enumerate([*range(half), *range(rows - half, rows)]):
         first, last = max(y - half, 0), min(y + half + 1, rows)
         partial_ref[i] = dotf(
             stack(sources, range(first, last)), weights(first - y + half, last - y + half)
         )
+    near = half * near_below()
+    near_ref[...] = partial_ref[pl.ds(near, half), :, pl.ds(ch, ch)].astype(bf16)
+    far_ref[...] = partial_ref[pl.ds(half - near, half), :, pl.ds(ch, ch)].astype(bf16)
+
+
+def own_sums(outer, inner, low, high, gates):
+    count, width, ch = outer.shape
+    half = gates.shape[0] // 2
+    sent = jax.ShapeDtypeStruct((half, width, ch), bf16)
+    return pl.pallas_call(
+        own_sums_kernel,
+        in_specs=[IN_VMEM] * 5,
+        out_specs=[IN_VMEM] * 3,
+        out_shape=[jax.ShapeDtypeStruct((count, width, 2 * ch), f32), sent, sent],
+        compiler_params=params(4),
+        name="own_sums",
+    )(outer, inner, low, high, gates)
+
+
+def gates_kernel(outer_ref, inner_ref, low_ref, high_ref, gates_ref, update_ref, reset_ref):
+    taps, _, wide = gates_ref.shape
+    ch = wide // 2
+    half = taps // 2
+    state = banded(outer_ref, inner_ref, half)
+    sources = (state, state_rows(low_ref, high_ref))
+    inner = range(half, len(state) - half)
+    weights = gates_ref[...].reshape(-1, wide)
+    sums = [dotf(stack(sources, range(y - half, y + half + 1)), weights) for y in inner]
     for i, y in enumerate(inner):
         piece, at = state[y]
         update_ref[i] = sigmoid(sums[i][:, :ch])
         reset_ref[i] = (sigmoid(sums[i][:, ch:]) * piece[at].astype(f32)).astype(bf16)
 
 
-def inner_gates(outer, inner, low, high, gates):
+def inner_gates(outer, inner, low, high, gates, *earlier):
     count, width, ch = inner.shape
-    half = gates.shape[0] // 2
-    return pl.pallas_call(
-        gates_kernel,
-        in_specs=[IN_VMEM] * 5,
-        out_specs=[IN_VMEM] * 3,
+    return pl.pallas_call(
+        ordered(gates_kernel, 5, earlier),
+        in_specs=[IN_VMEM] * (5 + len(earlier)),
+        out_specs=[IN_VMEM] * 2,
         out_shape=[
             jax.ShapeDtypeStruct((count, width, ch), f32),
             jax.ShapeDtypeStruct((count, width, ch), bf16),
-            jax.ShapeDtypeStruct((2 * half, width, 2 * ch), f32),
         ],
         compiler_params=params(4),
         name="inner_gates",
-    )(outer, inner, low, high, gates)
+    )(outer, inner, low, high, gates, *earlier)
 
 
 def outer_kernel(
@@ -485,11 +495,10 @@
     above, below = state_rows(hidden_rim)[:half], state_rows(hidden_rim)[half:]
     own, flow = state_rows(outer_ref), state_rows(low_ref, high_ref)
     rim = state_rows(motion_rim)
-    top = (above + own[:half], rim[half : 2 * half] + flow[:half])
-    bottom = (own[half:] + below, flow[-half:] + rim[2 * half : 3 * half])
+    top = (above + own[:half], rim[:half] + flow[:half])
+    bottom = (own[half:] + below, flow[-half:] + rim[half:])
     weights = lambda first, last: gates_ref[pl.ds(first, last - first)].reshape(-1, wide)
     pairs = lambda first, last: pairs_ref[pl.ds(first, last - first)].reshape(-1, wide)
-    flow_pairs = lambda first: pairs_ref[pl.ds(first, half), ch:, :].reshape(-1, wide)
     sums = []
     for i in range(half):
         sums.append(dotf(stack(top, range(i, half)), weights(0, half - i)))
@@ -497,10 +506,8 @@
         rows = range(half, half + i + 1)
         sums.append(dotf(stack(bottom, rows), weights(taps - 1 - i, taps)))
     beyond = [
-        dotf(stack(top, range(2 * half)), pairs(half, taps + 1))
-        + dotf(stack((rim,), range(half)), flow_pairs(0)),
-        dotf(stack(bottom, range(2 * half)), pairs(0, 2 * half))
-        + dotf(stack((rim,), range(3 * half, 4 * half)), flow_pairs(2 * half)),
+        dotf(stack(top, range(half, 2 * half)), pairs(2 * half, 3 * half)),
+        dotf(stack(bottom, range(half)), pairs(0, half)),
     ]
     for i in range(2 * half):
         total = sums[i] + partial_ref[i]
@@ -522,7 +529,7 @@
             shape(f32),
             shape(bf16),
             shape(f32),
-            jax.ShapeDtypeStruct((4 * half, width, ch), bf16),
+            shape(bf16),
         ],
         scratch_shapes=[pltpu.VMEM((2 * half, width, ch), bf16)],
         compiler_params=params(4),
@@ -557,7 +564,7 @@
         first, last = max(y - half, 0), min(y + half + 2, rows)
         total = dotf(stack(sources, range(first, last)), weights(first - y + half, last - y + half))
         at = (0, half) if i == 0 else (blocks - half, blocks)
-        total += dotf(stack((rim,), range(half * (i + 1), half * (i + 2))), flow_weights(*at))
+        total += dotf(stack((rim,), range(half * i, half * (i + 1))), flow_weights(*at))
         partial_ref[2 * i], partial_ref[2 * i + 1] = total[:, :ch], total[:, ch:]
     for y in range(half, rows - half, 2):
         for k in range(2):
@@ -584,7 +591,7 @@
 
 def final_kernel(
     inner_ref, edge_near, edge_far, last_near, last_far, outer_ref, update_ref, partial_ref,
-    beyond_ref, reset_pairs, cand_pairs, out_ref, edge_rim, last_rim, reset_rim, done, sems,
+    beyond_ref, cand_pairs, out_ref, edge_rim, last_rim, reset_rim, done, sems,
 ):
     blocks, _, wide = cand_pairs.shape
     ch = wide // 2
@@ -595,15 +602,12 @@
     stores[0].start()
     fill_rim(edge_rim, edge_near, edge_far)
     fill_rim(last_rim, last_near, last_far)
-    last, rim = state_rows(last_rim), state_rows(reset_rim)
+    rim = state_rows(reset_rim)
     side = lambda i: range(half * i, half * i + half)
     weights = lambda ref, i: ref[pl.ds((blocks - half) * i, half), :ch, :].reshape(-1, wide)
-    beyond = [dotf(stack((last,), side(i)), weights(reset_pairs, i)) for i in range(2)]
-    for i in range(2):
-        for k in range(2):
-            at = 2 * i + k
-            total = beyond_ref[at] + beyond[i][:, k * ch : (k + 1) * ch]
-            reset_rim[at] = (sigmoid(total) * edge_rim[at].astype(f32)).astype(bf16)
+    for at in range(2 * half):
+        total = beyond_ref[at] + last_rim[at].astype(f32)
+        reset_rim[at] = (sigmoid(total) * edge_rim[at].astype(f32)).astype(bf16)
     sums = [dotf(stack((rim,), side(i)), weights(cand_pairs, i)) for i in range(2)]
     for i in range(2):
         for k in range(2):
@@ -617,18 +621,18 @@
         store.wait()
 
 
-def final_states(inner, edge_rims, last_rims, outer, update, partial, beyond, reset_pairs, cand_pairs):
+def final_states(inner, edge_rims, last_rims, outer, update, partial, beyond, cand_pairs):
     count, width, ch = outer.shape
     rows = count + inner.shape[0]
     return pl.pallas_call(
         final_kernel,
-        in_specs=[IN_VMEM] * 11,
+        in_specs=[IN_VMEM] * 10,
         out_specs=IN_HBM,
         out_shape=jax.ShapeDtypeStruct((1, rows, width, ch), bf16),
         scratch_shapes=[pltpu.VMEM((count, width, ch), bf16)] * 4 + [pltpu.SemaphoreType.DMA((3,))],
         compiler_params=params(4),
         name="final_states",
-    )(inner, *edge_rims, *last_rims, outer, update, partial, beyond, reset_pairs, cand_pairs)
+    )(inner, *edge_rims, *last_rims, outer, update, partial, beyond, cand_pairs)
 
 
 def shards(
@@ -650,20 +654,20 @@
     near, far = swap_rows(*blocks)
     high = motion_of(rows // 2, rows // 2, left_feats, right_feats, edge, enc_weight, *blocks)
     reset_pairs, cand_pairs = pairs_of(vgate_w, vcand_w)
-    edges = held_until(edges_of(low, high, rows // 2), near, far, reset_pairs)
+    edges = edges_of(low, high, half)
     motion_rims = swap_rows(*edges)
     seam = seam_of(warp_list, prev_hidden, near, far, low, high)
     warped = warp_of(warp_list, prev_hidden, near, far, seam)
     seam = swap_cols(seam)
-    outer, *edges = horizontal_pass(outer_rows, warped, low, high, seam, hgate_w, hcand_w)
+    outer, *edges = horizontal_pass(outer_rows, True, warped, low, high, seam, hgate_w, hcand_w)
+    warped, edges, motion_rims = pinned((warped, edges, motion_rims))
     edge_rims = swap_rows(*edges)
-    inner, *edges = horizontal_pass(
-        inner_rows, warped, low, high, seam, hgate_w, hcand_w, *edges
-    )
-    inner, edges, motion_near = pinned((inner, edges, motion_rims[0]))
-    motion_rims = (motion_near, motion_rims[1])
+    (inner,) = horizontal_pass(
+        inner_rows, False, warped, low, high, seam, hgate_w, hcand_w
+    )
+    partial, *edges = own_sums(outer, inner, low, high, vgate_w)
     last_rims = swap_rows(*edges)
-    update_inner, reset_inner, partial = inner_gates(outer, inner, low, high, vgate_w)
+    update_inner, reset_inner = inner_gates(outer, inner, low, high, vgate_w, *edges)
     update_outer, reset_outer, beyond, motion_rim = outer_gates(
         outer, partial, low, high, edge_rims, motion_rims, vgate_w, reset_pairs
     )
@@ -672,7 +676,7 @@
         resets, low, high, motion_rim, inner, update_inner, cand_pairs
     )
     return final_states(
-        inner, edge_rims, last_rims, outer, update_outer, partial, beyond, reset_pairs, cand_pairs
+        inner, edge_rims, last_rims, outer, update_outer, partial, beyond, cand_pairs
     )
 
 

time: 47.9 us -> 45 us (0.939)
  waiting for transfers between devices: 8.47 us -> 4.87 us
  starting transfers between devices: 16.2 us -> 17.1 us
    ppermute x5, waiting for transfers between devices: 6.3 us -> 3.15 us  [swap_far(): return lax.ppermute(value, axis, pairs)]
    ppermute x5, starting transfers between devices: 14.5 us -> 15.7 us  [swap_far(): return lax.ppermute(value, axis, pairs)]
  transfers between devices with their start and end apart: 12 -> 12, of which waited for: 6 -> 6; matrix products, arithmetic and copies ran while one was open for 0% -> 0% of each run, Pallas kernels for 41% -> 43%
where the time goes in v3:
time: 45 us; the launch traced here: 44.6 us
  Pallas kernels  22.2 us (49%)
  starting transfers between devices  17.1 us (38%)
  waiting for transfers between devices  4.87 us (11%)
    ppermute x5, starting transfers between devices, swap_far(): return lax.ppermute(value, axis, pairs)  15.7 us
    pallas_call x2, Pallas kernels, horizontal_pass(): pl.pallas_call(functools.partial(horizontal_kernel, rows), in_specs=[IN_V...  5.91 us
    pallas_call x2, Pallas kernels, motion_of(): pl.pallas_call(ordered(functools.partial(motion_kernel, first), 4, earlie...  5.29 us
    ppermute x5, waiting for transfers between devices, swap_far(): return lax.ppermute(value, axis, pairs)  3.15 us
    pallas_call x1, Pallas kernels, inner_states(): pl.pallas_call(cand_kernel, in_specs=[IN_VMEM] * 8, out_specs=[IN_VMEM] *...  1.66 us
    ppermute x5, waiting for transfers between devices, swap_near(): return lax.ppermute(value, axis, pairs)  1.65 us
    pallas_call x1, Pallas kernels, inner_gates(): pl.pallas_call(ordered(gates_kernel, 5, earlier), in_specs=[IN_VMEM] * (5...  1.58 us
    pallas_call x1, Pallas kernels, gather_blocks(): pl.pallas_call(ordered(gather_kernel, 3, earlier), in_specs=[IN_VMEM, IN_...  1.57 us
  transfers between devices with their start and end apart: 12, of which 6 were waited for; matrix products, arithmetic and copies ran while one was open for 0% of the time, Pallas kernels for 43%

profile of v3, /device:TPU:8, one launch (start us, length us, event | category | flops | bytes accessed | tf_op | source)
XLA Modules:
  0.0 44.6 jit_solution(11648243181403524037)
XLA Ops:
  0.0 0.0 collective-permute-start.2
  0.0 3.5 %collective-permute-start.1 = (s32[1,4,4,8]{3,2,1,0:T(4,128)}, s32[1,4,4,8]{3,2,1,0:T(4,128)S(1)}, u32[]{:S(2)}, u32[]{:S(2)}) collective-permute-start(s32[1,4,4,8]{3,2,1,0:T(4,128)} %bitcast.1), channel_id=1, source_target_pairs={{4,8},{8,4},{5,9},{9,5},{6,10},{10,6},{7,11},{11,7},{20,24},{24,20... | collective-permute-start | bytes 1544 | tf_op jit(solution)/shard_map/ppermute | solution.py:45
  3.5 0.1 collective-permute-start
  3.6 0.0 collective-permute-done.2.refs_2_
  3.6 2.6 %motion.2.refs_3_.low_ref.refs_2_ = bf16[4,512,128]{2,1,0:T(8,128)(2,1)S(1)} custom-call(bf16[1,8,512,128]{3,2,1,0:T(8,128)(2,1)} %refs_0_.3, bf16[1,8,512,128]{3,2,1,0:T(8,128)(2,1)} %refs_1_.4, bf16[1,8,512,128]{3,2,1,0:T(8,128)(2,1)S(1)} %collective-permute-done.2.refs_2_, bf16[192,128]{1,0:T(8,128)(2,1)} %refs_3_.3), custom_call_target="tpu_custom_call" | custom-call | tf_op jit(solution)/shard_map/motion/pallas_call | solution.py:139
  6.2 0.0 collective-permute-done.1.refs_1_
  6.2 1.2 %collective-permute-done.refs_0_ = s32[1,4,4,8]{3,2,1,0:T(4,128)S(1)} collective-permute-done((s32[1,4,4,8]{3,2,1,0:T(4,128)}, s32[1,4,4,8]{3,2,1,0:T(4,128)S(1)}, u32[]{:S(2)}, u32[]{:S(2)}) %collective-permute-start) | collective-permute-done | bytes 544 | tf_op jit(solution)/shard_map/ppermute | solution.py:37
  7.4 1.6 %gather.1 = (bf16[8,128,128]{2,1,0:T(8,128)(2,1)S(1)}, bf16[8,128,128]{2,1,0:T(8,128)(2,1)S(1)}) custom-call(s32[1,4,4,8]{3,2,1,0:T(4,128)S(1)} %collective-permute-done.refs_0_, s32[1,4,4,8]{3,2,1,0:T(4,128)S(1)} %collective-permute-done.1.refs_1_, bf16[1,8,512,128]{3,2,1,0:T(8,128)(2,1)} %refs_1_.5, bf16[4,512,128]{2,1,0:T(8,128)(2,1)S(1)} %motion.2.refs_3_.low_ref.refs_2_), custom_call_target="tpu_custom_call" | custom-call | tf_op jit(solution)/shard_map/gather/pallas_call | solution.py:213
  9.0 1.1 %collective-permute-start.3 = (bf16[8,128,128]{2,1,0:T(8,128)(2,1)S(1)}, bf16[8,128,128]{2,1,0:T(8,128)(2,1)S(1)}, u32[]{:S(2)}, u32[]{:S(2)}) collective-permute-start(bf16[8,128,128]{2,1,0:T(8,128)(2,1)S(1)} %get-tuple-element.30.refs_4_), channel_id=1, source_target_pairs={{0,4},{4,0},{8,12},{12,8},{1,5},{5,1},{9,13},{13,9},{2,6},{6,2},{1... | collective-permute-start | bytes 786440 | tf_op jit(solution)/shard_map/ppermute | solution.py:37
  10.1 0.0 copy-start.1
  10.1 2.5 %collective-permute-start.4 = (bf16[8,128,128]{2,1,0:T(8,128)(2,1)S(1)}, bf16[8,128,128]{2,1,0:T(8,128)(2,1)S(1)}, u32[]{:S(2)}, u32[]{:S(2)}) collective-permute-start(bf16[8,128,128]{2,1,0:T(8,128)(2,1)S(1)} %get-tuple-element.31.refs_5_), channel_id=1, source_target_pairs={{4,8},{8,4},{5,9},{9,5},{6,10},{10,6},{7,11},{11,7},{20,24},{24,20... | collective-permute-start | bytes 786440 | tf_op jit(solution)/shard_map/ppermute | solution.py:45
  12.6 2.6 %motion.3.high_ref.refs_3_ = bf16[4,512,128]{2,1,0:T(8,128)(2,1)S(1)} custom-call(bf16[1,8,512,128]{3,2,1,0:T(8,128)(2,1)} %refs_0_.3, bf16[1,8,512,128]{3,2,1,0:T(8,128)(2,1)} %refs_1_.4, bf16[1,8,512,128]{3,2,1,0:T(8,128)(2,1)S(1)} %collective-permute-done.2.refs_2_, bf16[192,128]{1,0:T(8,128)(2,1)} %refs_3_.3, ...), custom_call_target="tpu_custom_call" | custom-call | tf_op jit(solution)/shard_map/motion/pallas_call | solution.py:139
  15.2 0.1 edges.1
  15.4 0.1 collective-permute-start.6
  15.5 0.0 copy-start.2
  15.5 0.0 copy-start.3
  15.5 3.6 %collective-permute-start.7 = (bf16[2,512,128]{2,1,0:T(8,128)(2,1)S(1)}, bf16[2,512,128]{2,1,0:T(8,128)(2,1)S(1)}, u32[]{:S(2)}, u32[]{:S(2)}) collective-permute-start(bf16[2,512,128]{2,1,0:T(8,128)(2,1)S(1)} %get-tuple-element.36), channel_id=1, source_target_pairs={{4,8},{8,4},{5,9},{9,5},{6,10},{10,6},{7,11},{11,7},{20,24},{24,20... | collective-permute-start | bytes 786440 | tf_op jit(solution)/shard_map/ppermute | solution.py:45
  19.1 0.0 collective-permute-done.3.near_ref.refs_2_
  19.1 1.1 %collective-permute-done.4.far_ref.refs_3_ = bf16[8,128,128]{2,1,0:T(8,128)(2,1)S(1)} collective-permute-done((bf16[8,128,128]{2,1,0:T(8,128)(2,1)S(1)}, bf16[8,128,128]{2,1,0:T(8,128)(2,1)S(1)}, u32[]{:S(2)}, u32[]{:S(2)}) %collective-permute-start.4) | collective-permute-done | bytes 262176 | tf_op jit(solution)/shard_map/ppermute | solution.py:45
  20.2 0.0 copy-done.1
  20.2 0.0 copy-done.5
  20.2 0.9 %seam.1.refs_4_ = bf16[8,16,256]{2,1,0:T(8,128)(2,1)S(1)} custom-call(s32[1,4,4,8]{3,2,1,0:T(4,128)S(1)} %bitcast.3, bf16[1,8,512,128]{3,2,1,0:T(8,128)(2,1)S(1)} %copy-done.1, bf16[8,128,128]{2,1,0:T(8,128)(2,1)S(1)} %collective-permute-done.3.near_ref.refs_2_, bf16[8,128,128]{2,1,0:T(8,128)(2,1)S(1)} %collective-permute-done.4.far_ref.refs_3_, ...), custom_call_target="tpu_custom_call" | custom-call | tf_op jit(solution)/shard_map/seam/pallas_call | solution.py:269
  21.1 0.1 collective-permute-start.5
  21.2 1.2 %warp.1.hidden_ref = bf16[8,512,128]{2,1,0:T(8,128)(2,1)S(1)} custom-call(s32[1,4,4,8]{3,2,1,0:T(4,128)S(1)} %bitcast.4, bf16[1,8,512,128]{3,2,1,0:T(8,128)(2,1)S(1)} %copy-done.1, bf16[8,128,128]{2,1,0:T(8,128)(2,1)S(1)} %collective-permute-done.3.near_ref.refs_2_, bf16[8,128,128]{2,1,0:T(8,128)(2,1)S(1)} %collective-permute-done.4.far_ref.refs_3_, ...), custom_call_target="tpu_custom_call" | custom-call | tf_op jit(solution)/shard_map/warp/pallas_call | solution.py:296
  22.4 0.1 collective-permute-done.5.seam_ref
  22.4 0.0 copy-done.2
  22.4 0.0 copy-done.3
  22.4 3.0 %horizontal.2 = (bf16[4,512,128]{2,1,0:T(8,128)(2,1)S(1)}, bf16[2,512,128]{2,1,0:T(8,128)(2,1)S(1)}, bf16[2,512,128]{2,1,0:T(8,128)(2,1)S(1)}) custom-call(bf16[8,512,128]{2,1,0:T(8,128)(2,1)S(1)} %warp.1.hidden_ref, bf16[4,512,128]{2,1,0:T(8,128)(2,1)S(1)} %motion.2.refs_3_.low_ref.refs_2_, bf16[4,512,128]{2,1,0:T(8,128)(2,1)S(1)} %motion.3.high_ref.refs_3_, ...), custom_call_target="tpu_custom_call" | custom-call | tf_op jit(solution)/shard_map/horizontal/pallas_call | solution.py:373
  25.5 0.0 collective-permute-done.6.motion_near
  25.5 0.1 collective-permute-done.7.motion_far
  25.6 0.0 collective-permute-start.8
  25.6 3.0 %collective-permute-start.9 = (bf16[2,512,128]{2,1,0:T(8,128)(2,1)S(1)}, bf16[2,512,128]{2,1,0:T(8,128)(2,1)S(1)}, u32[]{:S(2)}, u32[]{:S(2)}) collective-permute-start(bf16[2,512,128]{2,1,0:T(8,128)(2,1)S(1)} %get-tuple-element.40), channel_id=1, source_target_pairs={{4,8},{8,4},{5,9},{9,5},{6,10},{10,6},{7,11},{11,7},{20,24},{24,20... | collective-permute-start | bytes 786440 | tf_op jit(solution)/shard_map/ppermute | solution.py:45
  28.6 2.9 %horizontal.3.inner_ref.refs_1_ = bf16[4,512,128]{2,1,0:T(8,128)(2,1)S(1)} custom-call(bf16[8,512,128]{2,1,0:T(8,128)(2,1)S(1)} %warp.1.hidden_ref, bf16[4,512,128]{2,1,0:T(8,128)(2,1)S(1)} %motion.2.refs_3_.low_ref.refs_2_, bf16[4,512,128]{2,1,0:T(8,128)(2,1)S(1)} %motion.3.high_ref.refs_3_, bf16[8,16,256]{2,1,0:T(8,128)(2,1)S(1)} %collective-permute-done.5.seam_ref, ...), custom_call_target="tpu_custom_call" | custom-call | tf_op jit(solution)/shard_map/horizontal/pallas_call | solution.py:373
  31.5 0.0 copy-start.4
  31.5 0.0 copy-done
  31.5 1.3 %own_sums.1 = (f32[4,512,256]{2,1,0:T(8,128)S(1)}, bf16[2,512,128]{2,1,0:T(8,128)(2,1)S(1)}, bf16[2,512,128]{2,1,0:T(8,128)(2,1)S(1)}) custom-call(bf16[4,512,128]{2,1,0:T(8,128)(2,1)S(1)} %get-tuple-element.32.outer_ref.refs_0_, bf16[4,512,128]{2,1,0:T(8,128)(2,1)S(1)} %horizontal.3.inner_ref.refs_1_, ...), custom_call_target="tpu_custom_call" | custom-call | tf_op jit(solution)/shard_map/own_sums/pallas_call | solution.py:446
  32.8 0.1 collective-permute-start.10
  32.8 3.2 %collective-permute-start.11 = (bf16[2,512,128]{2,1,0:T(8,128)(2,1)S(1)}, bf16[2,512,128]{2,1,0:T(8,128)(2,1)S(1)}, u32[]{:S(2)}, u32[]{:S(2)}) collective-permute-start(bf16[2,512,128]{2,1,0:T(8,128)(2,1)S(1)} %get-tuple-element.46.refs_6_), channel_id=1, source_target_pairs={{4,8},{8,4},{5,9},{9,5},{6,10},{10,6},{7,11},{11,7},{20,24},{24,20... | collective-permute-start | bytes 786440 | tf_op jit(solution)/shard_map/ppermute | solution.py:45
  36.0 0.0 copy-done.4
  36.0 0.2 pairs.1
  36.3 1.6 %inner_gates.1 = (f32[4,512,128]{2,1,0:T(8,128)S(1)}, bf16[4,512,128]{2,1,0:T(8,128)(2,1)S(1)}) custom-call(bf16[4,512,128]{2,1,0:T(8,128)(2,1)S(1)} %get-tuple-element.32.outer_ref.refs_0_, bf16[4,512,128]{2,1,0:T(8,128)(2,1)S(1)} %horizontal.3.inner_ref.refs_1_, bf16[4,512,128]{2,1,0:T(8,128)(2,1)S(1)} %motion.2.refs_3_.low_ref.refs_2_, ...), custom_call_target="tpu_custom_call" | custom-call | tf_op jit(solution)/shard_map/inner_gates/pallas_call | solution.py:473
  37.8 0.0 collective-permute-done.8.hidden_near.edge_near
  37.8 0.0 collective-permute-done.9.hidden_far.edge_far
  37.9 0.9 %outer_gates.1 = (f32[4,512,128]{2,1,0:T(8,128)S(1)}, bf16[4,512,128]{2,1,0:T(8,128)(2,1)S(1)}, f32[4,512,128]{2,1,0:T(8,128)S(1)}, bf16[4,512,128]{2,1,0:T(8,128)(2,1)S(1)}) custom-call(bf16[4,512,128]{2,1,0:T(8,128)(2,1)S(1)} %get-tuple-element.32.outer_ref.refs_0_, f32[4,512,256]{2,1,0:T(8,128)S(1)} %get-tuple-element.38.partial_ref, ...), custom_call_target="tpu_custom_call" | custom-call | tf_op jit(solution)/shard_map/outer_gates/pallas_call | solution.py:524
  38.8 1.7 %inner_states.1 = (bf16[4,512,128]{2,1,0:T(8,128)(2,1)S(1)}, f32[4,512,128]{2,1,0:T(8,128)S(1)}) custom-call(bf16[4,512,128]{2,1,0:T(8,128)(2,1)S(1)} %get-tuple-element.44.reset_outer, bf16[4,512,128]{2,1,0:T(8,128)(2,1)S(1)} %get-tuple-element.47.reset_inner, bf16[4,512,128]{2,1,0:T(8,128)(2,1)S(1)} %motion.2.refs_3_.low_ref.refs_2_, ...), custom_call_target="tpu_custom_call" | custom-call | tf_op jit(solution)/shard_map/inner_states/pallas_call | solution.py:579
  40.5 0.5 %collective-permute-done.10.last_near = bf16[2,512,128]{2,1,0:T(8,128)(2,1)S(1)} collective-permute-done((bf16[2,512,128]{2,1,0:T(8,128)(2,1)S(1)}, bf16[2,512,128]{2,1,0:T(8,128)(2,1)S(1)}, u32[]{:S(2)}, u32[]{:S(2)}) %collective-permute-start.10) | collective-permute-done | bytes 262176 | tf_op jit(solution)/shard_map/ppermute | solution.py:37
  40.9 1.9 %collective-permute-done.11.last_far = bf16[2,512,128]{2,1,0:T(8,128)(2,1)S(1)} collective-permute-done((bf16[2,512,128]{2,1,0:T(8,128)(2,1)S(1)}, bf16[2,512,128]{2,1,0:T(8,128)(2,1)S(1)}, u32[]{:S(2)}, u32[]{:S(2)}) %collective-permute-start.11) | collective-permute-done | bytes 262176 | tf_op jit(solution)/shard_map/ppermute | solution.py:45
  42.8 1.6 %final_states.1 = bf16[1,8,512,128]{3,2,1,0:T(8,128)(2,1)} custom-call(bf16[4,512,128]{2,1,0:T(8,128)(2,1)S(1)} %get-tuple-element.51.inner_ref, bf16[2,512,128]{2,1,0:T(8,128)(2,1)S(1)} %collective-permute-done.8.hidden_near.edge_near, bf16[2,512,128]{2,1,0:T(8,128)(2,1)S(1)} %collective-permute-done.9.hidden_far.edge_far, ...), custom_call_target="tpu_custom_call" | custom-call | tf_op jit(solution)/shard_map/final_states/pallas_call | solution.py:627
  (2 shorter events, 0.0 us)
Async XLA Ops:
  0.0 3.6 %collective-permute-start.2 = (bf16[1,8,512,128]{3,2,1,0:T(8,128)(2,1)}, bf16[1,8,512,128]{3,2,1,0:T(8,128)(2,1)S(1)}, u32[]{:S(2)}, u32[]{:S(2)}) collective-permute-start(bf16[1,8,512,128]{3,2,1,0:T(8,128)(2,1)} %refs_1_.4), channel_id=1, source_target_pairs={{0,1},{1,0},{2,3},{3,2},{4,5},{5,4},{6,7},{7,6},{8,9},{9,8},{10,11... | collective-permute-start | bytes 3145736 | tf_op jit(solution)/shard_map/ppermute | solution.py:645
  0.0 6.2 %collective-permute-start.1 = (s32[1,4,4,8]{3,2,1,0:T(4,128)}, s32[1,4,4,8]{3,2,1,0:T(4,128)S(1)}, u32[]{:S(2)}, u32[]{:S(2)}) collective-permute-start(s32[1,4,4,8]{3,2,1,0:T(4,128)} %bitcast.1), channel_id=1, source_target_pairs={{4,8},{8,4},{5,9},{9,5},{6,10},{10,6},{7,11},{11,7},{20,24},{24,20... | collective-permute-start | bytes 1544 | tf_op jit(solution)/shard_map/ppermute | solution.py:45
  3.5 3.9 %collective-permute-start = (s32[1,4,4,8]{3,2,1,0:T(4,128)}, s32[1,4,4,8]{3,2,1,0:T(4,128)S(1)}, u32[]{:S(2)}, u32[]{:S(2)}) collective-permute-start(s32[1,4,4,8]{3,2,1,0:T(4,128)} %bitcast.2), channel_id=1, source_target_pairs={{0,4},{4,0},{8,12},{12,8},{1,5},{5,1},{9,13},{13,9},{2,6},{6,2},{1... | collective-permute-start | bytes 1544 | tf_op jit(solution)/shard_map/ppermute | solution.py:37
  9.0 10.1 %collective-permute-start.3 = (bf16[8,128,128]{2,1,0:T(8,128)(2,1)S(1)}, bf16[8,128,128]{2,1,0:T(8,128)(2,1)S(1)}, u32[]{:S(2)}, u32[]{:S(2)}) collective-permute-start(bf16[8,128,128]{2,1,0:T(8,128)(2,1)S(1)} %get-tuple-element.30.refs_4_), channel_id=1, source_target_pairs={{0,4},{4,0},{8,12},{12,8},{1,5},{5,1},{9,13},{13,9},{2,6},{6,2},{1... | collective-permute-start | bytes 786440 | tf_op jit(solution)/shard_map/ppermute | solution.py:37
  10.1 10.2 %copy-start.1 = (bf16[1,8,512,128]{3,2,1,0:T(8,128)(2,1)S(1)}, bf16[1,8,512,128]{3,2,1,0:T(8,128)(2,1)}, u32[]{:S(2)}) copy-start(bf16[1,8,512,128]{3,2,1,0:T(8,128)(2,1)} %refs_1_.5) | copy-start | bytes 3145732
  10.1 10.2 %copy-start.5 = (s32[1,8,4,4]{1,3,2,0:T(4,128)S(1)}, s32[1,8,4,4]{1,3,2,0:T(4,128)}, u32[]{:S(2)}) copy-start(s32[1,8,4,4]{1,3,2,0:T(4,128)} %param.12) | copy-start | bytes 1540
  10.1 10.1 %collective-permute-start.4 = (bf16[8,128,128]{2,1,0:T(8,128)(2,1)S(1)}, bf16[8,128,128]{2,1,0:T(8,128)(2,1)S(1)}, u32[]{:S(2)}, u32[]{:S(2)}) collective-permute-start(bf16[8,128,128]{2,1,0:T(8,128)(2,1)S(1)} %get-tuple-element.31.refs_5_), channel_id=1, source_target_pairs={{4,8},{8,4},{5,9},{9,5},{6,10},{10,6},{7,11},{11,7},{20,24},{24,20... | collective-permute-start | bytes 786440 | tf_op jit(solution)/shard_map/ppermute | solution.py:45
  15.4 10.1 %collective-permute-start.6 = (bf16[2,512,128]{2,1,0:T(8,128)(2,1)S(1)}, bf16[2,512,128]{2,1,0:T(8,128)(2,1)S(1)}, u32[]{:S(2)}, u32[]{:S(2)}) collective-permute-start(bf16[2,512,128]{2,1,0:T(8,128)(2,1)S(1)} %get-tuple-element.35), channel_id=1, source_target_pairs={{0,4},{4,0},{8,12},{12,8},{1,5},{5,1},{9,13},{13,9},{2,6},{6,2},{1... | collective-permute-start | bytes 786440 | tf_op jit(solution)/shard_map/ppermute | solution.py:37
  15.5 7.0 %copy-start.2 = (bf16[5,256,256]{2,1,0:T(8,128)(2,1)S(1)}, bf16[5,256,256]{2,1,0:T(8,128)(2,1)}, u32[]{:S(2)}) copy-start(bf16[5,256,256]{2,1,0:T(8,128)(2,1)} %gates_ref.6) | copy-start | bytes 1966084
  15.5 7.0 %copy-start.3 = (bf16[5,256,128]{2,1,0:T(8,128)(2,1)S(1)}, bf16[5,256,128]{2,1,0:T(8,128)(2,1)}, u32[]{:S(2)}) copy-start(bf16[5,256,128]{2,1,0:T(8,128)(2,1)} %cand_ref.4) | copy-start | bytes 983044
  15.5 10.1 %collective-permute-start.7 = (bf16[2,512,128]{2,1,0:T(8,128)(2,1)S(1)}, bf16[2,512,128]{2,1,0:T(8,128)(2,1)S(1)}, u32[]{:S(2)}, u32[]{:S(2)}) collective-permute-start(bf16[2,512,128]{2,1,0:T(8,128)(2,1)S(1)} %get-tuple-element.36), channel_id=1, source_target_pairs={{4,8},{8,4},{5,9},{9,5},{6,10},{10,6},{7,11},{11,7},{20,24},{24,20... | collective-permute-start | bytes 786440 | tf_op jit(solution)/shard_map/ppermute | solution.py:45
  21.1 1.3 %collective-permute-start.5 = (bf16[8,16,256]{2,1,0:T(8,128)(2,1)S(1)}, bf16[8,16,256]{2,1,0:T(8,128)(2,1)S(1)}, u32[]{:S(2)}, u32[]{:S(2)}) collective-permute-start(bf16[8,16,256]{2,1,0:T(8,128)(2,1)S(1)} %seam.1.refs_4_), channel_id=1, source_target_pairs={{0,1},{1,0},{2,3},{3,2},{4,5},{5,4},{6,7},{7,6},{8,9},{9,8},{10,11... | collective-permute-start | bytes 196616 | tf_op jit(solution)/shard_map/ppermute | solution.py:645
  25.5 6.0 %copy-start = (bf16[5,256,256]{2,1,0:T(8,128)(2,1)S(1)}, bf16[5,256,256]{2,1,0:T(8,128)(2,1)}, u32[]{:S(2)}) copy-start(bf16[5,256,256]{2,1,0:T(8,128)(2,1)} %refs_4_.1) | copy-start | bytes 1966084
  25.6 12.2 %collective-permute-start.8 = (bf16[2,512,128]{2,1,0:T(8,128)(2,1)S(1)}, bf16[2,512,128]{2,1,0:T(8,128)(2,1)S(1)}, u32[]{:S(2)}, u32[]{:S(2)}) collective-permute-start(bf16[2,512,128]{2,1,0:T(8,128)(2,1)S(1)} %get-tuple-element.39), channel_id=1, source_target_pairs={{0,4},{4,0},{8,12},{12,8},{1,5},{5,1},{9,13},{13,9},{2,6},{6,2},{1... | collective-permute-start | bytes 786440 | tf_op jit(solution)/shard_map/ppermute | solution.py:37
  25.6 12.2 %collective-permute-start.9 = (bf16[2,512,128]{2,1,0:T(8,128)(2,1)S(1)}, bf16[2,512,128]{2,1,0:T(8,128)(2,1)S(1)}, u32[]{:S(2)}, u32[]{:S(2)}) collective-permute-start(bf16[2,512,128]{2,1,0:T(8,128)(2,1)S(1)} %get-tuple-element.40), channel_id=1, source_target_pairs={{4,8},{8,4},{5,9},{9,5},{6,10},{10,6},{7,11},{11,7},{20,24},{24,20... | collective-permute-start | bytes 786440 | tf_op jit(solution)/shard_map/ppermute | solution.py:45
  31.5 4.6 %copy-start.4 = (bf16[5,256,128]{2,1,0:T(8,128)(2,1)S(1)}, bf16[5,256,128]{2,1,0:T(8,128)(2,1)}, u32[]{:S(2)}) copy-start(bf16[5,256,128]{2,1,0:T(8,128)(2,1)} %cand_ref.5) | copy-start | bytes 983044
  32.8 8.2 %collective-permute-start.10 = (bf16[2,512,128]{2,1,0:T(8,128)(2,1)S(1)}, bf16[2,512,128]{2,1,0:T(8,128)(2,1)S(1)}, u32[]{:S(2)}, u32[]{:S(2)}) collective-permute-start(bf16[2,512,128]{2,1,0:T(8,128)(2,1)S(1)} %get-tuple-element.45.refs_5_), channel_id=1, source_target_pairs={{0,4},{4,0},{8,12},{12,8},{1,5},{5,1},{9,13},{13,9},{2,6},{6,2},{1... | collective-permute-start | bytes 786440 | tf_op jit(solution)/shard_map/ppermute | solution.py:37
  32.8 10.0 %collective-permute-start.11 = (bf16[2,512,128]{2,1,0:T(8,128)(2,1)S(1)}, bf16[2,512,128]{2,1,0:T(8,128)(2,1)S(1)}, u32[]{:S(2)}, u32[]{:S(2)}) collective-permute-start(bf16[2,512,128]{2,1,0:T(8,128)(2,1)S(1)} %get-tuple-element.46.refs_6_), channel_id=1, source_target_pairs={{4,8},{8,4},{5,9},{9,5},{6,10},{10,6},{7,11},{11,7},{20,24},{24,20... | collective-permute-start | bytes 786440 | tf_op jit(solution)/shard_map/ppermute | solution.py:45

commit v4 on v3

--- a/solution.py
+++ b/solution.py
@@ -160,16 +160,16 @@
     far_ref[...] = jnp.where(below, low, high)
 
 
-def edges_of(low, high, count):
+def edges_of(low, high, count, *earlier):
     shape = jax.ShapeDtypeStruct((count,) + low.shape[1:], bf16)
     return pl.pallas_call(
-        edges_kernel,
-        in_specs=[IN_VMEM] * 2,
+        ordered(edges_kernel, 2, earlier),
+        in_specs=[IN_VMEM] * (2 + len(earlier)),
         out_specs=[IN_VMEM, IN_VMEM],
         out_shape=[shape, shape],
         compiler_params=params(4),
         name="edges",
-    )(low, high)
+    )(low, high, *earlier)
 
 
 def gather_kernel(near_list, far_list, prev_ref, near_out, far_out, sems):
@@ -385,12 +385,13 @@
     )(hidden, low, high, seam, gates, cand)
 
 
-def pairs_kernel(gates_ref, cand_ref, reset_out, cand_out):
+def pairs_kernel(gates_ref, cand_ref, update_out, reset_out, cand_out):
     taps, depth, ch = cand_ref.shape
     none = jnp.zeros((depth, ch), bf16)
+    update = lambda j: gates_ref[j, :, pl.ds(0, ch)]
     reset = lambda j: gates_ref[j, :, pl.ds(ch, ch)]
     cand = lambda j: cand_ref[j]
-    for out_ref, tap in ((reset_out, reset), (cand_out, cand)):
+    for out_ref, tap in ((update_out, update), (reset_out, reset), (cand_out, cand)):
         for j in range(taps + 1):
             out_ref[j, :, 0:ch] = tap(j) if j < taps else none
             out_ref[j, :, ch : 2 * ch] = tap(j - 1) if j > 0 else none
@@ -402,8 +403,8 @@
     return pl.pallas_call(
         pairs_kernel,
         in_specs=[IN_VMEM] * 2,
-        out_specs=[IN_VMEM] * 2,
-        out_shape=[shape, shape],
+        out_specs=[IN_VMEM] * 3,
+        out_shape=[shape, shape, shape],
         compiler_params=params(4),
         name="pairs",
     )(gates, cand)
@@ -420,40 +421,45 @@
     )
 
 
+def edge_sums(sources, pairs_ref, sums_ref):
+    blocks, _, wide = pairs_ref.shape
+    ch = wide // 2
+    half = (blocks - 1) // 2
+    rows = len(sources[0])
+    sides = ((range(2 * half), half), (range(rows - 2 * half, rows), 0))
+    for i, (own, first) in enumerate(sides):
+        weights = pairs_ref[pl.ds(first, 2 * half)].reshape(-1, wide)
+        both = dotf(stack(sources, own), weights)
+        sums_ref[2 * i], sums_ref[2 * i + 1] = both[:, :ch], both[:, ch:]
+
+
 def own_sums_kernel(
-    outer_ref, inner_ref, low_ref, high_ref, gates_ref, partial_ref, near_ref, far_ref
+    outer_ref, inner_ref, low_ref, high_ref, pairs_ref, sums_ref, near_ref, far_ref
 ):
-    taps, _, wide = gates_ref.shape
-    ch = wide // 2
-    half = taps // 2
+    half = near_ref.shape[0]
     sources = (banded(outer_ref, inner_ref, half), state_rows(low_ref, high_ref))
-    rows = len(sources[0])
-    weights = lambda first, last: gates_ref[pl.ds(first, last - first)].reshape(-1, wide)
-    for i, y in enumerate([*range(half), *range(rows - half, rows)]):
-        first, last = max(y - half, 0), min(y + half + 1, rows)
-        partial_ref[i] = dotf(
-            stack(sources, range(first, last)), weights(first - y + half, last - y + half)
-        )
+    edge_sums(sources, pairs_ref, sums_ref)
     near = half * near_below()
-    near_ref[...] = partial_ref[pl.ds(near, half), :, pl.ds(ch, ch)].astype(bf16)
-    far_ref[...] = partial_ref[pl.ds(half - near, half), :, pl.ds(ch, ch)].astype(bf16)
-
-
-def own_sums(outer, inner, low, high, gates):
+    near_ref[...] = sums_ref[pl.ds(near, half)].astype(bf16)
+    far_ref[...] = sums_ref[pl.ds(half - near, half)].astype(bf16)
+
+
+def own_sums(outer, inner, low, high, pairs):
     count, width, ch = outer.shape
-    half = gates.shape[0] // 2
-    sent = jax.ShapeDtypeStruct((half, width, ch), bf16)
+    sent = jax.ShapeDtypeStruct((count // 2, width, ch), bf16)
     return pl.pallas_call(
         own_sums_kernel,
         in_specs=[IN_VMEM] * 5,
         out_specs=[IN_VMEM] * 3,
-        out_shape=[jax.ShapeDtypeStruct((count, width, 2 * ch), f32), sent, sent],
+        out_shape=[jax.ShapeDtypeStruct((count, width, ch), f32), sent, sent],
         compiler_params=params(4),
         name="own_sums",
-    )(outer, inner, low, high, gates)
-
-
-def gates_kernel(outer_ref, inner_ref, low_ref, high_ref, gates_ref, update_ref, reset_ref):
+    )(outer, inner, low, high, pairs)
+
+
+def gates_kernel(
+    outer_ref, inner_ref, low_ref, high_ref, gates_ref, pairs_ref, update_ref, reset_ref, sums_ref
+):
     taps, _, wide = gates_ref.shape
     ch = wide // 2
     half = taps // 2
@@ -462,29 +468,28 @@
     inner = range(half, len(state) - half)
     weights = gates_ref[...].reshape(-1, wide)
     sums = [dotf(stack(sources, range(y - half, y + half + 1)), weights) for y in inner]
+    edge_sums(sources, pairs_ref, sums_ref)
     for i, y in enumerate(inner):
         piece, at = state[y]
         update_ref[i] = sigmoid(sums[i][:, :ch])
         reset_ref[i] = (sigmoid(sums[i][:, ch:]) * piece[at].astype(f32)).astype(bf16)
 
 
-def inner_gates(outer, inner, low, high, gates, *earlier):
+def inner_gates(outer, inner, low, high, gates, pairs, *earlier):
     count, width, ch = inner.shape
-    return pl.pallas_call(
-        ordered(gates_kernel, 5, earlier),
-        in_specs=[IN_VMEM] * (5 + len(earlier)),
-        out_specs=[IN_VMEM] * 2,
-        out_shape=[
-            jax.ShapeDtypeStruct((count, width, ch), f32),
-            jax.ShapeDtypeStruct((count, width, ch), bf16),
-        ],
+    shape = lambda n, kind: jax.ShapeDtypeStruct((n, width, ch), kind)
+    return pl.pallas_call(
+        ordered(gates_kernel, 6, earlier),
+        in_specs=[IN_VMEM] * (6 + len(earlier)),
+        out_specs=[IN_VMEM] * 3,
+        out_shape=[shape(count, f32), shape(count, bf16), shape(outer.shape[0], f32)],
         compiler_params=params(4),
         name="inner_gates",
-    )(outer, inner, low, high, gates, *earlier)
+    )(outer, inner, low, high, gates, pairs, *earlier)
 
 
 def outer_kernel(
-    outer_ref, partial_ref, low_ref, high_ref, hidden_near, hidden_far, motion_near, motion_far,
+    outer_ref, update_sums, reset_sums, low_ref, high_ref, hidden_near, hidden_far, motion_near, motion_far,
     gates_ref, pairs_ref, update_ref, reset_ref, rim_ref, motion_rim, hidden_rim,
 ):
     taps, _, wide = gates_ref.shape
@@ -510,20 +515,20 @@
         dotf(stack(bottom, range(half)), pairs(0, half)),
     ]
     for i in range(2 * half):
-        total = sums[i] + partial_ref[i]
-        update_ref[i] = sigmoid(total[:, :ch])
-        reset_ref[i] = (sigmoid(total[:, ch:]) * outer_ref[i].astype(f32)).astype(bf16)
+        update_ref[i] = sigmoid(sums[i][:, :ch] + update_sums[i])
+        reset = sigmoid(sums[i][:, ch:] + reset_sums[i])
+        reset_ref[i] = (reset * outer_ref[i].astype(f32)).astype(bf16)
     for i in range(2):
         rim_ref[2 * i], rim_ref[2 * i + 1] = beyond[i][:, :ch], beyond[i][:, ch:]
 
 
-def outer_gates(outer, partial, low, high, hidden_rims, motion_rims, gates, pairs):
+def outer_gates(outer, sums, low, high, hidden_rims, motion_rims, gates, pairs):
     count, width, ch = outer.shape
     half = gates.shape[0] // 2
     shape = lambda kind: jax.ShapeDtypeStruct((count, width, ch), kind)
     return pl.pallas_call(
         outer_kernel,
-        in_specs=[IN_VMEM] * 10,
+        in_specs=[IN_VMEM] * 11,
         out_specs=[IN_VMEM] * 4,
         out_shape=[
             shape(f32),
@@ -534,7 +539,7 @@
         scratch_shapes=[pltpu.VMEM((2 * half, width, ch), bf16)],
         compiler_params=params(4),
         name="outer_gates",
-    )(outer, partial, low, high, *hidden_rims, *motion_rims, gates, pairs)
+    )(outer, *sums, low, high, *hidden_rims, *motion_rims, gates, pairs)
 
 
 def blend(state, update, total):
@@ -590,33 +595,33 @@
 
 
 def final_kernel(
-    inner_ref, edge_near, edge_far, last_near, last_far, outer_ref, update_ref, partial_ref,
-    beyond_ref, cand_pairs, out_ref, edge_rim, last_rim, reset_rim, done, sems,
+    near, first_ref, edge_ref, last_ref, outer_ref, update_ref, partial_ref, beyond_ref, cand_pairs,
+    out_ref, done, sems,
 ):
     blocks, _, wide = cand_pairs.shape
     ch = wide // 2
     half = (blocks - 1) // 2
     rows = out_ref.shape[1]
-    count = inner_ref.shape[0]
-    stores = [pltpu.make_async_copy(inner_ref, out_ref.at[0, pl.ds(half, count)], sems.at[0])]
-    stores[0].start()
-    fill_rim(edge_rim, edge_near, edge_far)
-    fill_rim(last_rim, last_near, last_far)
-    rim = state_rows(reset_rim)
-    side = lambda i: range(half * i, half * i + half)
-    weights = lambda ref, i: ref[pl.ds((blocks - half) * i, half), :ch, :].reshape(-1, wide)
-    for at in range(2 * half):
-        total = beyond_ref[at] + last_rim[at].astype(f32)
-        reset_rim[at] = (sigmoid(total) * edge_rim[at].astype(f32)).astype(bf16)
-    sums = [dotf(stack((rim,), side(i)), weights(cand_pairs, i)) for i in range(2)]
-    for i in range(2):
-        for k in range(2):
-            at = 2 * i + k
-            total = partial_ref[at] + sums[i][:, k * ch : (k + 1) * ch]
-            done[at] = blend(outer_ref[at], update_ref[at], total)
-        target = out_ref.at[0, pl.ds(0 if i == 0 else rows - half, half)]
-        stores.append(pltpu.make_async_copy(done.at[pl.ds(half * i, half)], target, sems.at[i + 1]))
-        stores[-1].start()
+    stores = []
+    if near:
+        count = first_ref.shape[0]
+        target = out_ref.at[0, pl.ds(half, count)]
+        stores.append(pltpu.make_async_copy(first_ref, target, sems.at[0]))
+        stores[0].start()
+    side = near_below() if near else 1 - near_below()
+    at = half * side
+    reset = []
+    for k in range(half):
+        total = beyond_ref[at + k] + last_ref[k].astype(f32)
+        reset.append((sigmoid(total) * edge_ref[k].astype(f32)).astype(bf16))
+    weights = cand_pairs[pl.ds((blocks - half) * side, half), :ch, :].reshape(-1, wide)
+    sums = dotf(jnp.concatenate(reset, axis=1), weights)
+    for k in range(half):
+        total = partial_ref[at + k] + sums[:, k * ch : (k + 1) * ch]
+        done[k] = blend(outer_ref[at + k], update_ref[at + k], total)
+    target = out_ref.at[0, pl.ds((rows - half) * side, half)]
+    stores.append(pltpu.make_async_copy(done, target, sems.at[1]))
+    stores[-1].start()
     for store in stores:
         store.wait()
 
@@ -624,15 +629,22 @@
 def final_states(inner, edge_rims, last_rims, outer, update, partial, beyond, cand_pairs):
     count, width, ch = outer.shape
     rows = count + inner.shape[0]
-    return pl.pallas_call(
-        final_kernel,
-        in_specs=[IN_VMEM] * 10,
-        out_specs=IN_HBM,
-        out_shape=jax.ShapeDtypeStruct((1, rows, width, ch), bf16),
-        scratch_shapes=[pltpu.VMEM((count, width, ch), bf16)] * 4 + [pltpu.SemaphoreType.DMA((3,))],
-        compiler_params=params(4),
-        name="final_states",
-    )(inner, *edge_rims, *last_rims, outer, update, partial, beyond, cand_pairs)
+    half = edge_rims[0].shape[0]
+
+    def side(near, first, edge, last):
+        return pl.pallas_call(
+            functools.partial(final_kernel, near),
+            in_specs=[IN_VMEM if near else IN_HBM] + [IN_VMEM] * 7,
+            out_specs=IN_HBM,
+            out_shape=jax.ShapeDtypeStruct((1, rows, width, ch), bf16),
+            scratch_shapes=[pltpu.VMEM((half, width, ch), bf16), pltpu.SemaphoreType.DMA((2,))],
+            input_output_aliases={} if near else {0: 0},
+            compiler_params=params(4),
+            name="final_near" if near else "final_far",
+        )(first, edge, last, outer, update, partial, beyond, cand_pairs)
+
+    out = side(True, inner, edge_rims[0], last_rims[0])
+    return side(False, out, edge_rims[1], last_rims[1])
 
 
 def shards(
@@ -653,8 +665,8 @@
     blocks = gather_blocks(*lists, prev_hidden, low)
     near, far = swap_rows(*blocks)
     high = motion_of(rows // 2, rows // 2, left_feats, right_feats, edge, enc_weight, *blocks)
-    reset_pairs, cand_pairs = pairs_of(vgate_w, vcand_w)
-    edges = edges_of(low, high, half)
+    update_pairs, reset_pairs, cand_pairs = pairs_of(vgate_w, vcand_w)
+    edges = edges_of(low, high, half, reset_pairs)
     motion_rims = swap_rows(*edges)
     seam = seam_of(warp_list, prev_hidden, near, far, low, high)
     warped = warp_of(warp_list, prev_hidden, near, far, seam)
@@ -665,11 +677,13 @@
     (inner,) = horizontal_pass(
         inner_rows, False, warped, low, high, seam, hgate_w, hcand_w
     )
-    partial, *edges = own_sums(outer, inner, low, high, vgate_w)
+    reset_sums, *edges = own_sums(outer, inner, low, high, reset_pairs)
     last_rims = swap_rows(*edges)
-    update_inner, reset_inner = inner_gates(outer, inner, low, high, vgate_w, *edges)
+    update_inner, reset_inner, update_sums = inner_gates(
+        outer, inner, low, high, vgate_w, update_pairs, *edges
+    )
     update_outer, reset_outer, beyond, motion_rim = outer_gates(
-        outer, partial, low, high, edge_rims, motion_rims, vgate_w, reset_pairs
+        outer, (update_sums, reset_sums), low, high, edge_rims, motion_rims, vgate_w, reset_pairs
     )
     resets = (reset_outer, reset_inner)
     inner, partial = inner_states(

time: 45 us -> 44.2 us (0.982)
  waiting for transfers between devices: 4.87 us -> 3.13 us
  Pallas kernels: 22.2 us -> 22.8 us
    ppermute x5, waiting for transfers between devices: 3.15 us -> 1.77 us  [swap_far(): return lax.ppermute(value, axis, pairs)]
    pallas_call x4 -> x5, Pallas kernels: 4.22 us -> 5.16 us  [the longest x1 2.07 us: inner_gates(): pl.pallas_call(ordered(gates_kernel, 6, earlier), in_specs=[IN_VMEM] * (6...]
  transfers between devices with their start and end apart: 12 -> 12, of which waited for: 6 -> 6; matrix products, arithmetic and copies ran while one was open for 0% -> 0% of each run, Pallas kernels for 43% -> 46%
where the time goes in v4:
time: 44.2 us; the launch traced here: 43.4 us
  Pallas kernels  22.8 us (52%)
  starting transfers between devices  17 us (38%)
  waiting for transfers between devices  3.13 us (7%)
    ppermute x5, starting transfers between devices, swap_far(): return lax.ppermute(value, axis, pairs)  15.6 us
    pallas_call x2, Pallas kernels, horizontal_pass(): pl.pallas_call(functools.partial(horizontal_kernel, rows), in_specs=[IN_V...  5.91 us
    pallas_call x2, Pallas kernels, motion_of(): pl.pallas_call(ordered(functools.partial(motion_kernel, first), 4, earlie...  5.29 us
    pallas_call x1, Pallas kernels, inner_gates(): pl.pallas_call(ordered(gates_kernel, 6, earlier), in_specs=[IN_VMEM] * (6...  2.07 us
    pallas_call x2, Pallas kernels, side(): pl.pallas_call(functools.partial(final_kernel, near), in_specs=[IN_VMEM i...  2.06 us
    ppermute x5, waiting for transfers between devices, swap_far(): return lax.ppermute(value, axis, pairs)  1.77 us
    pallas_call x1, Pallas kernels, inner_states(): pl.pallas_call(cand_kernel, in_specs=[IN_VMEM] * 8, out_specs=[IN_VMEM] *...  1.66 us
    pallas_call x1, Pallas kernels, gather_blocks(): pl.pallas_call(ordered(gather_kernel, 3, earlier), in_specs=[IN_VMEM, IN_...  1.57 us
  transfers between devices with their start and end apart: 12, of which 6 were waited for; matrix products, arithmetic and copies ran while one was open for 0% of the time, Pallas kernels for 46%

profile of v4, /device:TPU:8, one launch (start us, length us, event | category | flops | bytes accessed | tf_op | source)
XLA Modules:
  0.0 43.4 jit_solution(9292226626042368679)
XLA Ops:
  0.0 0.0 collective-permute-start.2
  0.0 3.5 %collective-permute-start.1 = (s32[1,4,4,8]{3,2,1,0:T(4,128)}, s32[1,4,4,8]{3,2,1,0:T(4,128)S(1)}, u32[]{:S(2)}, u32[]{:S(2)}) collective-permute-start(s32[1,4,4,8]{3,2,1,0:T(4,128)} %bitcast.1), channel_id=1, source_target_pairs={{4,8},{8,4},{5,9},{9,5},{6,10},{10,6},{7,11},{11,7},{20,24},{24,20... | collective-permute-start | bytes 1544 | tf_op jit(solution)/shard_map/ppermute | solution.py:45
  3.5 0.1 collective-permute-start
  3.6 0.0 collective-permute-done.2.refs_2_
  3.6 2.6 %motion.2.refs_3_.low_ref.refs_0_.refs_2_ = bf16[4,512,128]{2,1,0:T(8,128)(2,1)S(1)} custom-call(bf16[1,8,512,128]{3,2,1,0:T(8,128)(2,1)} %refs_0_.3, bf16[1,8,512,128]{3,2,1,0:T(8,128)(2,1)} %refs_1_.4, bf16[1,8,512,128]{3,2,1,0:T(8,128)(2,1)S(1)} %collective-permute-done.2.refs_2_, bf16[192,128]{1,0:T(8,128)(2,1)} %refs_3_.3), custom_call_target="tpu_custom_call" | custom-call | tf_op jit(solution)/shard_map/motion/pallas_call | solution.py:139
  6.2 0.0 copy-start.1
  6.2 0.0 copy-start.4
  6.3 0.0 collective-permute-done.1.refs_1_
  6.3 1.1 %collective-permute-done.refs_0_ = s32[1,4,4,8]{3,2,1,0:T(4,128)S(1)} collective-permute-done((s32[1,4,4,8]{3,2,1,0:T(4,128)}, s32[1,4,4,8]{3,2,1,0:T(4,128)S(1)}, u32[]{:S(2)}, u32[]{:S(2)}) %collective-permute-start) | collective-permute-done | bytes 544 | tf_op jit(solution)/shard_map/ppermute | solution.py:37
  7.4 1.6 %gather.1 = (bf16[8,128,128]{2,1,0:T(8,128)(2,1)S(1)}, bf16[8,128,128]{2,1,0:T(8,128)(2,1)S(1)}) custom-call(s32[1,4,4,8]{3,2,1,0:T(4,128)S(1)} %collective-permute-done.refs_0_, s32[1,4,4,8]{3,2,1,0:T(4,128)S(1)} %collective-permute-done.1.refs_1_, bf16[1,8,512,128]{3,2,1,0:T(8,128)(2,1)} %refs_1_.5, ...), custom_call_target="tpu_custom_call" | custom-call | tf_op jit(solution)/shard_map/gather/pallas_call | solution.py:213
  9.0 1.1 %collective-permute-start.3 = (bf16[8,128,128]{2,1,0:T(8,128)(2,1)S(1)}, bf16[8,128,128]{2,1,0:T(8,128)(2,1)S(1)}, u32[]{:S(2)}, u32[]{:S(2)}) collective-permute-start(bf16[8,128,128]{2,1,0:T(8,128)(2,1)S(1)} %get-tuple-element.32.refs_4_), channel_id=1, source_target_pairs={{0,4},{4,0},{8,12},{12,8},{1,5},{5,1},{9,13},{13,9},{2,6},{6,2},{1... | collective-permute-start | bytes 786440 | tf_op jit(solution)/shard_map/ppermute | solution.py:37
  10.1 2.3 %collective-permute-start.4 = (bf16[8,128,128]{2,1,0:T(8,128)(2,1)S(1)}, bf16[8,128,128]{2,1,0:T(8,128)(2,1)S(1)}, u32[]{:S(2)}, u32[]{:S(2)}) collective-permute-start(bf16[8,128,128]{2,1,0:T(8,128)(2,1)S(1)} %get-tuple-element.33.refs_5_), channel_id=1, source_target_pairs={{4,8},{8,4},{5,9},{9,5},{6,10},{10,6},{7,11},{11,7},{20,24},{24,20... | collective-permute-start | bytes 786440 | tf_op jit(solution)/shard_map/ppermute | solution.py:45
  12.5 0.0 copy-done.1
  12.5 0.0 copy-done.4
  12.5 0.3 pairs.1
  12.8 2.6 %motion.3.high_ref.refs_1_.refs_3_ = bf16[4,512,128]{2,1,0:T(8,128)(2,1)S(1)} custom-call(bf16[1,8,512,128]{3,2,1,0:T(8,128)(2,1)} %refs_0_.3, bf16[1,8,512,128]{3,2,1,0:T(8,128)(2,1)} %refs_1_.4, bf16[1,8,512,128]{3,2,1,0:T(8,128)(2,1)S(1)} %collective-permute-done.2.refs_2_, bf16[192,128]{1,0:T(8,128)(2,1)} %refs_3_.3, ...), custom_call_target="tpu_custom_call" | custom-call | tf_op jit(solution)/shard_map/motion/pallas_call | solution.py:139
  15.5 0.0 copy-start
  15.5 0.0 copy-start.5
  15.5 0.1 edges.1
  15.6 0.1 collective-permute-start.6
  15.7 3.6 %collective-permute-start.7 = (bf16[2,512,128]{2,1,0:T(8,128)(2,1)S(1)}, bf16[2,512,128]{2,1,0:T(8,128)(2,1)S(1)}, u32[]{:S(2)}, u32[]{:S(2)}) collective-permute-start(bf16[2,512,128]{2,1,0:T(8,128)(2,1)S(1)} %get-tuple-element.39), channel_id=1, source_target_pairs={{4,8},{8,4},{5,9},{9,5},{6,10},{10,6},{7,11},{11,7},{20,24},{24,20... | collective-permute-start | bytes 786440 | tf_op jit(solution)/shard_map/ppermute | solution.py:45
  19.3 0.0 collective-permute-done.3.near_ref.refs_2_
  19.3 0.5 %collective-permute-done.4.far_ref.refs_3_ = bf16[8,128,128]{2,1,0:T(8,128)(2,1)S(1)} collective-permute-done((bf16[8,128,128]{2,1,0:T(8,128)(2,1)S(1)}, bf16[8,128,128]{2,1,0:T(8,128)(2,1)S(1)}, u32[]{:S(2)}, u32[]{:S(2)}) %collective-permute-start.4) | collective-permute-done | bytes 262176 | tf_op jit(solution)/shard_map/ppermute | solution.py:45
  19.9 0.0 copy-done
  19.9 0.9 %seam.1.refs_4_ = bf16[8,16,256]{2,1,0:T(8,128)(2,1)S(1)} custom-call(s32[1,4,4,8]{3,2,1,0:T(4,128)S(1)} %bitcast.3, bf16[1,8,512,128]{3,2,1,0:T(8,128)(2,1)S(1)} %copy-done, bf16[8,128,128]{2,1,0:T(8,128)(2,1)S(1)} %collective-permute-done.3.near_ref.refs_2_, bf16[8,128,128]{2,1,0:T(8,128)(2,1)S(1)} %collective-permute-done.4.far_ref.refs_3_, ...), custom_call_target="tpu_custom_call" | custom-call | tf_op jit(solution)/shard_map/seam/pallas_call | solution.py:269
  20.8 0.0 copy-start.2
  20.8 0.0 copy-start.3
  20.8 0.1 collective-permute-start.5
  20.9 1.2 %warp.1.hidden_ref = bf16[8,512,128]{2,1,0:T(8,128)(2,1)S(1)} custom-call(s32[1,4,4,8]{3,2,1,0:T(4,128)S(1)} %bitcast.4, bf16[1,8,512,128]{3,2,1,0:T(8,128)(2,1)S(1)} %copy-done, bf16[8,128,128]{2,1,0:T(8,128)(2,1)S(1)} %collective-permute-done.3.near_ref.refs_2_, bf16[8,128,128]{2,1,0:T(8,128)(2,1)S(1)} %collective-permute-done.4.far_ref.refs_3_, ...), custom_call_target="tpu_custom_call" | custom-call | tf_op jit(solution)/shard_map/warp/pallas_call | solution.py:296
  22.0 0.1 collective-permute-done.5.seam_ref
  22.1 3.0 %horizontal.2 = (bf16[4,512,128]{2,1,0:T(8,128)(2,1)S(1)}, bf16[2,512,128]{2,1,0:T(8,128)(2,1)S(1)}, bf16[2,512,128]{2,1,0:T(8,128)(2,1)S(1)}) custom-call(bf16[8,512,128]{2,1,0:T(8,128)(2,1)S(1)} %warp.1.hidden_ref, bf16[4,512,128]{2,1,0:T(8,128)(2,1)S(1)} %motion.2.refs_3_.low_ref.refs_0_.refs_2_, bf16[4,512,128]{2,1,0:T(8,128)(2,1)S(1)} %motion.3.high_ref.refs_1_.refs_3_, ...), custom_call_target="tpu_custom_call" | custom-call | tf_op jit(solution)/shard_map/horizontal/pallas_call | solution.py:373
  25.1 0.0 collective-permute-done.6.motion_near
  25.1 0.4 collective-permute-done.7.motion_far
  25.5 0.0 collective-permute-start.8
  25.5 3.3 %collective-permute-start.9 = (bf16[2,512,128]{2,1,0:T(8,128)(2,1)S(1)}, bf16[2,512,128]{2,1,0:T(8,128)(2,1)S(1)}, u32[]{:S(2)}, u32[]{:S(2)}) collective-permute-start(bf16[2,512,128]{2,1,0:T(8,128)(2,1)S(1)} %get-tuple-element.47), channel_id=1, source_target_pairs={{4,8},{8,4},{5,9},{9,5},{6,10},{10,6},{7,11},{11,7},{20,24},{24,20... | collective-permute-start | bytes 786440 | tf_op jit(solution)/shard_map/ppermute | solution.py:45
  28.8 2.9 %horizontal.3.inner_ref.refs_1_ = bf16[4,512,128]{2,1,0:T(8,128)(2,1)S(1)} custom-call(bf16[8,512,128]{2,1,0:T(8,128)(2,1)S(1)} %warp.1.hidden_ref, bf16[4,512,128]{2,1,0:T(8,128)(2,1)S(1)} %motion.2.refs_3_.low_ref.refs_0_.refs_2_, bf16[4,512,128]{2,1,0:T(8,128)(2,1)S(1)} %motion.3.high_ref.refs_1_.refs_3_, ...), custom_call_target="tpu_custom_call" | custom-call | tf_op jit(solution)/shard_map/horizontal/pallas_call | solution.py:373
  31.7 0.9 %own_sums.1 = (f32[4,512,128]{2,1,0:T(8,128)S(1)}, bf16[2,512,128]{2,1,0:T(8,128)(2,1)S(1)}, bf16[2,512,128]{2,1,0:T(8,128)(2,1)S(1)}) custom-call(bf16[4,512,128]{2,1,0:T(8,128)(2,1)S(1)} %get-tuple-element.34.outer_ref.refs_0_, bf16[4,512,128]{2,1,0:T(8,128)(2,1)S(1)} %horizontal.3.inner_ref.refs_1_, ...), custom_call_target="tpu_custom_call" | custom-call | tf_op jit(solution)/shard_map/own_sums/pallas_call | solution.py:450
  32.6 0.1 collective-permute-start.10
  32.6 2.9 %collective-permute-start.11 = (bf16[2,512,128]{2,1,0:T(8,128)(2,1)S(1)}, bf16[2,512,128]{2,1,0:T(8,128)(2,1)S(1)}, u32[]{:S(2)}, u32[]{:S(2)}) collective-permute-start(bf16[2,512,128]{2,1,0:T(8,128)(2,1)S(1)} %get-tuple-element.43.refs_7_), channel_id=1, source_target_pairs={{4,8},{8,4},{5,9},{9,5},{6,10},{10,6},{7,11},{11,7},{20,24},{24,20... | collective-permute-start | bytes 786440 | tf_op jit(solution)/shard_map/ppermute | solution.py:45
  35.5 2.1 %inner_gates.1 = (f32[4,512,128]{2,1,0:T(8,128)S(1)}, bf16[4,512,128]{2,1,0:T(8,128)(2,1)S(1)}, f32[4,512,128]{2,1,0:T(8,128)S(1)}) custom-call(bf16[4,512,128]{2,1,0:T(8,128)(2,1)S(1)} %get-tuple-element.34.outer_ref.refs_0_, bf16[4,512,128]{2,1,0:T(8,128)(2,1)S(1)} %horizontal.3.inner_ref.refs_1_, ...), custom_call_target="tpu_custom_call" | custom-call | tf_op jit(solution)/shard_map/inner_gates/pallas_call | solution.py:481
  37.6 0.0 collective-permute-done.8.hidden_near.edge_ref
  37.6 0.0 collective-permute-done.9.hidden_far.edge_ref
  37.6 0.9 %outer_gates.1 = (f32[4,512,128]{2,1,0:T(8,128)S(1)}, bf16[4,512,128]{2,1,0:T(8,128)(2,1)S(1)}, f32[4,512,128]{2,1,0:T(8,128)S(1)}, bf16[4,512,128]{2,1,0:T(8,128)(2,1)S(1)}) custom-call(bf16[4,512,128]{2,1,0:T(8,128)(2,1)S(1)} %get-tuple-element.34.outer_ref.refs_0_, f32[4,512,128]{2,1,0:T(8,128)S(1)} %get-tuple-element.44.update_sums, ...), custom_call_target="tpu_custom_call" | custom-call | tf_op jit(solution)/shard_map/outer_gates/pallas_call | solution.py:529
  38.5 1.7 %inner_states.1 = (bf16[4,512,128]{2,1,0:T(8,128)(2,1)S(1)}, f32[4,512,128]{2,1,0:T(8,128)S(1)}) custom-call(bf16[4,512,128]{2,1,0:T(8,128)(2,1)S(1)} %get-tuple-element.50.reset_outer, bf16[4,512,128]{2,1,0:T(8,128)(2,1)S(1)} %get-tuple-element.51.reset_inner, bf16[4,512,128]{2,1,0:T(8,128)(2,1)S(1)} %motion.2.refs_3_.low_ref.refs_0_.refs_2_, ...), custom_call_target="tpu_custom_call" | custom-call | tf_op jit(solution)/shard_map/inner_states/pallas_call | solution.py:584
  40.2 0.1 collective-permute-done.10.last_ref
  40.3 1.0 %final_near.1.first_ref = bf16[1,8,512,128]{3,2,1,0:T(8,128)(2,1)} custom-call(bf16[4,512,128]{2,1,0:T(8,128)(2,1)S(1)} %get-tuple-element.55.first_ref, bf16[2,512,128]{2,1,0:T(8,128)(2,1)S(1)} %collective-permute-done.8.hidden_near.edge_ref, bf16[2,512,128]{2,1,0:T(8,128)(2,1)S(1)} %collective-permute-done.10.last_ref, ...), custom_call_target="tpu_custom_call" | custom-call | tf_op jit(solution)/shard_map/final_near/pallas_call | solution.py:635
  41.3 0.9 %collective-permute-done.11.last_ref = bf16[2,512,128]{2,1,0:T(8,128)(2,1)S(1)} collective-permute-done((bf16[2,512,128]{2,1,0:T(8,128)(2,1)S(1)}, bf16[2,512,128]{2,1,0:T(8,128)(2,1)S(1)}, u32[]{:S(2)}, u32[]{:S(2)}) %collective-permute-start.11) | collective-permute-done | bytes 262176 | tf_op jit(solution)/shard_map/ppermute | solution.py:45
  42.2 1.0 %final_far.1 = bf16[1,8,512,128]{3,2,1,0:T(8,128)(2,1)} custom-call(bf16[1,8,512,128]{3,2,1,0:T(8,128)(2,1)} %final_near.1.first_ref, bf16[2,512,128]{2,1,0:T(8,128)(2,1)S(1)} %collective-permute-done.9.hidden_far.edge_ref, bf16[2,512,128]{2,1,0:T(8,128)(2,1)S(1)} %collective-permute-done.11.last_ref, ...), custom_call_target="tpu_custom_call", output_to_operand_aliasing={{}: (0, {})} | custom-call | tf_op jit(solution)/shard_map/final_far/pallas_call | solution.py:635
  (3 shorter events, 0.0 us)
Async XLA Ops:
  0.0 3.6 %collective-permute-start.2 = (bf16[1,8,512,128]{3,2,1,0:T(8,128)(2,1)}, bf16[1,8,512,128]{3,2,1,0:T(8,128)(2,1)S(1)}, u32[]{:S(2)}, u32[]{:S(2)}) collective-permute-start(bf16[1,8,512,128]{3,2,1,0:T(8,128)(2,1)} %refs_1_.4), channel_id=1, source_target_pairs={{0,1},{1,0},{2,3},{3,2},{4,5},{5,4},{6,7},{7,6},{8,9},{9,8},{10,11... | collective-permute-start | bytes 3145736 | tf_op jit(solution)/shard_map/ppermute | solution.py:657
  0.0 6.3 %collective-permute-start.1 = (s32[1,4,4,8]{3,2,1,0:T(4,128)}, s32[1,4,4,8]{3,2,1,0:T(4,128)S(1)}, u32[]{:S(2)}, u32[]{:S(2)}) collective-permute-start(s32[1,4,4,8]{3,2,1,0:T(4,128)} %bitcast.1), channel_id=1, source_target_pairs={{4,8},{8,4},{5,9},{9,5},{6,10},{10,6},{7,11},{11,7},{20,24},{24,20... | collective-permute-start | bytes 1544 | tf_op jit(solution)/shard_map/ppermute | solution.py:45
  3.5 3.9 %collective-permute-start = (s32[1,4,4,8]{3,2,1,0:T(4,128)}, s32[1,4,4,8]{3,2,1,0:T(4,128)S(1)}, u32[]{:S(2)}, u32[]{:S(2)}) collective-permute-start(s32[1,4,4,8]{3,2,1,0:T(4,128)} %bitcast.2), channel_id=1, source_target_pairs={{0,4},{4,0},{8,12},{12,8},{1,5},{5,1},{9,13},{13,9},{2,6},{6,2},{1... | collective-permute-start | bytes 1544 | tf_op jit(solution)/shard_map/ppermute | solution.py:37
  6.2 6.2 %copy-start.1 = (bf16[5,256,256]{2,1,0:T(8,128)(2,1)S(1)}, bf16[5,256,256]{2,1,0:T(8,128)(2,1)}, u32[]{:S(2)}) copy-start(bf16[5,256,256]{2,1,0:T(8,128)(2,1)} %gates_ref.7) | copy-start | bytes 1966084
  6.2 6.2 %copy-start.4 = (bf16[5,256,128]{2,1,0:T(8,128)(2,1)S(1)}, bf16[5,256,128]{2,1,0:T(8,128)(2,1)}, u32[]{:S(2)}) copy-start(bf16[5,256,128]{2,1,0:T(8,128)(2,1)} %cand_ref.4) | copy-start | bytes 983044
  9.0 10.3 %collective-permute-start.3 = (bf16[8,128,128]{2,1,0:T(8,128)(2,1)S(1)}, bf16[8,128,128]{2,1,0:T(8,128)(2,1)S(1)}, u32[]{:S(2)}, u32[]{:S(2)}) collective-permute-start(bf16[8,128,128]{2,1,0:T(8,128)(2,1)S(1)} %get-tuple-element.32.refs_4_), channel_id=1, source_target_pairs={{0,4},{4,0},{8,12},{12,8},{1,5},{5,1},{9,13},{13,9},{2,6},{6,2},{1... | collective-permute-start | bytes 786440 | tf_op jit(solution)/shard_map/ppermute | solution.py:37
  10.1 9.8 %collective-permute-start.4 = (bf16[8,128,128]{2,1,0:T(8,128)(2,1)S(1)}, bf16[8,128,128]{2,1,0:T(8,128)(2,1)S(1)}, u32[]{:S(2)}, u32[]{:S(2)}) collective-permute-start(bf16[8,128,128]{2,1,0:T(8,128)(2,1)S(1)} %get-tuple-element.33.refs_5_), channel_id=1, source_target_pairs={{4,8},{8,4},{5,9},{9,5},{6,10},{10,6},{7,11},{11,7},{20,24},{24,20... | collective-permute-start | bytes 786440 | tf_op jit(solution)/shard_map/ppermute | solution.py:45
  15.5 4.4 %copy-start = (bf16[1,8,512,128]{3,2,1,0:T(8,128)(2,1)S(1)}, bf16[1,8,512,128]{3,2,1,0:T(8,128)(2,1)}, u32[]{:S(2)}) copy-start(bf16[1,8,512,128]{3,2,1,0:T(8,128)(2,1)} %refs_1_.5) | copy-start | bytes 3145732
  15.5 4.4 %copy-start.5 = (s32[1,8,4,4]{1,3,2,0:T(4,128)S(1)}, s32[1,8,4,4]{1,3,2,0:T(4,128)}, u32[]{:S(2)}) copy-start(s32[1,8,4,4]{1,3,2,0:T(4,128)} %param.12) | copy-start | bytes 1540
  15.6 9.5 %collective-permute-start.6 = (bf16[2,512,128]{2,1,0:T(8,128)(2,1)S(1)}, bf16[2,512,128]{2,1,0:T(8,128)(2,1)S(1)}, u32[]{:S(2)}, u32[]{:S(2)}) collective-permute-start(bf16[2,512,128]{2,1,0:T(8,128)(2,1)S(1)} %get-tuple-element.38), channel_id=1, source_target_pairs={{0,4},{4,0},{8,12},{12,8},{1,5},{5,1},{9,13},{13,9},{2,6},{6,2},{1... | collective-permute-start | bytes 786440 | tf_op jit(solution)/shard_map/ppermute | solution.py:37
  15.7 9.8 %collective-permute-start.7 = (bf16[2,512,128]{2,1,0:T(8,128)(2,1)S(1)}, bf16[2,512,128]{2,1,0:T(8,128)(2,1)S(1)}, u32[]{:S(2)}, u32[]{:S(2)}) collective-permute-start(bf16[2,512,128]{2,1,0:T(8,128)(2,1)S(1)} %get-tuple-element.39), channel_id=1, source_target_pairs={{4,8},{8,4},{5,9},{9,5},{6,10},{10,6},{7,11},{11,7},{20,24},{24,20... | collective-permute-start | bytes 786440 | tf_op jit(solution)/shard_map/ppermute | solution.py:45
  20.8 1.3 %copy-start.2 = (bf16[5,256,256]{2,1,0:T(8,128)(2,1)S(1)}, bf16[5,256,256]{2,1,0:T(8,128)(2,1)}, u32[]{:S(2)}) copy-start(bf16[5,256,256]{2,1,0:T(8,128)(2,1)} %gates_ref.6) | copy-start | bytes 1966084
  20.8 1.3 %copy-start.3 = (bf16[5,256,128]{2,1,0:T(8,128)(2,1)S(1)}, bf16[5,256,128]{2,1,0:T(8,128)(2,1)}, u32[]{:S(2)}) copy-start(bf16[5,256,128]{2,1,0:T(8,128)(2,1)} %cand_ref.5) | copy-start | bytes 983044
  20.8 1.3 %collective-permute-start.5 = (bf16[8,16,256]{2,1,0:T(8,128)(2,1)S(1)}, bf16[8,16,256]{2,1,0:T(8,128)(2,1)S(1)}, u32[]{:S(2)}, u32[]{:S(2)}) collective-permute-start(bf16[8,16,256]{2,1,0:T(8,128)(2,1)S(1)} %seam.1.refs_4_), channel_id=1, source_target_pairs={{0,1},{1,0},{2,3},{3,2},{4,5},{5,4},{6,7},{7,6},{8,9},{9,8},{10,11... | collective-permute-start | bytes 196616 | tf_op jit(solution)/shard_map/ppermute | solution.py:657
  25.5 12.1 %collective-permute-start.8 = (bf16[2,512,128]{2,1,0:T(8,128)(2,1)S(1)}, bf16[2,512,128]{2,1,0:T(8,128)(2,1)S(1)}, u32[]{:S(2)}, u32[]{:S(2)}) collective-permute-start(bf16[2,512,128]{2,1,0:T(8,128)(2,1)S(1)} %get-tuple-element.46), channel_id=1, source_target_pairs={{0,4},{4,0},{8,12},{12,8},{1,5},{5,1},{9,13},{13,9},{2,6},{6,2},{1... | collective-permute-start | bytes 786440 | tf_op jit(solution)/shard_map/ppermute | solution.py:37
  25.5 12.1 %collective-permute-start.9 = (bf16[2,512,128]{2,1,0:T(8,128)(2,1)S(1)}, bf16[2,512,128]{2,1,0:T(8,128)(2,1)S(1)}, u32[]{:S(2)}, u32[]{:S(2)}) collective-permute-start(bf16[2,512,128]{2,1,0:T(8,128)(2,1)S(1)} %get-tuple-element.47), channel_id=1, source_target_pairs={{4,8},{8,4},{5,9},{9,5},{6,10},{10,6},{7,11},{11,7},{20,24},{24,20... | collective-permute-start | bytes 786440 | tf_op jit(solution)/shard_map/ppermute | solution.py:45
  32.6 7.7 %collective-permute-start.10 = (bf16[2,512,128]{2,1,0:T(8,128)(2,1)S(1)}, bf16[2,512,128]{2,1,0:T(8,128)(2,1)S(1)}, u32[]{:S(2)}, u32[]{:S(2)}) collective-permute-start(bf16[2,512,128]{2,1,0:T(8,128)(2,1)S(1)} %get-tuple-element.42.refs_6_), channel_id=1, source_target_pairs={{0,4},{4,0},{8,12},{12,8},{1,5},{5,1},{9,13},{13,9},{2,6},{6,2},{1... | collective-permute-start | bytes 786440 | tf_op jit(solution)/shard_map/ppermute | solution.py:37
  32.6 9.6 %collective-permute-start.11 = (bf16[2,512,128]{2,1,0:T(8,128)(2,1)S(1)}, bf16[2,512,128]{2,1,0:T(8,128)(2,1)S(1)}, u32[]{:S(2)}, u32[]{:S(2)}) collective-permute-start(bf16[2,512,128]{2,1,0:T(8,128)(2,1)S(1)} %get-tuple-element.43.refs_7_), channel_id=1, source_target_pairs={{4,8},{8,4},{5,9},{9,5},{6,10},{10,6},{7,11},{11,7},{20,24},{24,20... | collective-permute-start | bytes 786440 | tf_op jit(solution)/shard_map/ppermute | solution.py:45

commit v5 on v4

--- a/solution.py
+++ b/solution.py
@@ -172,14 +172,13 @@
     )(low, high, *earlier)
 
 
-def gather_kernel(near_list, far_list, prev_ref, near_out, far_out, sems):
+def gather_kernel(near_list, far_list, prev_ref, near_out, far_out):
     _, band_blocks, _, band_rows = near_list.shape
     slots, width, _ = near_out.shape
     sign = 2 * near_below() - 1
     lane = lax.broadcasted_iota(jnp.int32, (1, band_rows), 1)
-    copies = []
     sides = ((near_list, near_out, sign), (far_list, far_out, -sign))
-    for side, (list_ref, out, wanted) in enumerate(sides):
+    for list_ref, out, wanted in sides:
         before = jnp.zeros((1, 1), jnp.int32)
         ranks, asked = [], []
         for block in range(band_blocks):
@@ -198,11 +197,7 @@
             source = jnp.sum(found)
             row = source // band_blocks
             column = pl.multiple_of(source % band_blocks * width, width)
-            block = prev_ref.at[0, row, pl.ds(column, width), :]
-            copies.append(pltpu.make_async_copy(block, out.at[slot], sems.at[side, slot]))
-            copies[-1].start()
-    for copy in copies:
-        copy.wait()
+            out[slot] = prev_ref[0, row, pl.ds(column, width), :]
 
 
 def gather_blocks(near_list, far_list, prev, *earlier):
@@ -212,13 +207,12 @@
     shape = jax.ShapeDtypeStruct((slots, width // band_blocks, hidden), bf16)
     return pl.pallas_call(
         ordered(gather_kernel, 3, earlier),
-        in_specs=[IN_VMEM, IN_VMEM, IN_HBM] + [IN_VMEM] * len(earlier),
+        in_specs=[IN_VMEM] * (3 + len(earlier)),
         out_specs=[IN_VMEM, IN_VMEM],
         out_shape=[shape, shape],
-        scratch_shapes=[pltpu.SemaphoreType.DMA((2, slots))],
         compiler_params=params(4),
         name="gather",
-    )(near_list, far_list, in_hbm(prev), *earlier)
+    )(near_list, far_list, prev, *earlier)
 
 
 def pick_blocks(list_ref, rows, blocks, visit):

time: 44.2 us -> 43.2 us (0.977)
  Pallas kernels: 22.8 us -> 21.8 us
    pallas_call x1, Pallas kernels: 1.57 us -> 0.57 us  [gather_blocks(): pl.pallas_call(ordered(gather_kernel, 3, earlier), in_specs=[IN_VMEM] * (...]
  transfers between devices with their start and end apart: 12 -> 12, of which waited for: 6 -> 6; matrix products, arithmetic and copies ran while one was open for 0% -> 0% of each run, Pallas kernels for 46% -> 48%
where the time goes in v5:
time: 43.2 us; the launch traced here: 42.4 us
  Pallas kernels  21.8 us (50%)
  starting transfers between devices  16.7 us (39%)
  waiting for transfers between devices  3.48 us (8%)
    ppermute x5, starting transfers between devices, swap_far(): return lax.ppermute(value, axis, pairs)  15.5 us
    pallas_call x2, Pallas kernels, horizontal_pass(): pl.pallas_call(functools.partial(horizontal_kernel, rows), in_specs=[IN_V...  5.9 us
    pallas_call x2, Pallas kernels, motion_of(): pl.pallas_call(ordered(functools.partial(motion_kernel, first), 4, earlie...  5.29 us
    ppermute x5, waiting for transfers between devices, swap_far(): return lax.ppermute(value, axis, pairs)  2.13 us
    pallas_call x1, Pallas kernels, inner_gates(): pl.pallas_call(ordered(gates_kernel, 6, earlier), in_specs=[IN_VMEM] * (6...  2.07 us
    pallas_call x2, Pallas kernels, side(): pl.pallas_call(functools.partial(final_kernel, near), in_specs=[IN_VMEM i...  2.06 us
    pallas_call x1, Pallas kernels, inner_states(): pl.pallas_call(cand_kernel, in_specs=[IN_VMEM] * 8, out_specs=[IN_VMEM] *...  1.66 us
    ppermute x5, waiting for transfers between devices, swap_near(): return lax.ppermute(value, axis, pairs)  1.27 us
  transfers between devices with their start and end apart: 12, of which 6 were waited for; matrix products, arithmetic and copies ran while one was open for 0% of the time, Pallas kernels for 48%

profile of v5, /device:TPU:8, one launch (start us, length us, event | category | flops | bytes accessed | tf_op | source)
XLA Modules:
  0.0 42.4 jit_solution(2424339542509096247)
XLA Ops:
  0.0 0.0 collective-permute-start.2
  0.0 3.6 %collective-permute-start.1 = (s32[1,4,4,8]{3,2,1,0:T(4,128)}, s32[1,4,4,8]{3,2,1,0:T(4,128)S(1)}, u32[]{:S(2)}, u32[]{:S(2)}) collective-permute-start(s32[1,4,4,8]{3,2,1,0:T(4,128)} %bitcast.1), channel_id=1, source_target_pairs={{4,8},{8,4},{5,9},{9,5},{6,10},{10,6},{7,11},{11,7},{20,24},{24,20... | collective-permute-start | bytes 1544 | tf_op jit(solution)/shard_map/ppermute | solution.py:45
  3.6 0.1 collective-permute-start
  3.7 0.0 collective-permute-done.2.refs_2_
  3.7 2.6 %motion.2.refs_3_.low_ref.refs_0_.refs_2_ = bf16[4,512,128]{2,1,0:T(8,128)(2,1)S(1)} custom-call(bf16[1,8,512,128]{3,2,1,0:T(8,128)(2,1)} %refs_0_.3, bf16[1,8,512,128]{3,2,1,0:T(8,128)(2,1)} %refs_1_.4, bf16[1,8,512,128]{3,2,1,0:T(8,128)(2,1)S(1)} %collective-permute-done.2.refs_2_, bf16[192,128]{1,0:T(8,128)(2,1)} %refs_3_.3), custom_call_target="tpu_custom_call" | custom-call | tf_op jit(solution)/shard_map/motion/pallas_call | solution.py:139
  6.4 0.0 copy-start.1
  6.4 0.0 copy-start.4
  6.4 0.0 collective-permute-done.1.refs_1_
  6.4 1.1 %collective-permute-done.refs_0_ = s32[1,4,4,8]{3,2,1,0:T(4,128)S(1)} collective-permute-done((s32[1,4,4,8]{3,2,1,0:T(4,128)}, s32[1,4,4,8]{3,2,1,0:T(4,128)S(1)}, u32[]{:S(2)}, u32[]{:S(2)}) %collective-permute-start) | collective-permute-done | bytes 544 | tf_op jit(solution)/shard_map/ppermute | solution.py:37
  7.6 0.0 copy-done
  7.6 0.6 %gather.1 = (bf16[8,128,128]{2,1,0:T(8,128)(2,1)S(1)}, bf16[8,128,128]{2,1,0:T(8,128)(2,1)S(1)}) custom-call(s32[1,4,4,8]{3,2,1,0:T(4,128)S(1)} %collective-permute-done.refs_0_, s32[1,4,4,8]{3,2,1,0:T(4,128)S(1)} %collective-permute-done.1.refs_1_, bf16[1,8,512,128]{3,2,1,0:T(8,128)(2,1)S(1)} %copy-done, ...), custom_call_target="tpu_custom_call" | custom-call | tf_op jit(solution)/shard_map/gather/pallas_call | solution.py:208
  8.1 0.9 %collective-permute-start.3 = (bf16[8,128,128]{2,1,0:T(8,128)(2,1)S(1)}, bf16[8,128,128]{2,1,0:T(8,128)(2,1)S(1)}, u32[]{:S(2)}, u32[]{:S(2)}) collective-permute-start(bf16[8,128,128]{2,1,0:T(8,128)(2,1)S(1)} %get-tuple-element.32.refs_4_), channel_id=1, source_target_pairs={{0,4},{4,0},{8,12},{12,8},{1,5},{5,1},{9,13},{13,9},{2,6},{6,2},{1... | collective-permute-start | bytes 786440 | tf_op jit(solution)/shard_map/ppermute | solution.py:37
  9.1 2.3 %collective-permute-start.4 = (bf16[8,128,128]{2,1,0:T(8,128)(2,1)S(1)}, bf16[8,128,128]{2,1,0:T(8,128)(2,1)S(1)}, u32[]{:S(2)}, u32[]{:S(2)}) collective-permute-start(bf16[8,128,128]{2,1,0:T(8,128)(2,1)S(1)} %get-tuple-element.33.refs_5_), channel_id=1, source_target_pairs={{4,8},{8,4},{5,9},{9,5},{6,10},{10,6},{7,11},{11,7},{20,24},{24,20... | collective-permute-start | bytes 786440 | tf_op jit(solution)/shard_map/ppermute | solution.py:45
  11.4 0.0 copy-done.1
  11.4 0.0 copy-done.4
  11.5 0.3 pairs.1
  11.8 2.6 %motion.3.high_ref.refs_1_.refs_3_ = bf16[4,512,128]{2,1,0:T(8,128)(2,1)S(1)} custom-call(bf16[1,8,512,128]{3,2,1,0:T(8,128)(2,1)} %refs_0_.3, bf16[1,8,512,128]{3,2,1,0:T(8,128)(2,1)} %refs_1_.4, bf16[1,8,512,128]{3,2,1,0:T(8,128)(2,1)S(1)} %collective-permute-done.2.refs_2_, bf16[192,128]{1,0:T(8,128)(2,1)} %refs_3_.3, ...), custom_call_target="tpu_custom_call" | custom-call | tf_op jit(solution)/shard_map/motion/pallas_call | solution.py:139
  14.4 0.0 copy-start.5
  14.4 0.1 edges.1
  14.6 0.1 collective-permute-start.6
  14.7 3.5 %collective-permute-start.7 = (bf16[2,512,128]{2,1,0:T(8,128)(2,1)S(1)}, bf16[2,512,128]{2,1,0:T(8,128)(2,1)S(1)}, u32[]{:S(2)}, u32[]{:S(2)}) collective-permute-start(bf16[2,512,128]{2,1,0:T(8,128)(2,1)S(1)} %get-tuple-element.39), channel_id=1, source_target_pairs={{4,8},{8,4},{5,9},{9,5},{6,10},{10,6},{7,11},{11,7},{20,24},{24,20... | collective-permute-start | bytes 786440 | tf_op jit(solution)/shard_map/ppermute | solution.py:45
  18.1 0.0 collective-permute-done.3.near_ref.refs_2_
  18.2 0.9 %collective-permute-done.4.far_ref.refs_3_ = bf16[8,128,128]{2,1,0:T(8,128)(2,1)S(1)} collective-permute-done((bf16[8,128,128]{2,1,0:T(8,128)(2,1)S(1)}, bf16[8,128,128]{2,1,0:T(8,128)(2,1)S(1)}, u32[]{:S(2)}, u32[]{:S(2)}) %collective-permute-start.4) | collective-permute-done | bytes 262176 | tf_op jit(solution)/shard_map/ppermute | solution.py:45
  19.1 0.9 %seam.1.refs_4_ = bf16[8,16,256]{2,1,0:T(8,128)(2,1)S(1)} custom-call(s32[1,4,4,8]{3,2,1,0:T(4,128)S(1)} %bitcast.3, bf16[1,8,512,128]{3,2,1,0:T(8,128)(2,1)S(1)} %copy-done, bf16[8,128,128]{2,1,0:T(8,128)(2,1)S(1)} %collective-permute-done.3.near_ref.refs_2_, bf16[8,128,128]{2,1,0:T(8,128)(2,1)S(1)} %collective-permute-done.4.far_ref.refs_3_, ...), custom_call_target="tpu_custom_call" | custom-call | tf_op jit(solution)/shard_map/seam/pallas_call | solution.py:263
  19.9 0.0 copy-start.2
  19.9 0.0 copy-start.3
  19.9 0.1 collective-permute-start.5
  20.0 1.2 %warp.1.hidden_ref = bf16[8,512,128]{2,1,0:T(8,128)(2,1)S(1)} custom-call(s32[1,4,4,8]{3,2,1,0:T(4,128)S(1)} %bitcast.4, bf16[1,8,512,128]{3,2,1,0:T(8,128)(2,1)S(1)} %copy-done, bf16[8,128,128]{2,1,0:T(8,128)(2,1)S(1)} %collective-permute-done.3.near_ref.refs_2_, bf16[8,128,128]{2,1,0:T(8,128)(2,1)S(1)} %collective-permute-done.4.far_ref.refs_3_, ...), custom_call_target="tpu_custom_call" | custom-call | tf_op jit(solution)/shard_map/warp/pallas_call | solution.py:290
  21.2 0.1 collective-permute-done.5.seam_ref
  21.3 0.0 copy-done.2
  21.3 3.0 %horizontal.2 = (bf16[4,512,128]{2,1,0:T(8,128)(2,1)S(1)}, bf16[2,512,128]{2,1,0:T(8,128)(2,1)S(1)}, bf16[2,512,128]{2,1,0:T(8,128)(2,1)S(1)}) custom-call(bf16[8,512,128]{2,1,0:T(8,128)(2,1)S(1)} %warp.1.hidden_ref, bf16[4,512,128]{2,1,0:T(8,128)(2,1)S(1)} %motion.2.refs_3_.low_ref.refs_0_.refs_2_, bf16[4,512,128]{2,1,0:T(8,128)(2,1)S(1)} %motion.3.high_ref.refs_1_.refs_3_, ...), custom_call_target="tpu_custom_call" | custom-call | tf_op jit(solution)/shard_map/horizontal/pallas_call | solution.py:367
  24.3 0.0 collective-permute-done.6.motion_near
  24.3 0.1 collective-permute-done.7.motion_far
  24.5 0.0 collective-permute-start.8
  24.5 3.2 %collective-permute-start.9 = (bf16[2,512,128]{2,1,0:T(8,128)(2,1)S(1)}, bf16[2,512,128]{2,1,0:T(8,128)(2,1)S(1)}, u32[]{:S(2)}, u32[]{:S(2)}) collective-permute-start(bf16[2,512,128]{2,1,0:T(8,128)(2,1)S(1)} %get-tuple-element.47), channel_id=1, source_target_pairs={{4,8},{8,4},{5,9},{9,5},{6,10},{10,6},{7,11},{11,7},{20,24},{24,20... | collective-permute-start | bytes 786440 | tf_op jit(solution)/shard_map/ppermute | solution.py:45
  27.6 2.9 %horizontal.3.inner_ref.refs_1_ = bf16[4,512,128]{2,1,0:T(8,128)(2,1)S(1)} custom-call(bf16[8,512,128]{2,1,0:T(8,128)(2,1)S(1)} %warp.1.hidden_ref, bf16[4,512,128]{2,1,0:T(8,128)(2,1)S(1)} %motion.2.refs_3_.low_ref.refs_0_.refs_2_, bf16[4,512,128]{2,1,0:T(8,128)(2,1)S(1)} %motion.3.high_ref.refs_1_.refs_3_, ...), custom_call_target="tpu_custom_call" | custom-call | tf_op jit(solution)/shard_map/horizontal/pallas_call | solution.py:367
  30.5 0.9 %own_sums.1 = (f32[4,512,128]{2,1,0:T(8,128)S(1)}, bf16[2,512,128]{2,1,0:T(8,128)(2,1)S(1)}, bf16[2,512,128]{2,1,0:T(8,128)(2,1)S(1)}) custom-call(bf16[4,512,128]{2,1,0:T(8,128)(2,1)S(1)} %get-tuple-element.34.outer_ref.refs_0_, bf16[4,512,128]{2,1,0:T(8,128)(2,1)S(1)} %horizontal.3.inner_ref.refs_1_, ...), custom_call_target="tpu_custom_call" | custom-call | tf_op jit(solution)/shard_map/own_sums/pallas_call | solution.py:444
  31.4 0.1 collective-permute-start.10
  31.5 2.9 %collective-permute-start.11 = (bf16[2,512,128]{2,1,0:T(8,128)(2,1)S(1)}, bf16[2,512,128]{2,1,0:T(8,128)(2,1)S(1)}, u32[]{:S(2)}, u32[]{:S(2)}) collective-permute-start(bf16[2,512,128]{2,1,0:T(8,128)(2,1)S(1)} %get-tuple-element.43.refs_7_), channel_id=1, source_target_pairs={{4,8},{8,4},{5,9},{9,5},{6,10},{10,6},{7,11},{11,7},{20,24},{24,20... | collective-permute-start | bytes 786440 | tf_op jit(solution)/shard_map/ppermute | solution.py:45
  34.3 2.1 %inner_gates.1 = (f32[4,512,128]{2,1,0:T(8,128)S(1)}, bf16[4,512,128]{2,1,0:T(8,128)(2,1)S(1)}, f32[4,512,128]{2,1,0:T(8,128)S(1)}) custom-call(bf16[4,512,128]{2,1,0:T(8,128)(2,1)S(1)} %get-tuple-element.34.outer_ref.refs_0_, bf16[4,512,128]{2,1,0:T(8,128)(2,1)S(1)} %horizontal.3.inner_ref.refs_1_, ...), custom_call_target="tpu_custom_call" | custom-call | tf_op jit(solution)/shard_map/inner_gates/pallas_call | solution.py:475
  36.4 0.0 collective-permute-done.8.hidden_near.edge_ref
  36.4 0.0 collective-permute-done.9.hidden_far.edge_ref
  36.4 0.9 %outer_gates.1 = (f32[4,512,128]{2,1,0:T(8,128)S(1)}, bf16[4,512,128]{2,1,0:T(8,128)(2,1)S(1)}, f32[4,512,128]{2,1,0:T(8,128)S(1)}, bf16[4,512,128]{2,1,0:T(8,128)(2,1)S(1)}) custom-call(bf16[4,512,128]{2,1,0:T(8,128)(2,1)S(1)} %get-tuple-element.34.outer_ref.refs_0_, f32[4,512,128]{2,1,0:T(8,128)S(1)} %get-tuple-element.44.update_sums, ...), custom_call_target="tpu_custom_call" | custom-call | tf_op jit(solution)/shard_map/outer_gates/pallas_call | solution.py:523
  37.3 1.7 %inner_states.1 = (bf16[4,512,128]{2,1,0:T(8,128)(2,1)S(1)}, f32[4,512,128]{2,1,0:T(8,128)S(1)}) custom-call(bf16[4,512,128]{2,1,0:T(8,128)(2,1)S(1)} %get-tuple-element.50.reset_outer, bf16[4,512,128]{2,1,0:T(8,128)(2,1)S(1)} %get-tuple-element.51.reset_inner, bf16[4,512,128]{2,1,0:T(8,128)(2,1)S(1)} %motion.2.refs_3_.low_ref.refs_0_.refs_2_, ...), custom_call_target="tpu_custom_call" | custom-call | tf_op jit(solution)/shard_map/inner_states/pallas_call | solution.py:578
  39.0 0.1 collective-permute-done.10.last_ref
  39.1 1.0 %final_near.1.first_ref = bf16[1,8,512,128]{3,2,1,0:T(8,128)(2,1)} custom-call(bf16[4,512,128]{2,1,0:T(8,128)(2,1)S(1)} %get-tuple-element.55.first_ref, bf16[2,512,128]{2,1,0:T(8,128)(2,1)S(1)} %collective-permute-done.8.hidden_near.edge_ref, bf16[2,512,128]{2,1,0:T(8,128)(2,1)S(1)} %collective-permute-done.10.last_ref, ...), custom_call_target="tpu_custom_call" | custom-call | tf_op jit(solution)/shard_map/final_near/pallas_call | solution.py:629
  40.2 1.1 %collective-permute-done.11.last_ref = bf16[2,512,128]{2,1,0:T(8,128)(2,1)S(1)} collective-permute-done((bf16[2,512,128]{2,1,0:T(8,128)(2,1)S(1)}, bf16[2,512,128]{2,1,0:T(8,128)(2,1)S(1)}, u32[]{:S(2)}, u32[]{:S(2)}) %collective-permute-start.11) | collective-permute-done | bytes 262176 | tf_op jit(solution)/shard_map/ppermute | solution.py:45
  41.2 1.0 %final_far.1 = bf16[1,8,512,128]{3,2,1,0:T(8,128)(2,1)} custom-call(bf16[1,8,512,128]{3,2,1,0:T(8,128)(2,1)} %final_near.1.first_ref, bf16[2,512,128]{2,1,0:T(8,128)(2,1)S(1)} %collective-permute-done.9.hidden_far.edge_ref, bf16[2,512,128]{2,1,0:T(8,128)(2,1)S(1)} %collective-permute-done.11.last_ref, ...), custom_call_target="tpu_custom_call", output_to_operand_aliasing={{}: (0, {})} | custom-call | tf_op jit(solution)/shard_map/final_far/pallas_call | solution.py:629
  (3 shorter events, 0.0 us)
Async XLA Ops:
  0.0 3.7 %collective-permute-start.2 = (bf16[1,8,512,128]{3,2,1,0:T(8,128)(2,1)}, bf16[1,8,512,128]{3,2,1,0:T(8,128)(2,1)S(1)}, u32[]{:S(2)}, u32[]{:S(2)}) collective-permute-start(bf16[1,8,512,128]{3,2,1,0:T(8,128)(2,1)} %refs_1_.4), channel_id=1, source_target_pairs={{0,1},{1,0},{2,3},{3,2},{4,5},{5,4},{6,7},{7,6},{8,9},{9,8},{10,11... | collective-permute-start | bytes 3145736 | tf_op jit(solution)/shard_map/ppermute | solution.py:651
  0.0 7.6 %copy-start = (bf16[1,8,512,128]{3,2,1,0:T(8,128)(2,1)S(1)}, bf16[1,8,512,128]{3,2,1,0:T(8,128)(2,1)}, u32[]{:S(2)}) copy-start(bf16[1,8,512,128]{3,2,1,0:T(8,128)(2,1)} %refs_1_.5) | copy-start | bytes 3145732
  0.0 6.4 %collective-permute-start.1 = (s32[1,4,4,8]{3,2,1,0:T(4,128)}, s32[1,4,4,8]{3,2,1,0:T(4,128)S(1)}, u32[]{:S(2)}, u32[]{:S(2)}) collective-permute-start(s32[1,4,4,8]{3,2,1,0:T(4,128)} %bitcast.1), channel_id=1, source_target_pairs={{4,8},{8,4},{5,9},{9,5},{6,10},{10,6},{7,11},{11,7},{20,24},{24,20... | collective-permute-start | bytes 1544 | tf_op jit(solution)/shard_map/ppermute | solution.py:45
  3.6 3.9 %collective-permute-start = (s32[1,4,4,8]{3,2,1,0:T(4,128)}, s32[1,4,4,8]{3,2,1,0:T(4,128)S(1)}, u32[]{:S(2)}, u32[]{:S(2)}) collective-permute-start(s32[1,4,4,8]{3,2,1,0:T(4,128)} %bitcast.2), channel_id=1, source_target_pairs={{0,4},{4,0},{8,12},{12,8},{1,5},{5,1},{9,13},{13,9},{2,6},{6,2},{1... | collective-permute-start | bytes 1544 | tf_op jit(solution)/shard_map/ppermute | solution.py:37
  6.4 5.1 %copy-start.1 = (bf16[5,256,256]{2,1,0:T(8,128)(2,1)S(1)}, bf16[5,256,256]{2,1,0:T(8,128)(2,1)}, u32[]{:S(2)}) copy-start(bf16[5,256,256]{2,1,0:T(8,128)(2,1)} %gates_ref.7) | copy-start | bytes 1966084
  6.4 5.1 %copy-start.4 = (bf16[5,256,128]{2,1,0:T(8,128)(2,1)S(1)}, bf16[5,256,128]{2,1,0:T(8,128)(2,1)}, u32[]{:S(2)}) copy-start(bf16[5,256,128]{2,1,0:T(8,128)(2,1)} %cand_ref.4) | copy-start | bytes 983044
  8.1 10.0 %collective-permute-start.3 = (bf16[8,128,128]{2,1,0:T(8,128)(2,1)S(1)}, bf16[8,128,128]{2,1,0:T(8,128)(2,1)S(1)}, u32[]{:S(2)}, u32[]{:S(2)}) collective-permute-start(bf16[8,128,128]{2,1,0:T(8,128)(2,1)S(1)} %get-tuple-element.32.refs_4_), channel_id=1, source_target_pairs={{0,4},{4,0},{8,12},{12,8},{1,5},{5,1},{9,13},{13,9},{2,6},{6,2},{1... | collective-permute-start | bytes 786440 | tf_op jit(solution)/shard_map/ppermute | solution.py:37
  9.1 10.0 %collective-permute-start.4 = (bf16[8,128,128]{2,1,0:T(8,128)(2,1)S(1)}, bf16[8,128,128]{2,1,0:T(8,128)(2,1)S(1)}, u32[]{:S(2)}, u32[]{:S(2)}) collective-permute-start(bf16[8,128,128]{2,1,0:T(8,128)(2,1)S(1)} %get-tuple-element.33.refs_5_), channel_id=1, source_target_pairs={{4,8},{8,4},{5,9},{9,5},{6,10},{10,6},{7,11},{11,7},{20,24},{24,20... | collective-permute-start | bytes 786440 | tf_op jit(solution)/shard_map/ppermute | solution.py:45
  14.4 4.6 %copy-start.5 = (s32[1,8,4,4]{1,3,2,0:T(4,128)S(1)}, s32[1,8,4,4]{1,3,2,0:T(4,128)}, u32[]{:S(2)}) copy-start(s32[1,8,4,4]{1,3,2,0:T(4,128)} %param.12) | copy-start | bytes 1540
  14.6 9.7 %collective-permute-start.6 = (bf16[2,512,128]{2,1,0:T(8,128)(2,1)S(1)}, bf16[2,512,128]{2,1,0:T(8,128)(2,1)S(1)}, u32[]{:S(2)}, u32[]{:S(2)}) collective-permute-start(bf16[2,512,128]{2,1,0:T(8,128)(2,1)S(1)} %get-tuple-element.38), channel_id=1, source_target_pairs={{0,4},{4,0},{8,12},{12,8},{1,5},{5,1},{9,13},{13,9},{2,6},{6,2},{1... | collective-permute-start | bytes 786440 | tf_op jit(solution)/shard_map/ppermute | solution.py:37
  14.7 9.8 %collective-permute-start.7 = (bf16[2,512,128]{2,1,0:T(8,128)(2,1)S(1)}, bf16[2,512,128]{2,1,0:T(8,128)(2,1)S(1)}, u32[]{:S(2)}, u32[]{:S(2)}) collective-permute-start(bf16[2,512,128]{2,1,0:T(8,128)(2,1)S(1)} %get-tuple-element.39), channel_id=1, source_target_pairs={{4,8},{8,4},{5,9},{9,5},{6,10},{10,6},{7,11},{11,7},{20,24},{24,20... | collective-permute-start | bytes 786440 | tf_op jit(solution)/shard_map/ppermute | solution.py:45
  19.9 1.3 %copy-start.2 = (bf16[5,256,256]{2,1,0:T(8,128)(2,1)S(1)}, bf16[5,256,256]{2,1,0:T(8,128)(2,1)}, u32[]{:S(2)}) copy-start(bf16[5,256,256]{2,1,0:T(8,128)(2,1)} %gates_ref.6) | copy-start | bytes 1966084
  19.9 1.3 %copy-start.3 = (bf16[5,256,128]{2,1,0:T(8,128)(2,1)S(1)}, bf16[5,256,128]{2,1,0:T(8,128)(2,1)}, u32[]{:S(2)}) copy-start(bf16[5,256,128]{2,1,0:T(8,128)(2,1)} %cand_ref.5) | copy-start | bytes 983044
  19.9 1.3 %collective-permute-start.5 = (bf16[8,16,256]{2,1,0:T(8,128)(2,1)S(1)}, bf16[8,16,256]{2,1,0:T(8,128)(2,1)S(1)}, u32[]{:S(2)}, u32[]{:S(2)}) collective-permute-start(bf16[8,16,256]{2,1,0:T(8,128)(2,1)S(1)} %seam.1.refs_4_), channel_id=1, source_target_pairs={{0,1},{1,0},{2,3},{3,2},{4,5},{5,4},{6,7},{7,6},{8,9},{9,8},{10,11... | collective-permute-start | bytes 196616 | tf_op jit(solution)/shard_map/ppermute | solution.py:651
  24.5 12.0 %collective-permute-start.8 = (bf16[2,512,128]{2,1,0:T(8,128)(2,1)S(1)}, bf16[2,512,128]{2,1,0:T(8,128)(2,1)S(1)}, u32[]{:S(2)}, u32[]{:S(2)}) collective-permute-start(bf16[2,512,128]{2,1,0:T(8,128)(2,1)S(1)} %get-tuple-element.46), channel_id=1, source_target_pairs={{0,4},{4,0},{8,12},{12,8},{1,5},{5,1},{9,13},{13,9},{2,6},{6,2},{1... | collective-permute-start | bytes 786440 | tf_op jit(solution)/shard_map/ppermute | solution.py:37
  24.5 12.0 %collective-permute-start.9 = (bf16[2,512,128]{2,1,0:T(8,128)(2,1)S(1)}, bf16[2,512,128]{2,1,0:T(8,128)(2,1)S(1)}, u32[]{:S(2)}, u32[]{:S(2)}) collective-permute-start(bf16[2,512,128]{2,1,0:T(8,128)(2,1)S(1)} %get-tuple-element.47), channel_id=1, source_target_pairs={{4,8},{8,4},{5,9},{9,5},{6,10},{10,6},{7,11},{11,7},{20,24},{24,20... | collective-permute-start | bytes 786440 | tf_op jit(solution)/shard_map/ppermute | solution.py:45
  31.4 7.7 %collective-permute-start.10 = (bf16[2,512,128]{2,1,0:T(8,128)(2,1)S(1)}, bf16[2,512,128]{2,1,0:T(8,128)(2,1)S(1)}, u32[]{:S(2)}, u32[]{:S(2)}) collective-permute-start(bf16[2,512,128]{2,1,0:T(8,128)(2,1)S(1)} %get-tuple-element.42.refs_6_), channel_id=1, source_target_pairs={{0,4},{4,0},{8,12},{12,8},{1,5},{5,1},{9,13},{13,9},{2,6},{6,2},{1... | collective-permute-start | bytes 786440 | tf_op jit(solution)/shard_map/ppermute | solution.py:37
  31.5 9.8 %collective-permute-start.11 = (bf16[2,512,128]{2,1,0:T(8,128)(2,1)S(1)}, bf16[2,512,128]{2,1,0:T(8,128)(2,1)S(1)}, u32[]{:S(2)}, u32[]{:S(2)}) collective-permute-start(bf16[2,512,128]{2,1,0:T(8,128)(2,1)S(1)} %get-tuple-element.43.refs_7_), channel_id=1, source_target_pairs={{4,8},{8,4},{5,9},{9,5},{6,10},{10,6},{7,11},{11,7},{20,24},{24,20... | collective-permute-start | bytes 786440 | tf_op jit(solution)/shard_map/ppermute | solution.py:45
